TPU v7x, 32 devices: a whole 2x2x4 slice. The times are simulated.
32 devices in a mesh: grp: 2 (over x), seq: 8 (over z, core), hd: 2 (over y).
Axes of the slice: x: 2, y: 2, z: 4, core: 2. Of those that a mesh axis runs over, the one named last changes fastest.
Arguments:
- latent_qkv: bfloat16 [2, 8, 256, 3, 3072], P('grp', 'seq', None, None, 'hd'), may hold values from -6 to 6
- cross_query: bfloat16 [2, 8, 256, 3072], P('grp', 'seq', None, 'hd'), may hold values from -6 to 6
- residual: bfloat16 [2, 8, 256, 3072], P('grp', 'seq', None, 'hd'), may hold values from -4 to 4
- prompt_states: bfloat16 [2, 512, 4096], P(None, 'seq', 'grp'), may hold values from -6 to 6
- kv_weight: bfloat16 [4096, 2, 3072], P(('grp', 'seq'), None, 'hd'), may hold values from -0.09375 to 0.09375, as said below
- prompt_lengths: int32 [2], replicated, may hold values from 32 to 512
- assignment: int32 [2], replicated, may hold values from 0 to 1, each once
Outputs:
- block_out: bfloat16 [2, 8, 256, 3072], P('grp', 'seq', None, 'hd')
Inputs may be any that keep to these rules, and one draw needn't show every extreme that they name: Replica g serves prompt assignment[g]; every prompt is served by exactly one replica. `prompt_lengths`: key positions at or beyond a prompt's length are padding. `kv_weight`: entries have mean 0 and deviation 4096 ** -0.5.
All inputs are finite; a program needn't handle non-finite values.
Results may differ from a plain program's by a relative error of at most 0.0075.
Values may be sent and summed in bfloat16 or wider, within the bound.
No kernel may reach another device: no remote copies, remote signals or barrier semaphores. Data moves between devices by JAX's collectives and lax.ppermute only.
A program may use at most 64 MiB of HBM per device.

v0:
```python
import math

import jax
import jax.numpy as jnp
from jax import lax
from jax.sharding import PartitionSpec as P

HDIM = 128


def attend(queries, key_rows, values, key_bias):
    scores = jnp.einsum("qhe,khe->hqk", queries, key_rows, preferred_element_type=jnp.float32)
    scores = scores / math.sqrt(queries.shape[-1]) + key_bias
    row_max = jnp.max(scores, axis=-1, keepdims=True)
    powered = jnp.exp(scores - row_max)
    weights = (powered / jnp.sum(powered, axis=-1, keepdims=True)).astype(jnp.bfloat16)
    return jnp.einsum("hqk,khe->qhe", weights, values, preferred_element_type=jnp.float32)


def frame_attention(mixed):
    frame_count, positions = (mixed.shape[0], mixed.shape[2])
    feat_width = mixed.shape[4]
    shaped = mixed.reshape(frame_count, positions, 3, feat_width // HDIM, HDIM)
    scores = jnp.einsum(
        "fnhe,gnhe->nhfg", shaped[:, :, 0], shaped[:, :, 1], preferred_element_type=jnp.float32
    )
    scores = scores / math.sqrt(HDIM)
    row_max = jnp.max(scores, axis=-1, keepdims=True)
    powered = jnp.exp(scores - row_max)
    weights = (powered / jnp.sum(powered, axis=-1, keepdims=True)).astype(jnp.bfloat16)
    mixed_out = jnp.einsum(
        "nhfg,gnhe->fnhe", weights, shaped[:, :, 2], preferred_element_type=jnp.float32
    )
    return mixed_out.astype(jnp.bfloat16).reshape(frame_count, 1, positions, feat_width)


def body(latent_qkv, cross_query, residual, prompt_states, kv_weight, prompt_lengths, assignment):
    spatial = latent_qkv.shape[2]
    feat_width = latent_qkv.shape[4]
    heads_here = feat_width // HDIM
    seq_count = lax.axis_size("seq")
    group_index = lax.axis_index("grp")
    picked = jnp.take(prompt_states, assignment, axis=0)
    slot_count, rows_here, feat_count = picked.shape
    flat_prompt = picked.reshape(slot_count * rows_here, feat_count)
    local = latent_qkv[0, 0].reshape(spatial, 3, heads_here, HDIM)
    spatial_out = attend(local[:, 0], local[:, 1], local[:, 2], jnp.float32(0.0))
    blocked = latent_qkv[0].reshape(1, seq_count, spatial // seq_count, 3, feat_width)
    moved = frame_attention(lax.all_to_all(blocked, "seq", split_axis=1, concat_axis=0, tiled=True))
    returned = lax.all_to_all(moved, "seq", split_axis=0, concat_axis=1, tiled=True)
    spatial_out, returned = (spatial_out, returned.reshape(spatial, feat_width))
    weight_piece = lax.all_gather(kv_weight, "seq", axis=0, tiled=True)
    piece_rows = weight_piece.shape[0]
    flat_piece = weight_piece.reshape(piece_rows, 2 * feat_width)
    partial_sum = jnp.dot(flat_prompt, flat_piece, preferred_element_type=jnp.float32)
    summed = lax.psum_scatter(partial_sum, "grp", scatter_dimension=0, tiled=True)
    own_rows = summed.astype(jnp.bfloat16).reshape(rows_here, 2, feat_width)
    pairs = lax.all_gather(own_rows, "seq", axis=0, tiled=True)
    prompt_total = pairs.shape[0]
    served = jnp.take(assignment, group_index)
    length_here = jnp.take(prompt_lengths, served)
    key_bias = jnp.where(jnp.arange(prompt_total) < length_here, 0.0, -1000000000.0).astype(
        jnp.float32
    )
    shaped_pairs = pairs.reshape(prompt_total, 2, heads_here, HDIM)
    crossing = cross_query[0, 0].reshape(spatial, heads_here, HDIM)
    cross_out = attend(crossing, shaped_pairs[:, 0], shaped_pairs[:, 1], key_bias)
    total = residual[0, 0].astype(jnp.float32) + spatial_out.reshape(spatial, feat_width)
    total = total + returned.astype(jnp.float32) + cross_out.reshape(spatial, feat_width)
    return total.astype(jnp.bfloat16)[None, None]


def solution(mesh):
    return jax.shard_map(
        body,
        mesh=mesh,
        in_specs=(
            P("grp", "seq", None, None, "hd"),
            P("grp", "seq", None, "hd"),
            P("grp", "seq", None, "hd"),
            P(None, "seq", "grp"),
            P(("grp", "seq"), None, "hd"),
            P(),
            P(),
        ),
        out_specs=P("grp", "seq", None, "hd"),
        check_vma=False,
    )
```

profile of v0, /device:TPU:0, one launch (start us, length us, event | category | flops | bytes accessed | tf_op | source)
XLA Modules:
  0.0 299.6 jit_solution(3480150094139915460)
XLA Ops:
  6.5 0.0 copy-start
  6.5 0.0 all-gather.3.cloned.1.call-start
  6.5 0.7 all-gather.3.cloned.1.call-update
  7.3 0.0 reduce-scatter.2.cloned.1.call-start
  7.3 0.7 compare_select_fusion
  8.0 0.0 copy-done
  8.0 0.6 gather_fusion
  8.6 0.7 compare_and_fusion
  9.2 0.1 broadcast_select_fusion
  9.4 119.1 %all-gather.3.cloned.1.call-done = bf16[2048,2,1536]{2,1,0:T(2,128)(2,1)} async-done(((bf16[256,2,1536]{2,1,0:T(2,128)(2,1)}), bf16[2048,2,1536]{2,1,0:T(2,128)(2,1)}) %all-gather.3.cloned.1.call-update) | async-done | bytes 12582928 | tf_op jit(solution)/shard_map/all_gather | solution.py:52
  128.4 8.8 %copy.78 = bf16[256,8,2,1536]{3,1,2,0:T(8,128)(2,1)S(1)} copy(bf16[256,8,2,1536]{3,2,1,0:T(2,128)(2,1)} %bitcast.80) | data formatting | bytes 25165824
  137.2 3.0 fusion.32
  140.2 0.0 reduce-scatter.2.cloned.1.call-update
  140.2 0.0 all-gather.5.cloned.1.call-start
  140.3 24.4 %reduce-scatter.2.cloned.1.call-done = f32[64,3072]{1,0:T(8,128)} async-done(((f32[128,3072]{1,0:T(8,128)}), f32[64,3072]{1,0:T(8,128)}) %reduce-scatter.2.cloned.1.call-update) | async-done | bytes 786448 | tf_op jit(solution)/shard_map/reduce_scatter | solution.py:56
  164.7 1.2 convert_element_type.46
  165.9 1.0 reshape.99
  166.9 0.0 all-gather.5.cloned.1.call-update
  166.9 0.0 copy-done.2
  166.9 1.6 copy.55
  168.5 4.7 %all-to-all-start = ((bf16[1,8,32,3,1536]{4,2,3,0,1:T(8,128)(2,1)}), bf16[1,8,32,3,1536]{4,2,3,0,1:T(8,128)(2,1)}, u32[]{:S(2)}, u32[]{:S(2)}) async-start(bf16[1,8,32,3,1536]{4,2,3,0,1:T(8,128)(2,1)} %copy.55), calls=%async_computation | async-start | bytes 4718592 | tf_op jit(solution)/shard_map/all_to_all | solution.py:49
  173.3 0.0 copy-start.5
  173.3 0.7 dynamic-slice.4
  174.7 2.5 copy.50
  177.2 0.0 copy-done.8
  177.2 0.6 dynamic-slice.5
  177.8 1.2 copy.64
  178.9 2.0 fusion.21
  180.9 2.4 fusion.31
  183.3 1.6 fusion.18
  184.9 1.7 copy.54
  187.1 66.2 %all-to-all-done = bf16[1,8,32,3,1536]{4,2,3,0,1:T(8,128)(2,1)} async-done(((bf16[1,8,32,3,1536]{4,2,3,0,1:T(8,128)(2,1)}), bf16[1,8,32,3,1536]{4,2,3,0,1:T(8,128)(2,1)}, u32[]{:S(2)}, u32[]{:S(2)}) %all-to-all-start) | async-done | bytes 2359328 | tf_op jit(solution)/shard_map/all_to_all | solution.py:49
  253.3 4.2 %reshape.96 = bf16[8,32,3,12,128]{4,3,1,2,0:T(8,128)(2,1)S(1)} reshape(bf16[1,8,32,3,1536]{4,2,3,0,1:T(8,128)(2,1)} %all-to-all-done) | data formatting | bytes 4718592 | tf_op jit(solution)/shard_map/reshape | solution.py:23
  257.5 1.9 fusion.28
  259.4 3.3 %fusion.30 = (f32[32,12,8]{2,1,0:T(8,128)S(1)}, f32[32,12,8,8]{2,3,1,0:T(8,128)S(1)}) fusion(bf16[8,32,1,12,128]{4,3,1,2,0:T(8,128)(2,1)} %get-tuple-element.28, bf16[8,32,1,12,128]{4,3,1,2,0:T(8,128)(2,1)} %get-tuple-element.29), kind=kOutput, calls=%fused_computation.51 | convolution fusion | flops 6365191 | bytes 1683456 | tf_op jit(solution)/shard_map/sub | solution.py:29
  262.6 0.8 fusion.20
  263.4 0.2 copy.60
  263.6 1.4 reshape.97
  265.0 4.4 %all-to-all-start.1 = ((bf16[8,1,32,1536]{3,2,1,0:T(8,128)(2,1)}), bf16[8,1,32,1536]{3,2,1,0:T(8,128)(2,1)}, u32[]{:S(2)}, u32[]{:S(2)}) async-start(bf16[8,1,32,1536]{3,2,1,0:T(8,128)(2,1)} %bitcast.11), calls=%async_computation.1 | async-start | bytes 1572864 | tf_op jit(solution)/shard_map/all_to_all | solution.py:50
  269.4 0.0 all-gather.5.cloned.1.call-done
  269.4 7.0 %copy.62 = bf16[512,2,1536]{0,2,1:T(8,128)(2,1)S(1)} copy(bf16[512,2,1536]{2,1,0:T(2,128)(2,1)} %all-gather.5.cloned.1.call-done) | data formatting | bytes 6291456 | tf_op jit(solution)/shard_map/all_gather | solution.py:58
  276.4 2.2 fusion.14
  278.6 2.5 fusion.29
  281.0 1.9 fusion.9
  282.9 3.2 %copy.67 = f32[1,1,256,1536]{3,2,1,0:T(8,128)} copy(f32[1,1,256,1536]{2,3,1,0:T(8,128)} %bitcast.89) | data formatting | bytes 3145728 | tf_op jit(solution)/shard_map/reshape | solution.py:69
  286.1 4.1 %all-to-all-done.1 = bf16[8,1,32,1536]{3,2,1,0:T(8,128)(2,1)} async-done(((bf16[8,1,32,1536]{3,2,1,0:T(8,128)(2,1)}), bf16[8,1,32,1536]{3,2,1,0:T(8,128)(2,1)}, u32[]{:S(2)}, u32[]{:S(2)}) %all-to-all-start.1) | async-done | bytes 786464 | tf_op jit(solution)/shard_map/all_to_all | solution.py:50
  290.2 2.9 fusion.16
  293.1 0.0 copy-done.1
  (14 shorter events, 0.0 us)
Async XLA Ops:
  6.5 1.4 copy-start
  6.5 121.9 %all-gather.3.cloned.1.call-start = ((), (), s32[]{:S(2)}) async-start(), calls=%async_computation.3 | async-start | bytes 14155776 | tf_op jit(solution)/shard_map/all_gather | solution.py:52
  7.3 157.4 %reduce-scatter.2.cloned.1.call-start = ((), (), s32[]{:S(2)}) async-start(), calls=%async_computation.4 | async-start | bytes 2359296 | tf_op jit(solution)/shard_map/reduce_scatter | solution.py:56
  140.2 26.8 %copy-start.2 = (bf16[1,1,256,3,1536]{4,2,3,1,0:T(8,128)(2,1)S(1)}, bf16[1,1,256,3,1536]{4,2,3,1,0:T(8,128)(2,1)}, u32[]{:S(2)}) copy-start(bf16[1,1,256,3,1536]{4,2,3,1,0:T(8,128)(2,1)} %param.7) | copy-start | bytes 7077892
  140.2 129.2 %all-gather.5.cloned.1.call-start = ((), (), s32[]{:S(2)}) async-start(), calls=%async_computation.5 | async-start | bytes 3538944 | tf_op jit(solution)/shard_map/all_gather | solution.py:58
  168.5 4.8 %copy-start.7 = (s32[2]{0:T(128)S(1)}, s32[2]{0:T(128)}, u32[]{:S(2)}) copy-start(s32[2]{0:T(128)} %param.13) | copy-start | bytes 28
  168.5 84.8 %all-to-all-start = ((bf16[1,8,32,3,1536]{4,2,3,0,1:T(8,128)(2,1)}), bf16[1,8,32,3,1536]{4,2,3,0,1:T(8,128)(2,1)}, u32[]{:S(2)}, u32[]{:S(2)}) async-start(bf16[1,8,32,3,1536]{4,2,3,0,1:T(8,128)(2,1)} %copy.55), calls=%async_computation | async-start | bytes 4718592 | tf_op jit(solution)/shard_map/all_to_all | solution.py:49
  173.3 3.9 %copy-start.8 = (s32[2]{0:T(128)S(1)}, s32[2]{0:T(128)}, u32[]{:S(2)}) copy-start(s32[2]{0:T(128)} %param.12) | copy-start | bytes 28
  173.3 4.5 %copy-start.5 = (bf16[1,1,256,1536]{3,2,1,0:T(8,128)(2,1)S(1)}, bf16[1,1,256,1536]{3,2,1,0:T(8,128)(2,1)}, u32[]{:S(2)}) copy-start(bf16[1,1,256,1536]{3,2,1,0:T(8,128)(2,1)} %param.8) | copy-start | bytes 2359300
  259.4 3.3 %copy-start.4 = (bf16[8,32,1,12,128]{4,3,1,2,0:T(8,128)(2,1)S(1)}, bf16[8,32,1,12,128]{4,3,1,2,0:T(8,128)(2,1)}, u32[]{:S(2)}) copy-start(bf16[8,32,1,12,128]{4,3,1,2,0:T(8,128)(2,1)} %get-tuple-element.27) | copy-start | bytes 2359300
  265.0 25.2 %all-to-all-start.1 = ((bf16[8,1,32,1536]{3,2,1,0:T(8,128)(2,1)}), bf16[8,1,32,1536]{3,2,1,0:T(8,128)(2,1)}, u32[]{:S(2)}, u32[]{:S(2)}) async-start(bf16[8,1,32,1536]{3,2,1,0:T(8,128)(2,1)} %bitcast.11), calls=%async_computation.1 | async-start | bytes 1572864 | tf_op jit(solution)/shard_map/all_to_all | solution.py:50
  282.9 7.3 %copy-start.3 = (f32[1,1,256,1536]{3,2,1,0:T(8,128)S(1)}, f32[1,1,256,1536]{3,2,1,0:T(8,128)}, u32[]{:S(2)}) copy-start(f32[1,1,256,1536]{3,2,1,0:T(8,128)} %copy.54) | copy-start | bytes 4718596
  282.9 7.3 %copy-start.6 = (bf16[1,1,256,1536]{3,2,1,0:T(8,128)(2,1)S(1)}, bf16[1,1,256,1536]{3,2,1,0:T(8,128)(2,1)}, u32[]{:S(2)}) copy-start(bf16[1,1,256,1536]{3,2,1,0:T(8,128)(2,1)} %param.9) | copy-start | bytes 2359300
  282.9 10.2 %copy-start.1 = (bf16[2,64,2048]{2,1,0:T(8,128)(2,1)S(1)}, bf16[2,64,2048]{2,1,0:T(8,128)(2,1)}, u32[]{:S(2)}) copy-start(bf16[2,64,2048]{2,1,0:T(8,128)(2,1)} %param.10) | copy-start | bytes 1572868
Sparse Core Ops, SparseCore 0:
  9.0 119.4 all-gather.2
  140.3 24.3 reduce-scatter.1
  167.1 75.9 all-gather.4
where the time goes:
time: 300 us
  waiting for transfers between devices  215 us (72%)
  local copies, waits for them, and re-layouts  36.4 us (12%)
  matrix products  14.6 us (5%)
  between operations  14.5 us (5%)
  other arithmetic  10.4 us (3%)
  starting transfers between devices  9.21 us (3%)
    all_gather x1, waiting for transfers between devices, body(): weight_piece = lax.all_gather(kv_weight, 'seq', axis=0, tiled=True)  119 us
    all_to_all x1, waiting for transfers between devices, body(): lax.all_to_all(blocked, 'seq', split_axis=1, concat_axis=0, tiled=True)  66.2 us
    reduce_scatter x1, waiting for transfers between devices, body(): lax.psum_scatter(partial_sum, 'grp', scatter_dimension=0, tiled=True)  24.4 us
    unnamed x21, local copies, waits for them, and re-layouts  12.5 us
    all_gather x1, local copies, waits for them, and re-layouts, body(): pairs = lax.all_gather(own_rows, 'seq', axis=0, tiled=True)  7 us
  transfers between devices with their start and end apart: 5, of which 4 were waited for; matrix products, arithmetic and copies ran while one was open for 15% of the time, Pallas kernels for 0%

commit v1 on v0

v1 whole, which is shorter than its diff:
```python
import functools
import math

import jax
import jax.numpy as jnp
from jax import lax
from jax.experimental import pallas as pl
from jax.experimental.pallas import tpu as pltpu
from jax.sharding import PartitionSpec as P


HDIM = 128
BF16 = jnp.bfloat16
F32 = jnp.float32


def swap(value, axis, bits):
    pairs = [(i, i ^ bits) for i in range(lax.axis_size(axis))]
    return lax.ppermute(value, axis, pairs)


def scores_of(queries, key_rows):
    scores = lax.dot_general(queries, key_rows, (((1,), (1,)), ((), ())), preferred_element_type=F32)
    return scores * (1.0 / math.sqrt(HDIM))


def softmax(scores):
    powered = jnp.exp(scores - jnp.max(scores, axis=-1, keepdims=True))
    return (powered * (1.0 / jnp.sum(powered, axis=-1, keepdims=True))).astype(BF16)


def lanes(head):
    return slice(head * HDIM, (head + 1) * HDIM)


def block_cols(width, most=3):
    heads = width // HDIM
    return HDIM * max(n for n in range(1, most + 1) if heads % n == 0)


def prompt_kernel(scalar_ref, in_ref, out_ref):
    out_ref[0] = in_ref[...]


def prompt_blocks(states, side, sides, blocks):
    prompts, rows, feats = states.shape
    rows, feats = rows // sides, feats // blocks
    if feats % HDIM:
        cut = lax.dynamic_slice_in_dim(states, side * rows, rows, 1)
        return cut.reshape(prompts, rows, blocks, feats).transpose(2, 0, 1, 3)
    return pl.pallas_call(
        prompt_kernel,
        grid_spec=pltpu.PrefetchScalarGridSpec(
            num_scalar_prefetch=1,
            grid=(blocks,),
            in_specs=[pl.BlockSpec((prompts, rows, feats), lambda j, s: (0, s[0], j))],
            out_specs=pl.BlockSpec((1, prompts, rows, feats), lambda j, s: (j, 0, 0, 0)),
        ),
        out_shape=jax.ShapeDtypeStruct((blocks, prompts, rows, feats), BF16),
        name="prompt_blocks",
    )(side.reshape(1), states)


def project_kernel(n_rows, n_grp, scalar_ref, *refs):
    state_refs = refs[: 2 * n_rows]
    weight_refs = refs[2 * n_rows : 2 * n_rows + n_grp]
    kept_ref, sent_ref = refs[2 * n_rows + n_grp :]
    rows = state_refs[0].shape[1]
    first = pl.program_id(0) == 0
    for i in range(n_rows):
        total = None
        for core in range(2):
            for g in range(n_grp):
                part = jnp.dot(
                    state_refs[2 * i + core][g], weight_refs[g][core], preferred_element_type=F32
                )
                total = part if total is None else total + part

        @pl.when(first)
        def _(total=total, i=i):
            kept_ref[i * rows : (i + 1) * rows, :] = total

        @pl.when(jnp.logical_not(first))
        def _(total=total, i=i):
            sent_ref[i * rows : (i + 1) * rows, :] = total.astype(BF16)


def project(states, weights, near):
    n_grp, rows, feats = states[0].shape
    n_rows = len(states) // 2
    cols = weights[0].shape[2] // 2
    whole = pl.BlockSpec((n_grp, rows, feats), lambda j, s: (0, 0, 0))
    side = pl.BlockSpec((2, feats, cols), lambda j, s: (0, 0, j ^ s[0]))
    out = pl.BlockSpec((n_rows * rows, cols), lambda j, s: (0, 0))
    return pl.pallas_call(
        functools.partial(project_kernel, n_rows, n_grp),
        grid_spec=pltpu.PrefetchScalarGridSpec(
            num_scalar_prefetch=1,
            grid=(2,),
            in_specs=[whole] * len(states) + [side] * n_grp,
            out_specs=[out, out],
        ),
        out_shape=[
            jax.ShapeDtypeStruct((n_rows * rows, cols), F32),
            jax.ShapeDtypeStruct((n_rows * rows, cols), BF16),
        ],
        name="project",
    )(near.reshape(1), *states, *weights)


def spatial_kernel(qkv_ref, residual_ref, out_ref):
    for head in range(out_ref.shape[1] // HDIM):
        at = lanes(head)
        weights = softmax(scores_of(qkv_ref[0, :, at], qkv_ref[1, :, at]))
        result = jnp.dot(weights, qkv_ref[2, :, at], preferred_element_type=F32)
        out_ref[:, at] = residual_ref[:, at].astype(F32) + result


def spatial_attention(qkv, residual):
    _, tokens, width = qkv.shape
    cols = block_cols(width)
    return pl.pallas_call(
        spatial_kernel,
        grid=(width // cols,),
        in_specs=[
            pl.BlockSpec((3, tokens, cols), lambda j: (0, 0, j)),
            pl.BlockSpec((tokens, cols), lambda j: (0, j)),
        ],
        out_specs=pl.BlockSpec((tokens, cols), lambda j: (0, j)),
        out_shape=jax.ShapeDtypeStruct((tokens, width), F32),
        name="spatial",
    )(qkv, residual)


def temporal_kernel(frames, scalar_ref, *refs):
    frame_refs, out_ref = refs[:frames], refs[frames]
    _, tokens, cols = frame_refs[0].shape
    rows = frames * tokens
    row_token = lax.rem(lax.broadcasted_iota(jnp.int32, (rows, rows), 0), tokens)
    col_token = lax.rem(lax.broadcasted_iota(jnp.int32, (rows, rows), 1), tokens)
    same = row_token == col_token
    for head in range(cols // HDIM):
        at = lanes(head)
        query, key_rows, values = (
            jnp.concatenate([r[i, :, at] for r in frame_refs], axis=0) for i in range(3)
        )
        weights = softmax(jnp.where(same, scores_of(query, key_rows), -jnp.inf))
        result = jnp.dot(weights, values, preferred_element_type=F32).astype(BF16)
        for j in range(frames):
            out_ref[scalar_ref[j], :, at] = result[j * tokens : (j + 1) * tokens]


def temporal_attention(places, pieces):
    frames = len(pieces)
    _, tokens, width = pieces[0].shape
    cols = block_cols(width)
    return pl.pallas_call(
        functools.partial(temporal_kernel, frames),
        grid_spec=pltpu.PrefetchScalarGridSpec(
            num_scalar_prefetch=1,
            grid=(width // cols,),
            in_specs=[pl.BlockSpec((3, tokens, cols), lambda j, s: (0, 0, j))] * frames,
            out_specs=pl.BlockSpec((frames, tokens, cols), lambda j, s: (0, 0, j)),
        ),
        out_shape=jax.ShapeDtypeStruct((frames, tokens, width), BF16),
        name="temporal",
    )(places, *pieces)


def weigh_kernel(bias_ref, kept_ref, come_ref, *refs):
    query_refs, out_ref = refs[:-1], refs[-1]
    key_rows = (kept_ref[...] + come_ref[...].astype(F32)).astype(BF16)
    for j, query_ref in enumerate(query_refs):
        scores = scores_of(query_ref[...], key_rows) + bias_ref[...]
        out_ref[0, j] = softmax(scores)


def cross_weights(bias, kept, come, queries):
    rows, width = kept.shape
    tokens = queries[0].shape[0]
    heads = width // HDIM
    key_spec = pl.BlockSpec((rows, HDIM), lambda h: (0, h))
    return pl.pallas_call(
        weigh_kernel,
        grid=(heads,),
        in_specs=[pl.BlockSpec((1, rows), lambda h: (0, 0)), key_spec, key_spec]
        + [pl.BlockSpec((tokens, HDIM), lambda h: (0, h))] * len(queries),
        out_specs=pl.BlockSpec((1, len(queries), tokens, rows), lambda h: (h, 0, 0, 0)),
        out_shape=jax.ShapeDtypeStruct((heads, len(queries), tokens, rows), BF16),
        name="cross_weights",
    )(bias, kept, come, *queries)


def value_kernel(weight_ref, kept_ref, come_ref, *out_refs):
    values = (kept_ref[...] + come_ref[...].astype(F32)).astype(BF16)
    for j, out_ref in enumerate(out_refs):
        result = jnp.dot(weight_ref[0, j], values, preferred_element_type=F32)
        out_ref[...] = result.astype(out_ref.dtype)


def cross_values(weights, kept, come):
    rows, width = kept.shape
    heads, count, tokens, _ = weights.shape
    key_spec = pl.BlockSpec((rows, HDIM), lambda h: (0, h))
    return pl.pallas_call(
        value_kernel,
        grid=(heads,),
        in_specs=[pl.BlockSpec((1, count, tokens, rows), lambda h: (h, 0, 0, 0)), key_spec, key_spec],
        out_specs=[pl.BlockSpec((tokens, HDIM), lambda h: (0, h))] * count,
        out_shape=[jax.ShapeDtypeStruct((tokens, width), F32 if j == 0 else BF16) for j in range(count)],
        name="cross_values",
    )(weights, kept, come)


def final_kernel(scalar_ref, base_ref, temporal_ref, *refs):
    piece_refs, out_ref = refs[:-1], refs[-1]
    partial = base_ref[...] + temporal_ref[...].astype(F32)
    for j, piece_ref in enumerate(piece_refs):

        @pl.when(pl.program_id(0) == j)
        def _(piece_ref=piece_ref):
            out_ref[...] = (partial + piece_ref[...].astype(F32)).astype(BF16)


def final_sum(place, base, temporal, pieces):
    tokens, width = base.shape
    cols = width // len(pieces)
    side = pl.BlockSpec((tokens, cols), lambda j, s: (0, j ^ s[0]))
    whole = pl.BlockSpec((tokens, cols), lambda j, s: (0, 0))
    return pl.pallas_call(
        final_kernel,
        grid_spec=pltpu.PrefetchScalarGridSpec(
            num_scalar_prefetch=1,
            grid=(len(pieces),),
            in_specs=[side, side] + [whole] * len(pieces),
            out_specs=side,
        ),
        out_shape=jax.ShapeDtypeStruct((tokens, width), BF16),
        name="final",
    )(place.reshape(1), base, temporal, *pieces)


def temporal_plan(seq):
    if seq != 8:
        return [(k, k) for k in range(seq - 1, 0, -1)]
    return [(6, 2), (2, 6), (7, 3), (3, 7), (4, 4), (5, 5), (1, 1)]


def block(latent_qkv, cross_query, residual, prompt_states, kv_weight, prompt_lengths, assignment):
    tokens, width = cross_query.shape[2:]
    seq, grp, sides = (lax.axis_size(name) for name in ("seq", "grp", "hd"))
    me, group, side = (lax.axis_index(name) for name in ("seq", "grp", "hd"))
    core, near = me & 1, (me >> 1) & 1
    place = core * 2 + near
    feats = kv_weight.shape[0]
    _, rows_here, _ = prompt_states.shape
    rows_side = rows_here // sides
    rows = seq * rows_side

    parts = prompt_blocks(prompt_states, side, sides, seq)
    parts = lax.all_to_all(parts, "seq", 0, 0, tiled=True)

    qkv = latent_qkv[0, 0].transpose(1, 0, 2)
    share = tokens // seq
    steps = temporal_plan(seq)
    own_block = lax.dynamic_slice_in_dim(qkv, me * share, share, 1)
    pieces, sources = [own_block], [me]
    for even, odd in steps:
        crossing = even & 1
        target = me ^ jnp.where(core == 0, even, odd)
        block = lax.dynamic_slice_in_dim(qkv, target * share, share, 1)
        pairs = [(i, i ^ (odd if i & 1 else even)) for i in range(seq)]
        pieces.append(lax.ppermute(block, "seq", pairs))
        sender_core = core ^ crossing
        sources.append(me ^ jnp.where(sender_core == 0, even, odd))

    half = width // 2
    weights = []
    for kind in range(2):
        plane = kv_weight[:, kind]
        mine = lax.dynamic_slice_in_dim(plane, core * half, half, 1)
        theirs = lax.dynamic_slice_in_dim(plane, (1 - core) * half, half, 1)
        come = swap(theirs, "seq", 1)
        both = jnp.stack([mine, come])
        weights.append([both] + [swap(both, "grp", k) for k in range(1, grp)])

    def slot(k):
        index = jnp.take(assignment, group ^ k)
        return lax.dynamic_index_in_dim(parts, index, 1, keepdims=False).reshape(rows, feats)

    wanted = jnp.stack([slot(0)] + [swap(slot(k), "grp", k) for k in range(1, grp)])
    n_pairs = [(s, h) for s in range(seq) for h in range(sides)]
    states = []
    for k in range(sides):
        for c in range(2):
            pairs = [(s * sides + h, (s ^ c) * sides + (h ^ k)) for s, h in n_pairs]
            states.append(wanted if k + c == 0 else lax.ppermute(wanted, ("seq", "hd"), pairs))

    quarter = width // 4
    query = cross_query[0, 0]
    queries = []
    for k, other in enumerate((0, 2, 1, 3)):
        block = lax.dynamic_slice_in_dim(query, (place ^ other) * quarter, quarter, 1)
        queries.append(block if k == 0 else swap(block, "seq", k))

    sums = []
    for kind in range(2):
        kept, sent = project(states, weights[kind], near)
        kept = kept + swap(sent, "seq", 2).astype(F32)
        bit = 4
        while bit < seq:
            come = swap(kept.astype(BF16), "seq", bit)
            bit *= 2
            if bit < seq:
                kept = kept + come.astype(F32)
        sums.append((kept, come))

    row = jnp.arange(rows * sides)
    which, source, inner = row // rows, (row % rows) // rows_side, row % rows_side
    position = source * rows_here + (which ^ side) * rows_side + inner
    length = jnp.take(prompt_lengths, jnp.take(assignment, group))
    bias = jnp.where(position < length, 0.0, -1e9).astype(F32)[None]

    base = spatial_attention(qkv, residual[0, 0])
    temporal = temporal_attention(jnp.stack(sources).astype(jnp.int32), pieces)
    temporal = lax.all_to_all(temporal, "seq", 0, 0, tiled=True).reshape(tokens, width)

    shares = cross_weights(bias, *sums[0], queries)
    crossed = cross_values(shares, *sums[1])
    results = [crossed[0]]
    for k in range(1, 4):
        results.append(swap(crossed[k], "seq", k))
    results[1], results[2] = results[2], results[1]
    return final_sum(place, base, temporal, results)[None, None]


def solution(mesh):
    return jax.shard_map(
        block,
        mesh=mesh,
        in_specs=(
            P("grp", "seq", None, None, "hd"),
            P("grp", "seq", None, "hd"),
            P("grp", "seq", None, "hd"),
            P(None, "seq", "grp"),
            P(("grp", "seq"), None, "hd"),
            P(),
            P(),
        ),
        out_specs=P("grp", "seq", None, "hd"),
        check_vma=False,
    )
```

time: 300 us -> 187 us (0.62)
  the two profiles are of different devices: /device:TPU:0 before, /device:TPU:25 now
where the time goes in v1:
time: 187 us; the launch traced here: 185 us
  waiting for transfers between devices  85.4 us (46%)
  Pallas kernels  39.6 us (21%)
  starting transfers between devices  33 us (18%)
  local copies, waits for them, and re-layouts  19.4 us (10%)
  other arithmetic  5.87 us (3%)
  between operations  2.27 us (1%)
    ppermute x15, waiting for transfers between devices, swap(): return lax.ppermute(value, axis, pairs)  56 us
    ppermute x7, waiting for transfers between devices, block(): pieces.append(lax.ppermute(block, 'seq', pairs))  23.5 us
    ppermute x15, starting transfers between devices, swap(): return lax.ppermute(value, axis, pairs)  11.6 us
    pallas_call x2, Pallas kernels, project(): pl.pallas_call(functools.partial(project_kernel, n_rows, n_grp), grid_spe...  8.62 us
    all_to_all x1, starting transfers between devices, block(): lax.all_to_all(temporal, 'seq', 0, 0, tiled=True).reshape(tokens, width)  7.86 us
    pallas_call x1, Pallas kernels, temporal_attention(): pl.pallas_call(functools.partial(temporal_kernel, frames), grid_spec=pltp...  6.83 us
    pallas_call x1, Pallas kernels, spatial_attention(): pl.pallas_call(spatial_kernel, grid=(width // cols,), in_specs=[pl.BlockS...  6.31 us
    unnamed x60, local copies, waits for them, and re-layouts  5.96 us
  transfers between devices with their start and end apart: 27, of which 10 were waited for; matrix products, arithmetic and copies ran while one was open for 6% of the time, Pallas kernels for 19%

profile of v1, /device:TPU:25, one launch (start us, length us, event | category | flops | bytes accessed | tf_op | source)
XLA Modules:
  0.0 185.5 jit_solution(4410499397130048573)
XLA Ops:
  0.0 4.3 %fusion.6 = (bf16[256,1,1536]{2,1,0:T(2,128)(2,1)S(1)}, bf16[256,1,1536]{2,1,0:T(2,128)(2,1)S(1)}) fusion(bf16[256,2,1536]{2,1,0:T(2,128)(2,1)} %param.11), kind=kLoop, calls=%fused_computation.43 | loop fusion | bytes 3145728 | tf_op jit(solution)/shard_map/slice | solution.py:280
  4.4 4.2 %constant_dynamic-slice_fusion.1 = (bf16[256,1,768]{2,1,0:T(2,128)(2,1)}, bf16[256,1,768]{2,1,0:T(2,128)(2,1)}, bf16[256,1,768]{2,1,0:T(2,128)(2,1)S(1)}, bf16[256,1,768]{2,1,0:T(2,128)(2,1)}) fusion(bf16[256,1,1536]{2,1,0:T(2,128)(2,1)S(1)} %get-tuple-element.68, s32[]{:T(128)S(6)} %select_n.185, s32[]{:T(128)S(6)} %select_n.186, ...), kind=kLoop, calls=%fused_computation.27 | loop fusion | bytes 3145736 | tf_op jit(solution)/shard_map/dynamic_slice | solution.py:281
  8.5 0.8 copy.22
  10.0 4.3 %prompt_blocks.1 = bf16[8,2,32,256]{3,2,1,0:T(8,128)(2,1)} custom-call(s32[1]{0:T(128)} %bitcast.34.scalar_ref, bf16[2,64,2048]{2,1,0:T(8,128)(2,1)} %in_ref.1), custom_call_target="tpu_custom_call" | custom-call | tf_op jit(solution)/shard_map/prompt_blocks/pallas_call | solution.py:51
  14.3 4.8 %all-to-all-start.1 = ((bf16[8,2,32,256]{3,2,1,0:T(8,128)(2,1)}), bf16[8,2,32,256]{3,2,1,0:T(8,128)(2,1)}, u32[]{:S(2)}, u32[]{:S(2)}) async-start(bf16[8,2,32,256]{3,2,1,0:T(8,128)(2,1)} %prompt_blocks.1), calls=%async_computation.1 | async-start | bytes 524288 | tf_op jit(solution)/shard_map/all_to_all | solution.py:261
  19.1 0.8 copy.20
  22.4 1.2 pad_maximum_fusion.refs_4_
  23.7 1.3 collective-permute-start.12
  24.9 1.4 all-to-all-done.1
  26.4 1.0 constant_dynamic-slice_fusion.5
  27.4 1.3 collective-permute-start.7
  28.6 1.1 dynamic-slice_bitcast_fusion
  29.8 1.7 collective-permute-start.1
  31.5 14.0 %collective-permute-done.7 = bf16[256,256]{1,0:T(8,128)(2,1)S(1)} collective-permute-done((bf16[256,256]{1,0:T(8,128)(2,1)S(1)}, bf16[256,256]{1,0:T(8,128)(2,1)S(1)}, u32[]{:S(2)}, u32[]{:S(2)}) %collective-permute-start.7) | collective-permute-done | bytes 131104 | tf_op jit(solution)/shard_map/ppermute | solution.py:19
  45.5 1.1 collective-permute-start.2
  46.7 1.0 collective-permute-start.10
  47.7 1.1 pad_maximum_fusion.1.refs_4_
  48.8 1.3 collective-permute-start.19
  50.1 1.0 collective-permute-start.8
  51.1 4.0 %collective-permute-done.2.refs_3_ = bf16[3,32,1536]{2,1,0:T(8,128)(2,1)S(1)} collective-permute-done((bf16[3,32,1536]{2,1,0:T(8,128)(2,1)S(1)}, bf16[3,32,1536]{2,1,0:T(8,128)(2,1)S(1)}, u32[]{:S(2)}, u32[]{:S(2)}) %collective-permute-start.2) | collective-permute-done | bytes 294944 | tf_op jit(solution)/shard_map/ppermute | solution.py:273
  55.1 1.2 collective-permute-start.9
  56.4 1.4 collective-permute-start.3
  57.7 1.0 collective-permute-start.4
  58.7 4.5 %collective-permute-done.9.refs_2_ = bf16[2,256,256]{2,1,0:T(8,128)(2,1)S(1)} collective-permute-done((bf16[2,256,256]{2,1,0:T(8,128)(2,1)S(1)}, bf16[2,256,256]{2,1,0:T(8,128)(2,1)S(1)}, u32[]{:S(2)}, u32[]{:S(2)}) %collective-permute-start.9) | collective-permute-done | bytes 262176 | tf_op jit(solution)/shard_map/ppermute | solution.py:297
  63.9 4.3 %project.2 = (f32[512,384]{1,0:T(8,128)}, bf16[512,384]{1,0:T(8,128)(2,1)}) custom-call(s32[1]{0:T(128)} %bitcast.33.scalar_ref, bf16[2,256,256]{2,1,0:T(8,128)(2,1)} %copy-done.7, bf16[2,256,256]{2,1,0:T(8,128)(2,1)} %copy-done.9, bf16[2,256,256]{2,1,0:T(8,128)(2,1)} %copy-done.10, bf16[2,256,256]{2,1,0:T(8,128)(2,1)} %copy-done.8, ...), custom_call_target="tpu_custom_call" | custom-call | tf_op jit(solution)/shard_map/project/pallas_call | solution.py:95
  68.2 0.9 collective-permute-start.13
  69.8 18.2 %collective-permute-done.4.refs_5_ = bf16[3,32,1536]{2,1,0:T(8,128)(2,1)} collective-permute-done((bf16[3,32,1536]{2,1,0:T(8,128)(2,1)}, bf16[3,32,1536]{2,1,0:T(8,128)(2,1)}, u32[]{:S(2)}, u32[]{:S(2)}) %collective-permute-start.4) | collective-permute-done | bytes 294944 | tf_op jit(solution)/shard_map/ppermute | solution.py:273
  88.0 1.2 collective-permute-done.5.refs_6_
  89.2 0.7 copy-done.19
  89.9 6.8 %temporal.1 = bf16[8,32,1536]{2,1,0:T(8,128)(2,1)} custom-call(s32[8]{0:T(128)} %stack.59.scalar_ref, bf16[3,32,1536]{2,1,0:T(8,128)(2,1)} %get-tuple-element.64.refs_0_, bf16[3,32,1536]{2,1,0:T(8,128)(2,1)} %copy-done.17, bf16[3,32,1536]{2,1,0:T(8,128)(2,1)} %collective-permute-done.1.refs_2_, bf16[3,32,1536]{2,1,0:T(8,128)(2,1)} %copy-done.18, ...), custom_call_target="tpu_custom_call" | custom-call | tf_op jit(solution)/shard_map/temporal/pallas_call | solution.py:157
  96.7 7.9 %all-to-all-start = ((bf16[8,32,1536]{2,1,0:T(8,128)(2,1)}), bf16[8,32,1536]{2,1,0:T(8,128)(2,1)S(1)}, u32[]{:S(2)}, u32[]{:S(2)}) async-start(bf16[8,32,1536]{2,1,0:T(8,128)(2,1)} %temporal.1), calls=%async_computation | async-start | bytes 1572864 | tf_op jit(solution)/shard_map/all_to_all | solution.py:326
  104.6 0.9 copy-done.12
  105.5 4.3 %project.3 = (f32[512,384]{1,0:T(8,128)}, bf16[512,384]{1,0:T(8,128)(2,1)}) custom-call(s32[1]{0:T(128)} %bitcast.33.scalar_ref, bf16[2,256,256]{2,1,0:T(8,128)(2,1)} %copy-done.7, bf16[2,256,256]{2,1,0:T(8,128)(2,1)} %copy-done.9, bf16[2,256,256]{2,1,0:T(8,128)(2,1)} %copy-done.10, bf16[2,256,256]{2,1,0:T(8,128)(2,1)} %copy-done.8, ...), custom_call_target="tpu_custom_call" | custom-call | tf_op jit(solution)/shard_map/project/pallas_call | solution.py:95
  110.1 2.0 %fusion.5 = (bf16[512,384]{1,0:T(8,128)(2,1)S(1)}, f32[512,384]{1,0:T(8,128)}) fusion(f32[512,384]{1,0:T(8,128)S(1)} %copy-done.13, bf16[512,384]{1,0:T(8,128)(2,1)} %collective-permute-done.13), kind=kLoop, calls=%fused_computation.42 | loop fusion | flops 589824 | bytes 2359296 | tf_op jit(solution)/shard_map/convert_element_type | solution.py:312
  112.3 19.1 %collective-permute-done.20 = bf16[512,384]{1,0:T(8,128)(2,1)S(1)} collective-permute-done((bf16[512,384]{1,0:T(8,128)(2,1)}, bf16[512,384]{1,0:T(8,128)(2,1)S(1)}, u32[]{:S(2)}, u32[]{:S(2)}) %collective-permute-start.20) | collective-permute-done | bytes 393248 | tf_op jit(solution)/shard_map/ppermute | solution.py:19
  131.4 1.0 fusion.4
  132.6 0.8 dynamic-slice_bitcast_fusion.8
  133.5 1.0 collective-permute-start.15
  134.5 2.1 %collective-permute-start.16 = (bf16[256,384]{1,0:T(8,128)(2,1)S(1)}, bf16[256,384]{1,0:T(8,128)(2,1)S(1)}, u32[]{:S(2)}, u32[]{:S(2)}) collective-permute-start(bf16[256,384]{1,0:T(8,128)(2,1)S(1)} %get-tuple-element.75), channel_id=1, source_target_pairs={{0,4},{2,6},{4,0},{6,2},{8,12},{10,14},{12,8},{14,10},{1,5},{3,7},... | collective-permute-start | bytes 589832 | tf_op jit(solution)/shard_map/ppermute | solution.py:19
  138.4 8.6 %collective-permute-done.16.refs_2_ = bf16[256,384]{1,0:T(8,128)(2,1)S(1)} collective-permute-done((bf16[256,384]{1,0:T(8,128)(2,1)S(1)}, bf16[256,384]{1,0:T(8,128)(2,1)S(1)}, u32[]{:S(2)}, u32[]{:S(2)}) %collective-permute-start.16) | collective-permute-done | bytes 196640 | tf_op jit(solution)/shard_map/ppermute | solution.py:19
  147.0 11.6 %collective-permute-done.17.refs_3_ = bf16[256,384]{1,0:T(8,128)(2,1)S(1)} collective-permute-done((bf16[256,384]{1,0:T(8,128)(2,1)S(1)}, bf16[256,384]{1,0:T(8,128)(2,1)S(1)}, u32[]{:S(2)}, u32[]{:S(2)}) %collective-permute-start.17) | collective-permute-done | bytes 196640 | tf_op jit(solution)/shard_map/ppermute | solution.py:19
  159.5 5.2 %cross_weights.1.weight_ref = bf16[3,4,256,512]{3,2,1,0:T(8,128)(2,1)} custom-call(f32[1,512]{1,0:T(1,128)} %compare_select_fusion.bias_ref, f32[512,384]{1,0:T(8,128)} %get-tuple-element.57.kept_ref, bf16[512,384]{1,0:T(8,128)(2,1)} %copy-done.16, bf16[256,384]{1,0:T(8,128)(2,1)} %get-tuple-element.74.refs_0_, bf16[256,384]{1,0:T(8,128)(2,1)} %copy-done.20, ...), custom_call_target="tpu_custom_call" | custom-call | tf_op jit(solution)/shard_map/cross_weights/pallas_call | solution.py:183
  164.7 0.8 copy-done.15
  165.4 4.3 %cross_values.1 = (f32[256,384]{1,0:T(8,128)}, bf16[256,384]{1,0:T(8,128)(2,1)}, bf16[256,384]{1,0:T(8,128)(2,1)}, bf16[256,384]{1,0:T(8,128)(2,1)}) custom-call(bf16[3,4,256,512]{3,2,1,0:T(8,128)(2,1)} %cross_weights.1.weight_ref, f32[512,384]{1,0:T(8,128)} %get-tuple-element.55.kept_ref, bf16[512,384]{1,0:T(8,128)(2,1)} %copy-done.15), custom_call_target="tpu_custom_call" | custom-call | tf_op jit(solution)/shard_map/cross_values/pallas_call | solution.py:205
  170.2 1.6 collective-permute-start.24
  171.8 6.3 %spatial.1.base_ref = f32[256,1536]{1,0:T(8,128)} custom-call(bf16[3,256,1536]{2,1,0:T(8,128)(2,1)} %bitcast.80, bf16[256,1536]{1,0:T(8,128)(2,1)} %bitcast.84), custom_call_target="tpu_custom_call" | custom-call | tf_op jit(solution)/shard_map/spatial/pallas_call | solution.py:122
  178.1 2.7 %collective-permute-done.24.refs_3_ = bf16[256,384]{1,0:T(8,128)(2,1)S(1)} collective-permute-done((bf16[256,384]{1,0:T(8,128)(2,1)}, bf16[256,384]{1,0:T(8,128)(2,1)S(1)}, u32[]{:S(2)}, u32[]{:S(2)}) %collective-permute-start.24) | collective-permute-done | bytes 196640 | tf_op jit(solution)/shard_map/ppermute | solution.py:19
  181.5 4.0 %final.1 = bf16[256,1536]{1,0:T(8,128)(2,1)} custom-call(s32[1]{0:T(128)} %bitcast.scalar_ref, f32[256,1536]{1,0:T(8,128)} %spatial.1.base_ref, bf16[256,1536]{1,0:T(8,128)(2,1)} %bitcast.81, f32[256,384]{1,0:T(8,128)} %get-tuple-element.17.refs_0_, bf16[256,384]{1,0:T(8,128)(2,1)} %copy-done.23, bf16[256,384]{1,0:T(8,128)(2,1)} %copy-done.24, ...), custom_call_target="tpu_custom_call" | custom-call | tf_op jit(solution)/shard_map/final/pallas_call | solution.py:230
  (88 shorter events, 7.1 us)
Async XLA Ops:
  8.5 10.6 %copy-start.6 = (bf16[256,1,768]{2,1,0:T(2,128)(2,1)S(1)}, bf16[256,1,768]{2,1,0:T(2,128)(2,1)}, u32[]{:S(2)}) copy-start(bf16[256,1,768]{2,1,0:T(2,128)(2,1)} %get-tuple-element.67) | copy-start | bytes 1179652
  8.5 11.8 %copy-start.26 = (s32[2]{0:T(128)S(1)}, s32[2]{0:T(128)}, u32[]{:S(2)}) copy-start(s32[2]{0:T(128)} %param.13) | copy-start | bytes 28
  9.3 13.0 %copy-start.5 = (bf16[256,1,768]{2,1,0:T(2,128)(2,1)S(1)}, bf16[256,1,768]{2,1,0:T(2,128)(2,1)}, u32[]{:S(2)}) copy-start(bf16[256,1,768]{2,1,0:T(2,128)(2,1)} %get-tuple-element.81) | copy-start | bytes 1179652
  9.3 13.1 %collective-permute-start.11 = (bf16[256,768]{1,0:T(8,128)(2,1)}, bf16[256,768]{1,0:T(8,128)(2,1)}, u32[]{:S(2)}, u32[]{:S(2)}) collective-permute-start(bf16[256,768]{1,0:T(8,128)(2,1)} %bitcast.78), channel_id=1, source_target_pairs={{0,2},{2,0},{4,6},{6,4},{8,10},{10,8},{12,14},{14,12},{1,3},{3,1},... | collective-permute-start | bytes 1179656 | tf_op jit(solution)/shard_map/ppermute | solution.py:19
  14.3 12.0 %all-to-all-start.1 = ((bf16[8,2,32,256]{3,2,1,0:T(8,128)(2,1)}), bf16[8,2,32,256]{3,2,1,0:T(8,128)(2,1)}, u32[]{:S(2)}, u32[]{:S(2)}) async-start(bf16[8,2,32,256]{3,2,1,0:T(8,128)(2,1)} %prompt_blocks.1), calls=%async_computation.1 | async-start | bytes 524288 | tf_op jit(solution)/shard_map/all_to_all | solution.py:261
  19.9 26.8 %collective-permute-start.18 = (bf16[256,768]{1,0:T(8,128)(2,1)}, bf16[256,768]{1,0:T(8,128)(2,1)}, u32[]{:S(2)}, u32[]{:S(2)}) collective-permute-start(bf16[256,768]{1,0:T(8,128)(2,1)} %bitcast.76), channel_id=1, source_target_pairs={{0,2},{2,0},{4,6},{6,4},{8,10},{10,8},{12,14},{14,12},{1,3},{3,1},... | collective-permute-start | bytes 1179656 | tf_op jit(solution)/shard_map/ppermute | solution.py:19
  22.3 6.3 %copy-start = (bf16[1,1,256,3,1536]{4,2,3,1,0:T(8,128)(2,1)S(1)}, bf16[1,1,256,3,1536]{4,2,3,1,0:T(8,128)(2,1)}, u32[]{:S(2)}) copy-start(bf16[1,1,256,3,1536]{4,2,3,1,0:T(8,128)(2,1)} %param.7) | copy-start | bytes 7077892
  23.7 6.1 %copy-start.2 = (bf16[2,256,768]{2,1,0:T(8,128)(2,1)}, bf16[2,256,768]{2,1,0:T(8,128)(2,1)S(1)}, u32[]{:S(2)}) copy-start(bf16[2,256,768]{2,1,0:T(8,128)(2,1)S(1)} %pad_maximum_fusion.refs_4_) | copy-start | bytes 2359300
  23.7 39.8 %collective-permute-start.12 = (bf16[2,256,768]{2,1,0:T(8,128)(2,1)S(1)}, bf16[2,256,768]{2,1,0:T(8,128)(2,1)}, u32[]{:S(2)}, u32[]{:S(2)}) collective-permute-start(bf16[2,256,768]{2,1,0:T(8,128)(2,1)S(1)} %pad_maximum_fusion.refs_4_), channel_id=1, source_target_pairs={{0,16},{16,0},{1,17},{17,1},{2,18},{18,2},{3,19},{19,3},{4,20},{20... | collective-permute-start | bytes 2359304 | tf_op jit(solution)/shard_map/ppermute | solution.py:19
  27.3 4.1 %copy-start.4 = (bf16[256,1,768]{2,1,0:T(2,128)(2,1)S(1)}, bf16[256,1,768]{2,1,0:T(2,128)(2,1)}, u32[]{:S(2)}) copy-start(bf16[256,1,768]{2,1,0:T(2,128)(2,1)} %get-tuple-element.66) | copy-start | bytes 1179652
  27.4 18.2 %collective-permute-start.7 = (bf16[256,256]{1,0:T(8,128)(2,1)S(1)}, bf16[256,256]{1,0:T(8,128)(2,1)S(1)}, u32[]{:S(2)}, u32[]{:S(2)}) collective-permute-start(bf16[256,256]{1,0:T(8,128)(2,1)S(1)} %bitcast.87), channel_id=1, source_target_pairs={{0,16},{16,0},{1,17},{17,1},{2,18},{18,2},{3,19},{19,3},{4,20},{20... | collective-permute-start | bytes 393224 | tf_op jit(solution)/shard_map/ppermute | solution.py:19
  29.8 19.1 %collective-permute-start = (bf16[3,32,1536]{2,1,0:T(8,128)(2,1)S(1)}, bf16[3,32,1536]{2,1,0:T(8,128)(2,1)S(1)}, u32[]{:S(2)}, u32[]{:S(2)}) collective-permute-start(bf16[3,32,1536]{2,1,0:T(8,128)(2,1)S(1)} %get-tuple-element.63), channel_id=1, source_target_pairs={{0,12},{2,6},{4,8},{6,2},{8,4},{10,14},{12,0},{14,10},{1,13},{3,7}... | collective-permute-start | bytes 884744 | tf_op jit(solution)/shard_map/ppermute | solution.py:273
  29.8 20.4 %collective-permute-start.1 = (bf16[3,32,1536]{2,1,0:T(8,128)(2,1)S(1)}, bf16[3,32,1536]{2,1,0:T(8,128)(2,1)}, u32[]{:S(2)}, u32[]{:S(2)}) collective-permute-start(bf16[3,32,1536]{2,1,0:T(8,128)(2,1)S(1)} %get-tuple-element.62), channel_id=1, source_target_pairs={{0,4},{2,14},{4,0},{6,10},{8,12},{10,6},{12,8},{14,2},{1,5},{3,15}... | collective-permute-start | bytes 884744 | tf_op jit(solution)/shard_map/ppermute | solution.py:273
  45.5 9.6 %collective-permute-start.2 = (bf16[3,32,1536]{2,1,0:T(8,128)(2,1)S(1)}, bf16[3,32,1536]{2,1,0:T(8,128)(2,1)S(1)}, u32[]{:S(2)}, u32[]{:S(2)}) collective-permute-start(bf16[3,32,1536]{2,1,0:T(8,128)(2,1)S(1)} %get-tuple-element.61), channel_id=1, source_target_pairs={{0,14},{2,4},{4,10},{6,0},{8,6},{10,12},{12,2},{14,8},{1,15},{3,5}... | collective-permute-start | bytes 884744 | tf_op jit(solution)/shard_map/ppermute | solution.py:273
  46.7 16.8 %copy-start.7 = (bf16[2,256,256]{2,1,0:T(8,128)(2,1)}, bf16[2,256,256]{2,1,0:T(8,128)(2,1)S(1)}, u32[]{:S(2)}) copy-start(bf16[2,256,256]{2,1,0:T(8,128)(2,1)S(1)} %pad_maximum_fusion.2.refs_0_) | copy-start | bytes 786436
  46.7 9.6 %collective-permute-start.10 = (bf16[2,256,256]{2,1,0:T(8,128)(2,1)S(1)}, bf16[2,256,256]{2,1,0:T(8,128)(2,1)S(1)}, u32[]{:S(2)}, u32[]{:S(2)}) collective-permute-start(bf16[2,256,256]{2,1,0:T(8,128)(2,1)S(1)} %pad_maximum_fusion.2.refs_0_), channel_id=1, source_target_pairs={{0,3},{1,2},{2,1},{3,0},{4,7},{5,6},{6,5},{7,4},{8,11},{9,10},{10,... | collective-permute-start | bytes 786440 | tf_op jit(solution)/shard_map/ppermute | solution.py:297
  48.8 47.9 %copy-start.3 = (bf16[2,256,768]{2,1,0:T(8,128)(2,1)}, bf16[2,256,768]{2,1,0:T(8,128)(2,1)S(1)}, u32[]{:S(2)}) copy-start(bf16[2,256,768]{2,1,0:T(8,128)(2,1)S(1)} %pad_maximum_fusion.1.refs_4_) | copy-start | bytes 2359300
  48.8 14.6 %copy-start.17 = (bf16[3,32,1536]{2,1,0:T(8,128)(2,1)}, bf16[3,32,1536]{2,1,0:T(8,128)(2,1)S(1)}, u32[]{:S(2)}) copy-start(bf16[3,32,1536]{2,1,0:T(8,128)(2,1)S(1)} %collective-permute-done.refs_1_) | copy-start | bytes 884740
  48.8 55.7 %collective-permute-start.19 = (bf16[2,256,768]{2,1,0:T(8,128)(2,1)S(1)}, bf16[2,256,768]{2,1,0:T(8,128)(2,1)S(1)}, u32[]{:S(2)}, u32[]{:S(2)}) collective-permute-start(bf16[2,256,768]{2,1,0:T(8,128)(2,1)S(1)} %pad_maximum_fusion.1.refs_4_), channel_id=1, source_target_pairs={{0,16},{16,0},{1,17},{17,1},{2,18},{18,2},{3,19},{19,3},{4,20},{20... | collective-permute-start | bytes 2359304 | tf_op jit(solution)/shard_map/ppermute | solution.py:19
  50.1 7.6 %collective-permute-start.8 = (bf16[2,256,256]{2,1,0:T(8,128)(2,1)S(1)}, bf16[2,256,256]{2,1,0:T(8,128)(2,1)S(1)}, u32[]{:S(2)}, u32[]{:S(2)}) collective-permute-start(bf16[2,256,256]{2,1,0:T(8,128)(2,1)S(1)} %pad_maximum_fusion.2.refs_0_), channel_id=1, source_target_pairs={{0,2},{1,3},{2,0},{3,1},{4,6},{5,7},{6,4},{7,5},{8,10},{9,11},{10,... | collective-permute-start | bytes 786440 | tf_op jit(solution)/shard_map/ppermute | solution.py:297
  55.1 8.3 %copy-start.18 = (bf16[3,32,1536]{2,1,0:T(8,128)(2,1)}, bf16[3,32,1536]{2,1,0:T(8,128)(2,1)S(1)}, u32[]{:S(2)}) copy-start(bf16[3,32,1536]{2,1,0:T(8,128)(2,1)S(1)} %collective-permute-done.2.refs_3_) | copy-start | bytes 884740
  55.1 8.1 %collective-permute-start.9 = (bf16[2,256,256]{2,1,0:T(8,128)(2,1)S(1)}, bf16[2,256,256]{2,1,0:T(8,128)(2,1)S(1)}, u32[]{:S(2)}, u32[]{:S(2)}) collective-permute-start(bf16[2,256,256]{2,1,0:T(8,128)(2,1)S(1)} %pad_maximum_fusion.2.refs_0_), channel_id=1, source_target_pairs={{0,1},{1,0},{2,3},{3,2},{4,5},{5,4},{6,7},{7,6},{8,9},{9,8},{10,11... | collective-permute-start | bytes 786440 | tf_op jit(solution)/shard_map/ppermute | solution.py:297
  56.4 7.2 %copy-start.8 = (bf16[2,256,256]{2,1,0:T(8,128)(2,1)}, bf16[2,256,256]{2,1,0:T(8,128)(2,1)S(1)}, u32[]{:S(2)}) copy-start(bf16[2,256,256]{2,1,0:T(8,128)(2,1)S(1)} %collective-permute-done.10.refs_3_) | copy-start | bytes 786436
  56.4 11.8 %collective-permute-start.3 = (bf16[3,32,1536]{2,1,0:T(8,128)(2,1)}, bf16[3,32,1536]{2,1,0:T(8,128)(2,1)}, u32[]{:S(2)}, u32[]{:S(2)}) collective-permute-start(bf16[3,32,1536]{2,1,0:T(8,128)(2,1)} %get-tuple-element.60), channel_id=1, source_target_pairs={{0,6},{2,12},{4,2},{6,8},{8,14},{10,4},{12,10},{14,0},{1,7},{3,13}... | collective-permute-start | bytes 884744 | tf_op jit(solution)/shard_map/ppermute | solution.py:273
  57.7 5.8 %copy-start.9 = (bf16[2,256,256]{2,1,0:T(8,128)(2,1)}, bf16[2,256,256]{2,1,0:T(8,128)(2,1)S(1)}, u32[]{:S(2)}) copy-start(bf16[2,256,256]{2,1,0:T(8,128)(2,1)S(1)} %collective-permute-done.8.refs_1_) | copy-start | bytes 786436
  57.7 30.3 %collective-permute-start.4 = (bf16[3,32,1536]{2,1,0:T(8,128)(2,1)}, bf16[3,32,1536]{2,1,0:T(8,128)(2,1)}, u32[]{:S(2)}, u32[]{:S(2)}) collective-permute-start(bf16[3,32,1536]{2,1,0:T(8,128)(2,1)} %get-tuple-element.59), channel_id=1, source_target_pairs={{0,8},{2,10},{4,12},{6,14},{8,0},{10,2},{12,4},{14,6},{1,9},{3,11}... | collective-permute-start | bytes 884744 | tf_op jit(solution)/shard_map/ppermute | solution.py:273
  63.2 26.0 %collective-permute-start.5 = (bf16[3,32,1536]{2,1,0:T(8,128)(2,1)}, bf16[3,32,1536]{2,1,0:T(8,128)(2,1)}, u32[]{:S(2)}, u32[]{:S(2)}) collective-permute-start(bf16[3,32,1536]{2,1,0:T(8,128)(2,1)} %get-tuple-element.65), channel_id=1, source_target_pairs={{0,10},{2,8},{4,14},{6,12},{8,2},{10,0},{12,6},{14,4},{1,11},{3,9}... | collective-permute-start | bytes 884744 | tf_op jit(solution)/shard_map/ppermute | solution.py:273
  63.4 25.8 %collective-permute-start.6 = (bf16[3,32,1536]{2,1,0:T(8,128)(2,1)}, bf16[3,32,1536]{2,1,0:T(8,128)(2,1)S(1)}, u32[]{:S(2)}, u32[]{:S(2)}) collective-permute-start(bf16[3,32,1536]{2,1,0:T(8,128)(2,1)} %get-tuple-element.58), channel_id=1, source_target_pairs={{0,2},{2,0},{4,6},{6,4},{8,10},{10,8},{12,14},{14,12},{1,3},{3,1},... | collective-permute-start | bytes 884744 | tf_op jit(solution)/shard_map/ppermute | solution.py:273
  68.2 41.9 %collective-permute-start.13 = (bf16[512,384]{1,0:T(8,128)(2,1)}, bf16[512,384]{1,0:T(8,128)(2,1)}, u32[]{:S(2)}, u32[]{:S(2)}) collective-permute-start(bf16[512,384]{1,0:T(8,128)(2,1)} %get-tuple-element.14), channel_id=1, source_target_pairs={{0,4},{2,6},{4,0},{6,2},{8,12},{10,14},{12,8},{14,10},{1,5},{3,7},... | collective-permute-start | bytes 1179656 | tf_op jit(solution)/shard_map/ppermute | solution.py:19
  96.7 81.3 %all-to-all-start = ((bf16[8,32,1536]{2,1,0:T(8,128)(2,1)}), bf16[8,32,1536]{2,1,0:T(8,128)(2,1)S(1)}, u32[]{:S(2)}, u32[]{:S(2)}) async-start(bf16[8,32,1536]{2,1,0:T(8,128)(2,1)} %temporal.1), calls=%async_computation | async-start | bytes 1572864 | tf_op jit(solution)/shard_map/all_to_all | solution.py:326
  104.6 5.5 %copy-start.13 = (f32[512,384]{1,0:T(8,128)S(1)}, f32[512,384]{1,0:T(8,128)}, u32[]{:S(2)}) copy-start(f32[512,384]{1,0:T(8,128)} %get-tuple-element.13) | copy-start | bytes 2359300
  109.8 21.6 %copy-start.14 = (f32[512,384]{1,0:T(8,128)S(1)}, f32[512,384]{1,0:T(8,128)}, u32[]{:S(2)}) copy-start(f32[512,384]{1,0:T(8,128)} %get-tuple-element.15) | copy-start | bytes 2359300
  109.8 21.6 %collective-permute-start.20 = (bf16[512,384]{1,0:T(8,128)(2,1)}, bf16[512,384]{1,0:T(8,128)(2,1)S(1)}, u32[]{:S(2)}, u32[]{:S(2)}) collective-permute-start(bf16[512,384]{1,0:T(8,128)(2,1)} %get-tuple-element.16), channel_id=1, source_target_pairs={{0,4},{2,6},{4,0},{6,2},{8,12},{10,14},{12,8},{14,10},{1,5},{3,7},... | collective-permute-start | bytes 1179656 | tf_op jit(solution)/shard_map/ppermute | solution.py:19
  112.1 20.5 %copy-start.11 = (bf16[1,1,256,1536]{3,2,1,0:T(8,128)(2,1)S(1)}, bf16[1,1,256,1536]{3,2,1,0:T(8,128)(2,1)}, u32[]{:S(2)}) copy-start(bf16[1,1,256,1536]{3,2,1,0:T(8,128)(2,1)} %param.8) | copy-start | bytes 2359300
  112.1 46.5 %collective-permute-start.14 = (bf16[512,384]{1,0:T(8,128)(2,1)S(1)}, bf16[512,384]{1,0:T(8,128)(2,1)S(1)}, u32[]{:S(2)}, u32[]{:S(2)}) collective-permute-start(bf16[512,384]{1,0:T(8,128)(2,1)S(1)} %get-tuple-element.56), channel_id=1, source_target_pairs={{0,8},{2,10},{4,12},{6,14},{8,0},{10,2},{12,4},{14,6},{1,9},{3,11}... | collective-permute-start | bytes 1179656 | tf_op jit(solution)/shard_map/ppermute | solution.py:19
  131.4 5.2 %copy-start.27 = (s32[2]{0:T(128)S(1)}, s32[2]{0:T(128)}, u32[]{:S(2)}) copy-start(s32[2]{0:T(128)} %param.12) | copy-start | bytes 28
  132.4 32.3 %collective-permute-start.21 = (bf16[512,384]{1,0:T(8,128)(2,1)S(1)}, bf16[512,384]{1,0:T(8,128)(2,1)S(1)}, u32[]{:S(2)}, u32[]{:S(2)}) collective-permute-start(bf16[512,384]{1,0:T(8,128)(2,1)S(1)} %get-tuple-element.54), channel_id=1, source_target_pairs={{0,8},{2,10},{4,12},{6,14},{8,0},{10,2},{12,4},{14,6},{1,9},{3,11}... | collective-permute-start | bytes 1179656 | tf_op jit(solution)/shard_map/ppermute | solution.py:19
  133.5 4.9 %collective-permute-start.15 = (bf16[256,384]{1,0:T(8,128)(2,1)}, bf16[256,384]{1,0:T(8,128)(2,1)S(1)}, u32[]{:S(2)}, u32[]{:S(2)}) collective-permute-start(bf16[256,384]{1,0:T(8,128)(2,1)} %get-tuple-element.73), channel_id=1, source_target_pairs={{0,2},{2,0},{4,6},{6,4},{8,10},{10,8},{12,14},{14,12},{1,3},{3,1},... | collective-permute-start | bytes 589832 | tf_op jit(solution)/shard_map/ppermute | solution.py:19
  134.5 12.5 %collective-permute-start.16 = (bf16[256,384]{1,0:T(8,128)(2,1)S(1)}, bf16[256,384]{1,0:T(8,128)(2,1)S(1)}, u32[]{:S(2)}, u32[]{:S(2)}) collective-permute-start(bf16[256,384]{1,0:T(8,128)(2,1)S(1)} %get-tuple-element.75), channel_id=1, source_target_pairs={{0,4},{2,6},{4,0},{6,2},{8,12},{10,14},{12,8},{14,10},{1,5},{3,7},... | collective-permute-start | bytes 589832 | tf_op jit(solution)/shard_map/ppermute | solution.py:19
  136.6 22.0 %collective-permute-start.17 = (bf16[256,384]{1,0:T(8,128)(2,1)S(1)}, bf16[256,384]{1,0:T(8,128)(2,1)S(1)}, u32[]{:S(2)}, u32[]{:S(2)}) collective-permute-start(bf16[256,384]{1,0:T(8,128)(2,1)S(1)} %get-tuple-element.72), channel_id=1, source_target_pairs={{0,6},{2,4},{4,2},{6,0},{8,14},{10,12},{12,10},{14,8},{1,7},{3,5},... | collective-permute-start | bytes 589832 | tf_op jit(solution)/shard_map/ppermute | solution.py:19
  138.4 20.2 %copy-start.20 = (bf16[256,384]{1,0:T(8,128)(2,1)}, bf16[256,384]{1,0:T(8,128)(2,1)S(1)}, u32[]{:S(2)}) copy-start(bf16[256,384]{1,0:T(8,128)(2,1)S(1)} %collective-permute-done.15.refs_1_) | copy-start | bytes 589828
  147.0 11.7 %copy-start.21 = (bf16[256,384]{1,0:T(8,128)(2,1)}, bf16[256,384]{1,0:T(8,128)(2,1)S(1)}, u32[]{:S(2)}) copy-start(bf16[256,384]{1,0:T(8,128)(2,1)S(1)} %collective-permute-done.16.refs_2_) | copy-start | bytes 589828
  169.7 8.3 %collective-permute-start.22 = (bf16[256,384]{1,0:T(8,128)(2,1)}, bf16[256,384]{1,0:T(8,128)(2,1)S(1)}, u32[]{:S(2)}, u32[]{:S(2)}) collective-permute-start(bf16[256,384]{1,0:T(8,128)(2,1)} %get-tuple-element.18), channel_id=1, source_target_pairs={{0,4},{2,6},{4,0},{6,2},{8,12},{10,14},{12,8},{14,10},{1,5},{3,7},... | collective-permute-start | bytes 589832 | tf_op jit(solution)/shard_map/ppermute | solution.py:19
  169.7 8.4 %collective-permute-start.23 = (bf16[256,384]{1,0:T(8,128)(2,1)}, bf16[256,384]{1,0:T(8,128)(2,1)S(1)}, u32[]{:S(2)}, u32[]{:S(2)}) collective-permute-start(bf16[256,384]{1,0:T(8,128)(2,1)} %get-tuple-element.19), channel_id=1, source_target_pairs={{0,2},{2,0},{4,6},{6,4},{8,10},{10,8},{12,14},{14,12},{1,3},{3,1},... | collective-permute-start | bytes 589832 | tf_op jit(solution)/shard_map/ppermute | solution.py:19
  170.2 10.6 %collective-permute-start.24 = (bf16[256,384]{1,0:T(8,128)(2,1)}, bf16[256,384]{1,0:T(8,128)(2,1)S(1)}, u32[]{:S(2)}, u32[]{:S(2)}) collective-permute-start(bf16[256,384]{1,0:T(8,128)(2,1)} %get-tuple-element.20), channel_id=1, source_target_pairs={{0,6},{2,4},{4,2},{6,0},{8,14},{10,12},{12,10},{14,8},{1,7},{3,5},... | collective-permute-start | bytes 589832 | tf_op jit(solution)/shard_map/ppermute | solution.py:19
  178.1 2.7 %copy-start.1 = (bf16[8,32,1536]{2,1,0:T(8,128)(2,1)}, bf16[8,32,1536]{2,1,0:T(8,128)(2,1)S(1)}, u32[]{:S(2)}) copy-start(bf16[8,32,1536]{2,1,0:T(8,128)(2,1)S(1)} %all-to-all-done) | copy-start | bytes 2359300
  178.1 2.7 %copy-start.23 = (bf16[256,384]{1,0:T(8,128)(2,1)}, bf16[256,384]{1,0:T(8,128)(2,1)S(1)}, u32[]{:S(2)}) copy-start(bf16[256,384]{1,0:T(8,128)(2,1)S(1)} %collective-permute-done.22.refs_1_) | copy-start | bytes 589828
  178.1 2.7 %copy-start.24 = (bf16[256,384]{1,0:T(8,128)(2,1)}, bf16[256,384]{1,0:T(8,128)(2,1)S(1)}, u32[]{:S(2)}) copy-start(bf16[256,384]{1,0:T(8,128)(2,1)S(1)} %collective-permute-done.23.refs_2_) | copy-start | bytes 589828
  (7 other events, 5.3 us)

commit v2 on v1

--- a/solution.py
+++ b/solution.py
@@ -39,71 +39,66 @@
 
 
 def prompt_kernel(scalar_ref, in_ref, out_ref):
-    out_ref[0] = in_ref[...]
+    blocks, _, _, feats = out_ref.shape
+    for j in range(blocks):
+        out_ref[j] = in_ref[:, :, j * feats : (j + 1) * feats]
 
 
 def prompt_blocks(states, side, sides, blocks):
-    prompts, rows, feats = states.shape
-    rows, feats = rows // sides, feats // blocks
+    prompts, rows, width = states.shape
+    rows, feats = rows // sides, width // blocks
     if feats % HDIM:
         cut = lax.dynamic_slice_in_dim(states, side * rows, rows, 1)
         return cut.reshape(prompts, rows, blocks, feats).transpose(2, 0, 1, 3)
+    shape = (blocks, prompts, rows, feats)
     return pl.pallas_call(
         prompt_kernel,
         grid_spec=pltpu.PrefetchScalarGridSpec(
             num_scalar_prefetch=1,
-            grid=(blocks,),
-            in_specs=[pl.BlockSpec((prompts, rows, feats), lambda j, s: (0, s[0], j))],
-            out_specs=pl.BlockSpec((1, prompts, rows, feats), lambda j, s: (j, 0, 0, 0)),
+            grid=(1,),
+            in_specs=[pl.BlockSpec((prompts, rows, width), lambda j, s: (0, s[0], 0))],
+            out_specs=pl.BlockSpec(shape, lambda j, s: (0, 0, 0, 0)),
         ),
-        out_shape=jax.ShapeDtypeStruct((blocks, prompts, rows, feats), BF16),
+        out_shape=jax.ShapeDtypeStruct(shape, BF16),
         name="prompt_blocks",
     )(side.reshape(1), states)
 
 
-def project_kernel(n_rows, n_grp, scalar_ref, *refs):
+def project_kernel(n_rows, scalar_ref, *refs):
+    near = scalar_ref[0]
     state_refs = refs[: 2 * n_rows]
-    weight_refs = refs[2 * n_rows : 2 * n_rows + n_grp]
-    kept_ref, sent_ref = refs[2 * n_rows + n_grp :]
-    rows = state_refs[0].shape[1]
-    first = pl.program_id(0) == 0
+    kept_ref, sent_ref = refs[-2:]
+    weight_refs = refs[2 * n_rows : -2]
+    rows, cols = state_refs[0].shape[1], kept_ref.shape[1]
+
+    def product(i, start):
+        total = None
+        for j, weight_ref in enumerate(weight_refs):
+            state = state_refs[2 * i + j % 2][j // 2]
+            weight = weight_ref[:, pl.ds(pl.multiple_of(start, HDIM), cols)]
+            part = jnp.dot(state, weight, preferred_element_type=F32)
+            total = part if total is None else total + part
+        return total
+
     for i in range(n_rows):
-        total = None
-        for core in range(2):
-            for g in range(n_grp):
-                part = jnp.dot(
-                    state_refs[2 * i + core][g], weight_refs[g][core], preferred_element_type=F32
-                )
-                total = part if total is None else total + part
-
-        @pl.when(first)
-        def _(total=total, i=i):
-            kept_ref[i * rows : (i + 1) * rows, :] = total
-
-        @pl.when(jnp.logical_not(first))
-        def _(total=total, i=i):
-            sent_ref[i * rows : (i + 1) * rows, :] = total.astype(BF16)
+        sent_ref[i * rows : (i + 1) * rows, :] = product(i, (1 - near) * cols).astype(BF16)
+    for i in range(n_rows):
+        kept_ref[i * rows : (i + 1) * rows, :] = product(i, near * cols)
+
+
+VMEM_SPEC = pl.BlockSpec(memory_space=pltpu.VMEM)
+SMEM_SPEC = pl.BlockSpec(memory_space=pltpu.SMEM)
 
 
 def project(states, weights, near):
-    n_grp, rows, feats = states[0].shape
+    _, rows, _ = states[0].shape
     n_rows = len(states) // 2
-    cols = weights[0].shape[2] // 2
-    whole = pl.BlockSpec((n_grp, rows, feats), lambda j, s: (0, 0, 0))
-    side = pl.BlockSpec((2, feats, cols), lambda j, s: (0, 0, j ^ s[0]))
-    out = pl.BlockSpec((n_rows * rows, cols), lambda j, s: (0, 0))
-    return pl.pallas_call(
-        functools.partial(project_kernel, n_rows, n_grp),
-        grid_spec=pltpu.PrefetchScalarGridSpec(
-            num_scalar_prefetch=1,
-            grid=(2,),
-            in_specs=[whole] * len(states) + [side] * n_grp,
-            out_specs=[out, out],
-        ),
-        out_shape=[
-            jax.ShapeDtypeStruct((n_rows * rows, cols), F32),
-            jax.ShapeDtypeStruct((n_rows * rows, cols), BF16),
-        ],
+    shape = (n_rows * rows, weights[0].shape[1] // 2)
+    return pl.pallas_call(
+        functools.partial(project_kernel, n_rows),
+        in_specs=[SMEM_SPEC] + [VMEM_SPEC] * (len(states) + len(weights)),
+        out_specs=[VMEM_SPEC] * 2,
+        out_shape=[jax.ShapeDtypeStruct(shape, F32), jax.ShapeDtypeStruct(shape, BF16)],
         name="project",
     )(near.reshape(1), *states, *weights)
 
@@ -169,44 +164,41 @@
 
 def weigh_kernel(bias_ref, kept_ref, come_ref, *refs):
     query_refs, out_ref = refs[:-1], refs[-1]
-    key_rows = (kept_ref[...] + come_ref[...].astype(F32)).astype(BF16)
-    for j, query_ref in enumerate(query_refs):
-        scores = scores_of(query_ref[...], key_rows) + bias_ref[...]
-        out_ref[0, j] = softmax(scores)
+    for head in range(out_ref.shape[0]):
+        at = lanes(head)
+        key_rows = (kept_ref[:, at] + come_ref[:, at].astype(F32)).astype(BF16)
+        for j, query_ref in enumerate(query_refs):
+            out_ref[head, j] = softmax(scores_of(query_ref[:, at], key_rows) + bias_ref[...])
 
 
 def cross_weights(bias, kept, come, queries):
     rows, width = kept.shape
     tokens = queries[0].shape[0]
-    heads = width // HDIM
-    key_spec = pl.BlockSpec((rows, HDIM), lambda h: (0, h))
     return pl.pallas_call(
         weigh_kernel,
-        grid=(heads,),
-        in_specs=[pl.BlockSpec((1, rows), lambda h: (0, 0)), key_spec, key_spec]
-        + [pl.BlockSpec((tokens, HDIM), lambda h: (0, h))] * len(queries),
-        out_specs=pl.BlockSpec((1, len(queries), tokens, rows), lambda h: (h, 0, 0, 0)),
-        out_shape=jax.ShapeDtypeStruct((heads, len(queries), tokens, rows), BF16),
+        in_specs=[VMEM_SPEC] * (3 + len(queries)),
+        out_specs=VMEM_SPEC,
+        out_shape=jax.ShapeDtypeStruct((width // HDIM, len(queries), tokens, rows), BF16),
         name="cross_weights",
     )(bias, kept, come, *queries)
 
 
 def value_kernel(weight_ref, kept_ref, come_ref, *out_refs):
-    values = (kept_ref[...] + come_ref[...].astype(F32)).astype(BF16)
-    for j, out_ref in enumerate(out_refs):
-        result = jnp.dot(weight_ref[0, j], values, preferred_element_type=F32)
-        out_ref[...] = result.astype(out_ref.dtype)
+    for head in range(weight_ref.shape[0]):
+        at = lanes(head)
+        values = (kept_ref[:, at] + come_ref[:, at].astype(F32)).astype(BF16)
+        for j, out_ref in enumerate(out_refs):
+            result = jnp.dot(weight_ref[head, j], values, preferred_element_type=F32)
+            out_ref[:, at] = result.astype(out_ref.dtype)
 
 
 def cross_values(weights, kept, come):
-    rows, width = kept.shape
-    heads, count, tokens, _ = weights.shape
-    key_spec = pl.BlockSpec((rows, HDIM), lambda h: (0, h))
+    _, width = kept.shape
+    _, count, tokens, _ = weights.shape
     return pl.pallas_call(
         value_kernel,
-        grid=(heads,),
-        in_specs=[pl.BlockSpec((1, count, tokens, rows), lambda h: (h, 0, 0, 0)), key_spec, key_spec],
-        out_specs=[pl.BlockSpec((tokens, HDIM), lambda h: (0, h))] * count,
+        in_specs=[VMEM_SPEC] * 3,
+        out_specs=[VMEM_SPEC] * count,
         out_shape=[jax.ShapeDtypeStruct((tokens, width), F32 if j == 0 else BF16) for j in range(count)],
         name="cross_values",
     )(weights, kept, come)
@@ -214,28 +206,19 @@
 
 def final_kernel(scalar_ref, base_ref, temporal_ref, *refs):
     piece_refs, out_ref = refs[:-1], refs[-1]
-    partial = base_ref[...] + temporal_ref[...].astype(F32)
+    cols = piece_refs[0].shape[1]
     for j, piece_ref in enumerate(piece_refs):
-
-        @pl.when(pl.program_id(0) == j)
-        def _(piece_ref=piece_ref):
-            out_ref[...] = (partial + piece_ref[...].astype(F32)).astype(BF16)
+        at = pl.ds(pl.multiple_of((scalar_ref[0] ^ j) * cols, HDIM), cols)
+        total = base_ref[:, at] + temporal_ref[:, at].astype(F32)
+        out_ref[:, at] = (total + piece_ref[...].astype(F32)).astype(BF16)
 
 
 def final_sum(place, base, temporal, pieces):
-    tokens, width = base.shape
-    cols = width // len(pieces)
-    side = pl.BlockSpec((tokens, cols), lambda j, s: (0, j ^ s[0]))
-    whole = pl.BlockSpec((tokens, cols), lambda j, s: (0, 0))
     return pl.pallas_call(
         final_kernel,
-        grid_spec=pltpu.PrefetchScalarGridSpec(
-            num_scalar_prefetch=1,
-            grid=(len(pieces),),
-            in_specs=[side, side] + [whole] * len(pieces),
-            out_specs=side,
-        ),
-        out_shape=jax.ShapeDtypeStruct((tokens, width), BF16),
+        in_specs=[SMEM_SPEC] + [VMEM_SPEC] * (2 + len(pieces)),
+        out_specs=VMEM_SPEC,
+        out_shape=jax.ShapeDtypeStruct(base.shape, BF16),
         name="final",
     )(place.reshape(1), base, temporal, *pieces)
 
@@ -263,26 +246,34 @@
     qkv = latent_qkv[0, 0].transpose(1, 0, 2)
     share = tokens // seq
     steps = temporal_plan(seq)
-    own_block = lax.dynamic_slice_in_dim(qkv, me * share, share, 1)
-    pieces, sources = [own_block], [me]
-    for even, odd in steps:
+    pieces, sources = [lax.dynamic_slice_in_dim(qkv, me * share, share, 1)], [me]
+    held = qkv
+    for number, (even, odd) in enumerate(steps):
         crossing = even & 1
         target = me ^ jnp.where(core == 0, even, odd)
-        block = lax.dynamic_slice_in_dim(qkv, target * share, share, 1)
-        pairs = [(i, i ^ (odd if i & 1 else even)) for i in range(seq)]
-        pieces.append(lax.ppermute(block, "seq", pairs))
+        if number == 2:
+            held, blocks = lax.optimization_barrier((qkv, blocks))
+        block = lax.dynamic_slice_in_dim(held, target * share, share, 1)
+        blocks = [block] if number == 0 else blocks + [block]
         sender_core = core ^ crossing
         sources.append(me ^ jnp.where(sender_core == 0, even, odd))
+    for number, (even, odd) in enumerate(steps):
+        pairs = [(i, i ^ (odd if i & 1 else even)) for i in range(seq)]
+        pieces.append(lax.ppermute(blocks[number], "seq", pairs))
 
     half = width // 2
+    planes = lax.optimization_barrier(kv_weight.transpose(1, 0, 2))
+    mine = lax.dynamic_slice_in_dim(planes, core * half, half, 2)
+    theirs = lax.dynamic_slice_in_dim(planes, (1 - core) * half, half, 2)
+    come = swap(theirs, "seq", 1)
+    across = [(g, s) for g in range(grp) for s in range(seq)]
     weights = []
     for kind in range(2):
-        plane = kv_weight[:, kind]
-        mine = lax.dynamic_slice_in_dim(plane, core * half, half, 1)
-        theirs = lax.dynamic_slice_in_dim(plane, (1 - core) * half, half, 1)
-        come = swap(theirs, "seq", 1)
-        both = jnp.stack([mine, come])
-        weights.append([both] + [swap(both, "grp", k) for k in range(1, grp)])
+        weights.append([mine[kind], come[kind]])
+        for k in range(1, grp):
+            for c, part in enumerate((mine[kind], theirs[kind])):
+                pairs = [(g * seq + s, (g ^ k) * seq + (s ^ c)) for g, s in across]
+                weights[kind].append(lax.ppermute(part, ("grp", "seq"), pairs))
 
     def slot(k):
         index = jnp.take(assignment, group ^ k)

time: 187 us -> 171 us (0.914)
  the two profiles are of different devices: /device:TPU:25 before, /device:TPU:0 now
where the time goes in v2:
time: 171 us; the launch traced here: 170 us
  waiting for transfers between devices  70.4 us (41%)
  starting transfers between devices  46.5 us (27%)
  Pallas kernels  34.8 us (20%)
  local copies, waits for them, and re-layouts  13.5 us (8%)
  other arithmetic  2.62 us (2%)
  between operations  2.07 us (1%)
    ppermute x12, waiting for transfers between devices, swap(): return lax.ppermute(value, axis, pairs)  37.4 us
    ppermute x7, waiting for transfers between devices, block(): pieces.append(lax.ppermute(blocks[number], 'seq', pairs))  31.4 us
    ppermute x12, starting transfers between devices, swap(): return lax.ppermute(value, axis, pairs)  17 us
    ppermute x7, starting transfers between devices, block(): pieces.append(lax.ppermute(blocks[number], 'seq', pairs))  10.8 us
    pallas_call x2, Pallas kernels, project(): pl.pallas_call(functools.partial(project_kernel, n_rows), in_specs=[SMEM_...  7.68 us
    pallas_call x1, Pallas kernels, temporal_attention(): pl.pallas_call(functools.partial(temporal_kernel, frames), grid_spec=pltp...  6.83 us
    all_to_all x1, starting transfers between devices, block(): parts = lax.all_to_all(parts, 'seq', 0, 0, tiled=True)  6.35 us
    pallas_call x1, Pallas kernels, spatial_attention(): pl.pallas_call(spatial_kernel, grid=(width // cols,), in_specs=[pl.BlockS...  6.31 us
  transfers between devices with their start and end apart: 28, of which 11 were waited for; matrix products, arithmetic and copies ran while one was open for 8% of the time, Pallas kernels for 18%

profile of v2, /device:TPU:0, one launch (start us, length us, event | category | flops | bytes accessed | tf_op | source)
XLA Modules:
  0.0 169.9 jit_solution(6708879938022747992)
XLA Ops:
  0.0 1.8 %prompt_blocks.1 = bf16[8,2,32,256]{3,2,1,0:T(8,128)(2,1)} custom-call(s32[1]{0:T(128)} %bitcast.25.scalar_ref, bf16[2,64,2048]{2,1,0:T(8,128)(2,1)} %in_ref.1), custom_call_target="tpu_custom_call" | custom-call | tf_op jit(solution)/shard_map/prompt_blocks/pallas_call | solution.py:54
  1.8 6.4 %all-to-all-start.1 = ((bf16[8,2,32,256]{3,2,1,0:T(8,128)(2,1)}), bf16[8,2,32,256]{3,2,1,0:T(8,128)(2,1)S(1)}, u32[]{:S(2)}, u32[]{:S(2)}) async-start(bf16[8,2,32,256]{3,2,1,0:T(8,128)(2,1)} %prompt_blocks.1), calls=%async_computation.1 | async-start | bytes 524288 | tf_op jit(solution)/shard_map/all_to_all | solution.py:244
  8.2 2.1 %dynamic-slice_bitcast_fusion.4 = (bf16[3,32,1536]{2,1,0:T(8,128)(2,1)}, bf16[3,32,1536]{2,1,0:T(8,128)(2,1)}, bf16[3,32,1536]{2,1,0:T(8,128)(2,1)}) fusion(bf16[1,1,256,3,1536]{4,2,3,1,0:T(8,128)(2,1)} %param.7, s32[]{:T(128)S(6)} %select_n.162, s32[]{:T(128)S(6)} %select_n.160, s32[]{:T(128)S(6)} %select_n.161), kind=kLoop, calls=%fused_computation.9 | loop fusion | bytes 1769484 | tf_op jit(solution)/shard_map/dynamic_slice | solution.py:256
  10.3 1.1 constant_dynamic-slice_fusion.3
  11.5 3.5 %collective-permute-start.2 = (bf16[3,32,1536]{2,1,0:T(8,128)(2,1)}, bf16[3,32,1536]{2,1,0:T(8,128)(2,1)}, u32[]{:S(2)}, u32[]{:S(2)}) collective-permute-start(bf16[3,32,1536]{2,1,0:T(8,128)(2,1)} %get-tuple-element.68), channel_id=1, source_target_pairs={{0,14},{2,4},{4,10},{6,0},{8,6},{10,12},{12,2},{14,8},{1,15},{3,5}... | collective-permute-start | bytes 884744 | tf_op jit(solution)/shard_map/ppermute | solution.py:262
  15.0 1.6 copy.10
  16.6 0.9 constant_dynamic-slice_fusion
  18.0 1.0 dynamic-slice_bitcast_fusion
  19.0 1.5 collective-permute-start.12
  20.5 0.6 fusion.6
  23.0 4.3 %collective-permute-done.2.refs_3_ = bf16[3,32,1536]{2,1,0:T(8,128)(2,1)} collective-permute-done((bf16[3,32,1536]{2,1,0:T(8,128)(2,1)}, bf16[3,32,1536]{2,1,0:T(8,128)(2,1)}, u32[]{:S(2)}, u32[]{:S(2)}) %collective-permute-start.2) | collective-permute-done | bytes 294944 | tf_op jit(solution)/shard_map/ppermute | solution.py:262
  27.4 2.8 %collective-permute-start.4 = (bf16[3,32,1536]{2,1,0:T(8,128)(2,1)}, bf16[3,32,1536]{2,1,0:T(8,128)(2,1)}, u32[]{:S(2)}, u32[]{:S(2)}) collective-permute-start(bf16[3,32,1536]{2,1,0:T(8,128)(2,1)} %get-tuple-element.66), channel_id=1, source_target_pairs={{0,8},{2,10},{4,12},{6,14},{8,0},{10,2},{12,4},{14,6},{1,9},{3,11}... | collective-permute-start | bytes 884744 | tf_op jit(solution)/shard_map/ppermute | solution.py:262
  30.7 2.1 %collective-permute-done.7 = bf16[256,256]{1,0:T(8,128)(2,1)S(1)} collective-permute-done((bf16[256,256]{1,0:T(8,128)(2,1)S(1)}, bf16[256,256]{1,0:T(8,128)(2,1)S(1)}, u32[]{:S(2)}, u32[]{:S(2)}) %collective-permute-start.7) | collective-permute-done | bytes 131104 | tf_op jit(solution)/shard_map/ppermute | solution.py:19
  33.1 17.9 %collective-permute-done.4.refs_5_ = bf16[3,32,1536]{2,1,0:T(8,128)(2,1)} collective-permute-done((bf16[3,32,1536]{2,1,0:T(8,128)(2,1)}, bf16[3,32,1536]{2,1,0:T(8,128)(2,1)}, u32[]{:S(2)}, u32[]{:S(2)}) %collective-permute-start.4) | collective-permute-done | bytes 294944 | tf_op jit(solution)/shard_map/ppermute | solution.py:262
  51.0 1.2 collective-permute-start.10
  52.2 5.2 %collective-permute-done.5.refs_6_ = bf16[3,32,1536]{2,1,0:T(8,128)(2,1)} collective-permute-done((bf16[3,32,1536]{2,1,0:T(8,128)(2,1)}, bf16[3,32,1536]{2,1,0:T(8,128)(2,1)}, u32[]{:S(2)}, u32[]{:S(2)}) %collective-permute-start.5) | collective-permute-done | bytes 294944 | tf_op jit(solution)/shard_map/ppermute | solution.py:262
  57.4 1.6 collective-permute-start.9
  59.2 1.5 collective-permute-start.19
  60.9 3.7 %collective-permute-start = (bf16[3,32,1536]{2,1,0:T(8,128)(2,1)}, bf16[3,32,1536]{2,1,0:T(8,128)(2,1)}, u32[]{:S(2)}, u32[]{:S(2)}) collective-permute-start(bf16[3,32,1536]{2,1,0:T(8,128)(2,1)} %get-tuple-element.16), channel_id=1, source_target_pairs={{0,12},{2,6},{4,8},{6,2},{8,4},{10,14},{12,0},{14,10},{1,13},{3,7}... | collective-permute-start | bytes 884744 | tf_op jit(solution)/shard_map/ppermute | solution.py:262
  64.6 1.5 collective-permute-done.9.refs_2_
  66.3 1.0 slice_bitcast_fusion
  67.3 3.9 %project.2 = (f32[512,384]{1,0:T(8,128)}, bf16[512,384]{1,0:T(8,128)(2,1)}) custom-call(s32[1]{0:T(128)} %bitcast.24.scalar_ref, bf16[2,256,256]{2,1,0:T(8,128)(2,1)} %copy-done.2, bf16[2,256,256]{2,1,0:T(8,128)(2,1)} %copy-done.6, bf16[2,256,256]{2,1,0:T(8,128)(2,1)} %copy-done.7, bf16[2,256,256]{2,1,0:T(8,128)(2,1)} %copy-done.5, ...), custom_call_target="tpu_custom_call" | custom-call | tf_op jit(solution)/shard_map/project/pallas_call | solution.py:97
  71.1 1.9 %collective-permute-start.14 = (bf16[512,384]{1,0:T(8,128)(2,1)}, bf16[512,384]{1,0:T(8,128)(2,1)S(1)}, u32[]{:S(2)}, u32[]{:S(2)}) collective-permute-start(bf16[512,384]{1,0:T(8,128)(2,1)} %get-tuple-element.20), channel_id=1, source_target_pairs={{0,4},{2,6},{4,0},{6,2},{8,12},{10,14},{12,8},{14,10},{1,5},{3,7},... | collective-permute-start | bytes 1179656 | tf_op jit(solution)/shard_map/ppermute | solution.py:19
  73.7 4.0 %collective-permute-done.1.refs_2_ = bf16[3,32,1536]{2,1,0:T(8,128)(2,1)} collective-permute-done((bf16[3,32,1536]{2,1,0:T(8,128)(2,1)}, bf16[3,32,1536]{2,1,0:T(8,128)(2,1)}, u32[]{:S(2)}, u32[]{:S(2)}) %collective-permute-start.1) | collective-permute-done | bytes 294944 | tf_op jit(solution)/shard_map/ppermute | solution.py:262
  77.7 6.8 %temporal.1 = bf16[8,32,1536]{2,1,0:T(8,128)(2,1)} custom-call(s32[8]{0:T(128)} %stack.41.scalar_ref, bf16[3,32,1536]{2,1,0:T(8,128)(2,1)} %get-tuple-element.70.refs_0_, bf16[3,32,1536]{2,1,0:T(8,128)(2,1)} %collective-permute-done.refs_1_, bf16[3,32,1536]{2,1,0:T(8,128)(2,1)} %collective-permute-done.1.refs_2_, ...), custom_call_target="tpu_custom_call" | custom-call | tf_op jit(solution)/shard_map/temporal/pallas_call | solution.py:152
  84.5 6.0 %all-to-all-start = ((bf16[8,32,1536]{2,1,0:T(8,128)(2,1)}), bf16[8,32,1536]{2,1,0:T(8,128)(2,1)S(1)}, u32[]{:S(2)}, u32[]{:S(2)}) async-start(bf16[8,32,1536]{2,1,0:T(8,128)(2,1)} %temporal.1), calls=%async_computation | async-start | bytes 1572864 | tf_op jit(solution)/shard_map/all_to_all | solution.py:317
  90.6 0.7 copy-done.14
  91.3 3.8 %project.3 = (f32[512,384]{1,0:T(8,128)}, bf16[512,384]{1,0:T(8,128)(2,1)}) custom-call(s32[1]{0:T(128)} %bitcast.24.scalar_ref, bf16[2,256,256]{2,1,0:T(8,128)(2,1)} %copy-done.2, bf16[2,256,256]{2,1,0:T(8,128)(2,1)} %copy-done.6, bf16[2,256,256]{2,1,0:T(8,128)(2,1)} %copy-done.7, bf16[2,256,256]{2,1,0:T(8,128)(2,1)} %copy-done.5, ...), custom_call_target="tpu_custom_call" | custom-call | tf_op jit(solution)/shard_map/project/pallas_call | solution.py:97
  95.2 2.0 %collective-permute-start.21 = (bf16[512,384]{1,0:T(8,128)(2,1)}, bf16[512,384]{1,0:T(8,128)(2,1)S(1)}, u32[]{:S(2)}, u32[]{:S(2)}) collective-permute-start(bf16[512,384]{1,0:T(8,128)(2,1)} %get-tuple-element.22), channel_id=1, source_target_pairs={{0,4},{2,6},{4,0},{6,2},{8,12},{10,14},{12,8},{14,10},{1,5},{3,7},... | collective-permute-start | bytes 1179656 | tf_op jit(solution)/shard_map/ppermute | solution.py:19
  97.2 1.0 fusion.5
  98.2 2.4 %collective-permute-start.15 = (bf16[512,384]{1,0:T(8,128)(2,1)S(1)}, bf16[512,384]{1,0:T(8,128)(2,1)S(1)}, u32[]{:S(2)}, u32[]{:S(2)}) collective-permute-start(bf16[512,384]{1,0:T(8,128)(2,1)S(1)} %get-tuple-element.62), channel_id=1, source_target_pairs={{0,8},{2,10},{4,12},{6,14},{8,0},{10,2},{12,4},{14,6},{1,9},{3,11}... | collective-permute-start | bytes 1179656 | tf_op jit(solution)/shard_map/ppermute | solution.py:19
  100.5 19.5 %collective-permute-done.21 = bf16[512,384]{1,0:T(8,128)(2,1)S(1)} collective-permute-done((bf16[512,384]{1,0:T(8,128)(2,1)}, bf16[512,384]{1,0:T(8,128)(2,1)S(1)}, u32[]{:S(2)}, u32[]{:S(2)}) %collective-permute-start.21) | collective-permute-done | bytes 393248 | tf_op jit(solution)/shard_map/ppermute | solution.py:19
  120.1 1.0 fusion.4
  121.1 0.9 dynamic-slice_bitcast_fusion.7
  122.0 2.0 %collective-permute-start.17 = (bf16[256,384]{1,0:T(8,128)(2,1)}, bf16[256,384]{1,0:T(8,128)(2,1)S(1)}, u32[]{:S(2)}, u32[]{:S(2)}) collective-permute-start(bf16[256,384]{1,0:T(8,128)(2,1)} %get-tuple-element.81), channel_id=1, source_target_pairs={{0,4},{2,6},{4,0},{6,2},{8,12},{10,14},{12,8},{14,10},{1,5},{3,7},... | collective-permute-start | bytes 589832 | tf_op jit(solution)/shard_map/ppermute | solution.py:19
  125.9 9.0 %collective-permute-done.17.refs_2_ = bf16[256,384]{1,0:T(8,128)(2,1)S(1)} collective-permute-done((bf16[256,384]{1,0:T(8,128)(2,1)}, bf16[256,384]{1,0:T(8,128)(2,1)S(1)}, u32[]{:S(2)}, u32[]{:S(2)}) %collective-permute-start.17) | collective-permute-done | bytes 196640 | tf_op jit(solution)/shard_map/ppermute | solution.py:19
  134.9 3.3 %collective-permute-done.18.refs_3_ = bf16[256,384]{1,0:T(8,128)(2,1)S(1)} collective-permute-done((bf16[256,384]{1,0:T(8,128)(2,1)}, bf16[256,384]{1,0:T(8,128)(2,1)S(1)}, u32[]{:S(2)}, u32[]{:S(2)}) %collective-permute-start.18) | collective-permute-done | bytes 196640 | tf_op jit(solution)/shard_map/ppermute | solution.py:19
  138.2 0.7 copy-done.17
  139.0 5.2 %cross_weights.1.weight_ref = bf16[3,4,256,512]{3,2,1,0:T(8,128)(2,1)} custom-call(f32[1,512]{1,0:T(1,128)} %compare_select_fusion.bias_ref, f32[512,384]{1,0:T(8,128)} %get-tuple-element.63.kept_ref, bf16[512,384]{1,0:T(8,128)(2,1)} %copy-done.12, bf16[256,384]{1,0:T(8,128)(2,1)} %get-tuple-element.80.refs_0_, bf16[256,384]{1,0:T(8,128)(2,1)} %copy-done.15, ...), custom_call_target="tpu_custom_call" | custom-call | tf_op jit(solution)/shard_map/cross_weights/pallas_call | solution.py:177
  144.3 1.1 collective-permute-done.22.come_ref
  145.4 0.8 copy-done.11
  146.1 3.9 %cross_values.1 = (f32[256,384]{1,0:T(8,128)}, bf16[256,384]{1,0:T(8,128)(2,1)}, bf16[256,384]{1,0:T(8,128)(2,1)}, bf16[256,384]{1,0:T(8,128)(2,1)}) custom-call(bf16[3,4,256,512]{3,2,1,0:T(8,128)(2,1)} %cross_weights.1.weight_ref, f32[512,384]{1,0:T(8,128)} %get-tuple-element.61.kept_ref, bf16[512,384]{1,0:T(8,128)(2,1)} %copy-done.11), custom_call_target="tpu_custom_call" | custom-call | tf_op jit(solution)/shard_map/cross_values/pallas_call | solution.py:198
  150.1 6.0 %collective-permute-start.23 = (bf16[256,384]{1,0:T(8,128)(2,1)}, bf16[256,384]{1,0:T(8,128)(2,1)S(1)}, u32[]{:S(2)}, u32[]{:S(2)}) collective-permute-start(bf16[256,384]{1,0:T(8,128)(2,1)} %get-tuple-element.24), channel_id=1, source_target_pairs={{0,4},{2,6},{4,0},{6,2},{8,12},{10,14},{12,8},{14,10},{1,5},{3,7},... | collective-permute-start | bytes 589832 | tf_op jit(solution)/shard_map/ppermute | solution.py:19
  156.2 1.4 collective-permute-start.25
  157.5 6.3 %spatial.1.base_ref = f32[256,1536]{1,0:T(8,128)} custom-call(bf16[3,256,1536]{2,1,0:T(8,128)(2,1)} %bitcast.63, bf16[256,1536]{1,0:T(8,128)(2,1)} %bitcast.66), custom_call_target="tpu_custom_call" | custom-call | tf_op jit(solution)/shard_map/spatial/pallas_call | solution.py:117
  163.9 2.3 %collective-permute-done.25.refs_3_ = bf16[256,384]{1,0:T(8,128)(2,1)S(1)} collective-permute-done((bf16[256,384]{1,0:T(8,128)(2,1)}, bf16[256,384]{1,0:T(8,128)(2,1)S(1)}, u32[]{:S(2)}, u32[]{:S(2)}) %collective-permute-start.25) | collective-permute-done | bytes 196640 | tf_op jit(solution)/shard_map/ppermute | solution.py:19
  166.2 0.7 copy-done.20
  166.9 3.0 %final.1 = bf16[256,1536]{1,0:T(8,128)(2,1)} custom-call(s32[1]{0:T(128)} %bitcast.scalar_ref, f32[256,1536]{1,0:T(8,128)} %spatial.1.base_ref, bf16[256,1536]{1,0:T(8,128)(2,1)} %bitcast.65, f32[256,384]{1,0:T(8,128)} %get-tuple-element.23.refs_0_, bf16[256,384]{1,0:T(8,128)(2,1)} %copy-done.18, bf16[256,384]{1,0:T(8,128)(2,1)} %copy-done.19, ...), custom_call_target="tpu_custom_call" | custom-call | tf_op jit(solution)/shard_map/final/pallas_call | solution.py:217
  (77 shorter events, 4.8 us)
Async XLA Ops:
  0.0 10.3 %copy-start = (bf16[1,1,256,3,1536]{4,2,3,1,0:T(8,128)(2,1)S(1)}, bf16[1,1,256,3,1536]{4,2,3,1,0:T(8,128)(2,1)}, u32[]{:S(2)}) copy-start(bf16[1,1,256,3,1536]{4,2,3,1,0:T(8,128)(2,1)} %param.7) | copy-start | bytes 7077892
  1.8 20.6 %all-to-all-start.1 = ((bf16[8,2,32,256]{3,2,1,0:T(8,128)(2,1)}), bf16[8,2,32,256]{3,2,1,0:T(8,128)(2,1)S(1)}, u32[]{:S(2)}, u32[]{:S(2)}) async-start(bf16[8,2,32,256]{3,2,1,0:T(8,128)(2,1)} %prompt_blocks.1), calls=%async_computation.1 | async-start | bytes 524288 | tf_op jit(solution)/shard_map/all_to_all | solution.py:244
  11.5 15.9 %collective-permute-start.2 = (bf16[3,32,1536]{2,1,0:T(8,128)(2,1)}, bf16[3,32,1536]{2,1,0:T(8,128)(2,1)}, u32[]{:S(2)}, u32[]{:S(2)}) collective-permute-start(bf16[3,32,1536]{2,1,0:T(8,128)(2,1)} %get-tuple-element.68), channel_id=1, source_target_pairs={{0,14},{2,4},{4,10},{6,0},{8,6},{10,12},{12,2},{14,8},{1,15},{3,5}... | collective-permute-start | bytes 884744 | tf_op jit(solution)/shard_map/ppermute | solution.py:262
  15.0 15.2 %collective-permute-start.3 = (bf16[3,32,1536]{2,1,0:T(8,128)(2,1)}, bf16[3,32,1536]{2,1,0:T(8,128)(2,1)}, u32[]{:S(2)}, u32[]{:S(2)}) collective-permute-start(bf16[3,32,1536]{2,1,0:T(8,128)(2,1)} %get-tuple-element.67), channel_id=1, source_target_pairs={{0,6},{2,12},{4,2},{6,8},{8,14},{10,4},{12,10},{14,0},{1,7},{3,13}... | collective-permute-start | bytes 884744 | tf_op jit(solution)/shard_map/ppermute | solution.py:262
  17.5 41.7 %collective-permute-start.11 = (bf16[2,256,768]{2,1,0:T(8,128)(2,1)}, bf16[2,256,768]{2,1,0:T(8,128)(2,1)S(1)}, u32[]{:S(2)}, u32[]{:S(2)}) collective-permute-start(bf16[2,256,768]{2,1,0:T(8,128)(2,1)} %constant_dynamic-slice_fusion), channel_id=1, source_target_pairs={{0,2},{2,0},{4,6},{6,4},{8,10},{10,8},{12,14},{14,12},{1,3},{3,1},... | collective-permute-start | bytes 2359304 | tf_op jit(solution)/shard_map/ppermute | solution.py:19
  18.0 2.5 %copy-start.21 = (s32[2]{0:T(128)S(1)}, s32[2]{0:T(128)}, u32[]{:S(2)}) copy-start(s32[2]{0:T(128)} %param.13) | copy-start | bytes 28
  19.0 48.2 %copy-start.4 = (bf16[256,768]{1,0:T(8,128)(2,1)}, bf16[256,768]{1,0:T(8,128)(2,1)S(1)}, u32[]{:S(2)}) copy-start(bf16[256,768]{1,0:T(8,128)(2,1)S(1)} %get-tuple-element.74.refs_4_) | copy-start | bytes 1179652
  19.0 52.1 %copy-start.3 = (bf16[256,768]{1,0:T(8,128)(2,1)}, bf16[256,768]{1,0:T(8,128)(2,1)S(1)}, u32[]{:S(2)}) copy-start(bf16[256,768]{1,0:T(8,128)(2,1)S(1)} %get-tuple-element.75.refs_4_) | copy-start | bytes 1179652
  19.0 38.4 %collective-permute-start.12 = (bf16[256,768]{1,0:T(8,128)(2,1)S(1)}, bf16[256,768]{1,0:T(8,128)(2,1)S(1)}, u32[]{:S(2)}, u32[]{:S(2)}) collective-permute-start(bf16[256,768]{1,0:T(8,128)(2,1)S(1)} %get-tuple-element.74.refs_4_), channel_id=1, source_target_pairs={{0,16},{2,18},{4,20},{6,22},{8,24},{10,26},{12,28},{14,30},{16,0},... | collective-permute-start | bytes 1179656 | tf_op jit(solution)/shard_map/ppermute | solution.py:276
  22.4 10.4 %collective-permute-start.7 = (bf16[256,256]{1,0:T(8,128)(2,1)S(1)}, bf16[256,256]{1,0:T(8,128)(2,1)S(1)}, u32[]{:S(2)}, u32[]{:S(2)}) collective-permute-start(bf16[256,256]{1,0:T(8,128)(2,1)S(1)} %bitcast.69), channel_id=1, source_target_pairs={{0,16},{16,0},{1,17},{17,1},{2,18},{18,2},{3,19},{19,3},{4,20},{20... | collective-permute-start | bytes 393224 | tf_op jit(solution)/shard_map/ppermute | solution.py:19
  27.4 23.6 %collective-permute-start.4 = (bf16[3,32,1536]{2,1,0:T(8,128)(2,1)}, bf16[3,32,1536]{2,1,0:T(8,128)(2,1)}, u32[]{:S(2)}, u32[]{:S(2)}) collective-permute-start(bf16[3,32,1536]{2,1,0:T(8,128)(2,1)} %get-tuple-element.66), channel_id=1, source_target_pairs={{0,8},{2,10},{4,12},{6,14},{8,0},{10,2},{12,4},{14,6},{1,9},{3,11}... | collective-permute-start | bytes 884744 | tf_op jit(solution)/shard_map/ppermute | solution.py:262
  30.2 27.2 %collective-permute-start.5 = (bf16[3,32,1536]{2,1,0:T(8,128)(2,1)}, bf16[3,32,1536]{2,1,0:T(8,128)(2,1)}, u32[]{:S(2)}, u32[]{:S(2)}) collective-permute-start(bf16[3,32,1536]{2,1,0:T(8,128)(2,1)} %get-tuple-element.65), channel_id=1, source_target_pairs={{0,10},{2,8},{4,14},{6,12},{8,2},{10,0},{12,6},{14,4},{1,11},{3,9}... | collective-permute-start | bytes 884744 | tf_op jit(solution)/shard_map/ppermute | solution.py:262
  32.8 26.2 %collective-permute-start.13 = (bf16[256,768]{1,0:T(8,128)(2,1)}, bf16[256,768]{1,0:T(8,128)(2,1)}, u32[]{:S(2)}, u32[]{:S(2)}) collective-permute-start(bf16[256,768]{1,0:T(8,128)(2,1)} %get-tuple-element.73), channel_id=1, source_target_pairs={{0,18},{2,16},{4,22},{6,20},{8,26},{10,24},{12,30},{14,28},{16,2},... | collective-permute-start | bytes 1179656 | tf_op jit(solution)/shard_map/ppermute | solution.py:276
  33.1 34.1 %copy-start.2 = (bf16[2,256,256]{2,1,0:T(8,128)(2,1)}, bf16[2,256,256]{2,1,0:T(8,128)(2,1)S(1)}, u32[]{:S(2)}) copy-start(bf16[2,256,256]{2,1,0:T(8,128)(2,1)S(1)} %pad_maximum_fusion.refs_0_) | copy-start | bytes 786436
  51.0 9.7 %collective-permute-start.10 = (bf16[2,256,256]{2,1,0:T(8,128)(2,1)S(1)}, bf16[2,256,256]{2,1,0:T(8,128)(2,1)S(1)}, u32[]{:S(2)}, u32[]{:S(2)}) collective-permute-start(bf16[2,256,256]{2,1,0:T(8,128)(2,1)S(1)} %pad_maximum_fusion.refs_0_), channel_id=1, source_target_pairs={{0,3},{1,2},{2,1},{3,0},{4,7},{5,6},{6,5},{7,4},{8,11},{9,10},{10,... | collective-permute-start | bytes 786440 | tf_op jit(solution)/shard_map/ppermute | solution.py:288
  57.4 3.5 %collective-permute-start.8 = (bf16[2,256,256]{2,1,0:T(8,128)(2,1)S(1)}, bf16[2,256,256]{2,1,0:T(8,128)(2,1)S(1)}, u32[]{:S(2)}, u32[]{:S(2)}) collective-permute-start(bf16[2,256,256]{2,1,0:T(8,128)(2,1)S(1)} %pad_maximum_fusion.refs_0_), channel_id=1, source_target_pairs={{0,2},{1,3},{2,0},{3,1},{4,6},{5,7},{6,4},{7,5},{8,10},{9,11},{10,... | collective-permute-start | bytes 786440 | tf_op jit(solution)/shard_map/ppermute | solution.py:288
  57.4 9.8 %copy-start.13 = (bf16[256,768]{1,0:T(8,128)(2,1)}, bf16[256,768]{1,0:T(8,128)(2,1)S(1)}, u32[]{:S(2)}) copy-start(bf16[256,768]{1,0:T(8,128)(2,1)S(1)} %collective-permute-done.12.refs_6_) | copy-start | bytes 1179652
  57.4 8.7 %collective-permute-start.9 = (bf16[2,256,256]{2,1,0:T(8,128)(2,1)S(1)}, bf16[2,256,256]{2,1,0:T(8,128)(2,1)S(1)}, u32[]{:S(2)}, u32[]{:S(2)}) collective-permute-start(bf16[2,256,256]{2,1,0:T(8,128)(2,1)S(1)} %pad_maximum_fusion.refs_0_), channel_id=1, source_target_pairs={{0,1},{1,0},{2,3},{3,2},{4,5},{5,4},{6,7},{7,6},{8,9},{9,8},{10,11... | collective-permute-start | bytes 786440 | tf_op jit(solution)/shard_map/ppermute | solution.py:288
  59.0 12.1 %collective-permute-start.6 = (bf16[3,32,1536]{2,1,0:T(8,128)(2,1)}, bf16[3,32,1536]{2,1,0:T(8,128)(2,1)}, u32[]{:S(2)}, u32[]{:S(2)}) collective-permute-start(bf16[3,32,1536]{2,1,0:T(8,128)(2,1)} %get-tuple-element.64), channel_id=1, source_target_pairs={{0,2},{2,0},{4,6},{6,4},{8,10},{10,8},{12,14},{14,12},{1,3},{3,1},... | collective-permute-start | bytes 884744 | tf_op jit(solution)/shard_map/ppermute | solution.py:262
  59.2 31.4 %collective-permute-start.19 = (bf16[256,768]{1,0:T(8,128)(2,1)S(1)}, bf16[256,768]{1,0:T(8,128)(2,1)S(1)}, u32[]{:S(2)}, u32[]{:S(2)}) collective-permute-start(bf16[256,768]{1,0:T(8,128)(2,1)S(1)} %get-tuple-element.75.refs_4_), channel_id=1, source_target_pairs={{0,16},{2,18},{4,20},{6,22},{8,24},{10,26},{12,28},{14,30},{16,0},... | collective-permute-start | bytes 1179656 | tf_op jit(solution)/shard_map/ppermute | solution.py:276
  60.7 6.5 %copy-start.5 = (bf16[2,256,256]{2,1,0:T(8,128)(2,1)}, bf16[2,256,256]{2,1,0:T(8,128)(2,1)S(1)}, u32[]{:S(2)}) copy-start(bf16[2,256,256]{2,1,0:T(8,128)(2,1)S(1)} %collective-permute-done.10.refs_3_) | copy-start | bytes 786436
  60.7 29.9 %collective-permute-start.20 = (bf16[256,768]{1,0:T(8,128)(2,1)}, bf16[256,768]{1,0:T(8,128)(2,1)}, u32[]{:S(2)}, u32[]{:S(2)}) collective-permute-start(bf16[256,768]{1,0:T(8,128)(2,1)} %get-tuple-element.72), channel_id=1, source_target_pairs={{0,18},{2,16},{4,22},{6,20},{8,26},{10,24},{12,30},{14,28},{16,2},... | collective-permute-start | bytes 1179656 | tf_op jit(solution)/shard_map/ppermute | solution.py:276
  60.9 6.3 %copy-start.6 = (bf16[2,256,256]{2,1,0:T(8,128)(2,1)}, bf16[2,256,256]{2,1,0:T(8,128)(2,1)S(1)}, u32[]{:S(2)}) copy-start(bf16[2,256,256]{2,1,0:T(8,128)(2,1)S(1)} %collective-permute-done.8.refs_1_) | copy-start | bytes 786436
  60.9 12.8 %collective-permute-start = (bf16[3,32,1536]{2,1,0:T(8,128)(2,1)}, bf16[3,32,1536]{2,1,0:T(8,128)(2,1)}, u32[]{:S(2)}, u32[]{:S(2)}) collective-permute-start(bf16[3,32,1536]{2,1,0:T(8,128)(2,1)} %get-tuple-element.16), channel_id=1, source_target_pairs={{0,12},{2,6},{4,8},{6,2},{8,4},{10,14},{12,0},{14,10},{1,13},{3,7}... | collective-permute-start | bytes 884744 | tf_op jit(solution)/shard_map/ppermute | solution.py:262
  66.2 1.1 copy-start.7
  66.2 11.6 %collective-permute-start.1 = (bf16[3,32,1536]{2,1,0:T(8,128)(2,1)}, bf16[3,32,1536]{2,1,0:T(8,128)(2,1)}, u32[]{:S(2)}, u32[]{:S(2)}) collective-permute-start(bf16[3,32,1536]{2,1,0:T(8,128)(2,1)} %get-tuple-element.17), channel_id=1, source_target_pairs={{0,4},{2,14},{4,0},{6,10},{8,12},{10,6},{12,8},{14,2},{1,5},{3,15}... | collective-permute-start | bytes 884744 | tf_op jit(solution)/shard_map/ppermute | solution.py:262
  71.1 26.1 %collective-permute-start.14 = (bf16[512,384]{1,0:T(8,128)(2,1)}, bf16[512,384]{1,0:T(8,128)(2,1)S(1)}, u32[]{:S(2)}, u32[]{:S(2)}) collective-permute-start(bf16[512,384]{1,0:T(8,128)(2,1)} %get-tuple-element.20), channel_id=1, source_target_pairs={{0,4},{2,6},{4,0},{6,2},{8,12},{10,14},{12,8},{14,10},{1,5},{3,7},... | collective-permute-start | bytes 1179656 | tf_op jit(solution)/shard_map/ppermute | solution.py:19
  84.5 79.3 %all-to-all-start = ((bf16[8,32,1536]{2,1,0:T(8,128)(2,1)}), bf16[8,32,1536]{2,1,0:T(8,128)(2,1)S(1)}, u32[]{:S(2)}, u32[]{:S(2)}) async-start(bf16[8,32,1536]{2,1,0:T(8,128)(2,1)} %temporal.1), calls=%async_computation | async-start | bytes 1572864 | tf_op jit(solution)/shard_map/all_to_all | solution.py:317
  90.6 6.6 %copy-start.9 = (f32[512,384]{1,0:T(8,128)S(1)}, f32[512,384]{1,0:T(8,128)}, u32[]{:S(2)}) copy-start(f32[512,384]{1,0:T(8,128)} %get-tuple-element.19) | copy-start | bytes 2359300
  95.2 24.9 %copy-start.10 = (f32[512,384]{1,0:T(8,128)S(1)}, f32[512,384]{1,0:T(8,128)}, u32[]{:S(2)}) copy-start(f32[512,384]{1,0:T(8,128)} %get-tuple-element.21) | copy-start | bytes 2359300
  95.2 24.9 %collective-permute-start.21 = (bf16[512,384]{1,0:T(8,128)(2,1)}, bf16[512,384]{1,0:T(8,128)(2,1)S(1)}, u32[]{:S(2)}, u32[]{:S(2)}) collective-permute-start(bf16[512,384]{1,0:T(8,128)(2,1)} %get-tuple-element.22), channel_id=1, source_target_pairs={{0,4},{2,6},{4,0},{6,2},{8,12},{10,14},{12,8},{14,10},{1,5},{3,7},... | collective-permute-start | bytes 1179656 | tf_op jit(solution)/shard_map/ppermute | solution.py:19
  98.2 22.9 %copy-start.8 = (bf16[1,1,256,1536]{3,2,1,0:T(8,128)(2,1)S(1)}, bf16[1,1,256,1536]{3,2,1,0:T(8,128)(2,1)}, u32[]{:S(2)}) copy-start(bf16[1,1,256,1536]{3,2,1,0:T(8,128)(2,1)} %param.8) | copy-start | bytes 2359300
  98.2 40.0 %collective-permute-start.15 = (bf16[512,384]{1,0:T(8,128)(2,1)S(1)}, bf16[512,384]{1,0:T(8,128)(2,1)S(1)}, u32[]{:S(2)}, u32[]{:S(2)}) collective-permute-start(bf16[512,384]{1,0:T(8,128)(2,1)S(1)} %get-tuple-element.62), channel_id=1, source_target_pairs={{0,8},{2,10},{4,12},{6,14},{8,0},{10,2},{12,4},{14,6},{1,9},{3,11}... | collective-permute-start | bytes 1179656 | tf_op jit(solution)/shard_map/ppermute | solution.py:19
  120.1 4.0 %copy-start.22 = (s32[2]{0:T(128)S(1)}, s32[2]{0:T(128)}, u32[]{:S(2)}) copy-start(s32[2]{0:T(128)} %param.12) | copy-start | bytes 28
  121.1 24.3 %collective-permute-start.22 = (bf16[512,384]{1,0:T(8,128)(2,1)S(1)}, bf16[512,384]{1,0:T(8,128)(2,1)S(1)}, u32[]{:S(2)}, u32[]{:S(2)}) collective-permute-start(bf16[512,384]{1,0:T(8,128)(2,1)S(1)} %get-tuple-element.60), channel_id=1, source_target_pairs={{0,8},{2,10},{4,12},{6,14},{8,0},{10,2},{12,4},{14,6},{1,9},{3,11}... | collective-permute-start | bytes 1179656 | tf_op jit(solution)/shard_map/ppermute | solution.py:19
  122.0 3.9 %collective-permute-start.16 = (bf16[256,384]{1,0:T(8,128)(2,1)}, bf16[256,384]{1,0:T(8,128)(2,1)S(1)}, u32[]{:S(2)}, u32[]{:S(2)}) collective-permute-start(bf16[256,384]{1,0:T(8,128)(2,1)} %get-tuple-element.79), channel_id=1, source_target_pairs={{0,2},{2,0},{4,6},{6,4},{8,10},{10,8},{12,14},{14,12},{1,3},{3,1},... | collective-permute-start | bytes 589832 | tf_op jit(solution)/shard_map/ppermute | solution.py:19
  122.0 12.9 %collective-permute-start.17 = (bf16[256,384]{1,0:T(8,128)(2,1)}, bf16[256,384]{1,0:T(8,128)(2,1)S(1)}, u32[]{:S(2)}, u32[]{:S(2)}) collective-permute-start(bf16[256,384]{1,0:T(8,128)(2,1)} %get-tuple-element.81), channel_id=1, source_target_pairs={{0,4},{2,6},{4,0},{6,2},{8,12},{10,14},{12,8},{14,10},{1,5},{3,7},... | collective-permute-start | bytes 589832 | tf_op jit(solution)/shard_map/ppermute | solution.py:19
  124.0 14.2 %collective-permute-start.18 = (bf16[256,384]{1,0:T(8,128)(2,1)}, bf16[256,384]{1,0:T(8,128)(2,1)S(1)}, u32[]{:S(2)}, u32[]{:S(2)}) collective-permute-start(bf16[256,384]{1,0:T(8,128)(2,1)} %get-tuple-element.78), channel_id=1, source_target_pairs={{0,6},{2,4},{4,2},{6,0},{8,14},{10,12},{12,10},{14,8},{1,7},{3,5},... | collective-permute-start | bytes 589832 | tf_op jit(solution)/shard_map/ppermute | solution.py:19
  125.9 12.3 %copy-start.15 = (bf16[256,384]{1,0:T(8,128)(2,1)}, bf16[256,384]{1,0:T(8,128)(2,1)S(1)}, u32[]{:S(2)}) copy-start(bf16[256,384]{1,0:T(8,128)(2,1)S(1)} %collective-permute-done.16.refs_1_) | copy-start | bytes 589828
  134.9 3.3 %copy-start.16 = (bf16[256,384]{1,0:T(8,128)(2,1)}, bf16[256,384]{1,0:T(8,128)(2,1)S(1)}, u32[]{:S(2)}) copy-start(bf16[256,384]{1,0:T(8,128)(2,1)S(1)} %collective-permute-done.17.refs_2_) | copy-start | bytes 589828
  138.2 0.8 copy-start.12
  145.4 0.8 copy-start.11
  150.1 13.8 %collective-permute-start.23 = (bf16[256,384]{1,0:T(8,128)(2,1)}, bf16[256,384]{1,0:T(8,128)(2,1)S(1)}, u32[]{:S(2)}, u32[]{:S(2)}) collective-permute-start(bf16[256,384]{1,0:T(8,128)(2,1)} %get-tuple-element.24), channel_id=1, source_target_pairs={{0,4},{2,6},{4,0},{6,2},{8,12},{10,14},{12,8},{14,10},{1,5},{3,7},... | collective-permute-start | bytes 589832 | tf_op jit(solution)/shard_map/ppermute | solution.py:19
  156.0 7.9 %collective-permute-start.24 = (bf16[256,384]{1,0:T(8,128)(2,1)}, bf16[256,384]{1,0:T(8,128)(2,1)S(1)}, u32[]{:S(2)}, u32[]{:S(2)}) collective-permute-start(bf16[256,384]{1,0:T(8,128)(2,1)} %get-tuple-element.25), channel_id=1, source_target_pairs={{0,2},{2,0},{4,6},{6,4},{8,10},{10,8},{12,14},{14,12},{1,3},{3,1},... | collective-permute-start | bytes 589832 | tf_op jit(solution)/shard_map/ppermute | solution.py:19
  156.2 10.0 %collective-permute-start.25 = (bf16[256,384]{1,0:T(8,128)(2,1)}, bf16[256,384]{1,0:T(8,128)(2,1)S(1)}, u32[]{:S(2)}, u32[]{:S(2)}) collective-permute-start(bf16[256,384]{1,0:T(8,128)(2,1)} %get-tuple-element.26), channel_id=1, source_target_pairs={{0,6},{2,4},{4,2},{6,0},{8,14},{10,12},{12,10},{14,8},{1,7},{3,5},... | collective-permute-start | bytes 589832 | tf_op jit(solution)/shard_map/ppermute | solution.py:19
  163.8 2.4 %copy-start.1 = (bf16[8,32,1536]{2,1,0:T(8,128)(2,1)}, bf16[8,32,1536]{2,1,0:T(8,128)(2,1)S(1)}, u32[]{:S(2)}) copy-start(bf16[8,32,1536]{2,1,0:T(8,128)(2,1)S(1)} %all-to-all-done) | copy-start | bytes 2359300
  163.8 2.3 %copy-start.18 = (bf16[256,384]{1,0:T(8,128)(2,1)}, bf16[256,384]{1,0:T(8,128)(2,1)S(1)}, u32[]{:S(2)}) copy-start(bf16[256,384]{1,0:T(8,128)(2,1)S(1)} %collective-permute-done.23.refs_1_) | copy-start | bytes 589828
  163.9 2.3 %copy-start.19 = (bf16[256,384]{1,0:T(8,128)(2,1)}, bf16[256,384]{1,0:T(8,128)(2,1)S(1)}, u32[]{:S(2)}) copy-start(bf16[256,384]{1,0:T(8,128)(2,1)S(1)} %collective-permute-done.24.refs_2_) | copy-start | bytes 589828
  (3 other events, 2.1 us)

commit v3 on v2

--- a/solution.py
+++ b/solution.py
@@ -12,6 +12,9 @@
 HDIM = 128
 BF16 = jnp.bfloat16
 F32 = jnp.float32
+
+
+MODEST = pltpu.CompilerParams(vmem_limit_bytes=24 << 20)
 
 
 def swap(value, axis, bits):
@@ -60,6 +63,7 @@
             out_specs=pl.BlockSpec(shape, lambda j, s: (0, 0, 0, 0)),
         ),
         out_shape=jax.ShapeDtypeStruct(shape, BF16),
+        compiler_params=MODEST,
         name="prompt_blocks",
     )(side.reshape(1), states)
 
@@ -90,6 +94,10 @@
 SMEM_SPEC = pl.BlockSpec(memory_space=pltpu.SMEM)
 
 
+def on_chip(*values):
+    return [pltpu.with_memory_space_constraint(v, pltpu.VMEM) for v in values]
+
+
 def project(states, weights, near):
     _, rows, _ = states[0].shape
     n_rows = len(states) // 2
@@ -98,9 +106,10 @@
         functools.partial(project_kernel, n_rows),
         in_specs=[SMEM_SPEC] + [VMEM_SPEC] * (len(states) + len(weights)),
         out_specs=[VMEM_SPEC] * 2,
-        out_shape=[jax.ShapeDtypeStruct(shape, F32), jax.ShapeDtypeStruct(shape, BF16)],
+        out_shape=[pltpu.VMEM(shape, F32), pltpu.VMEM(shape, BF16)],
+        compiler_params=MODEST,
         name="project",
-    )(near.reshape(1), *states, *weights)
+    )(near.reshape(1), *on_chip(*states, *weights))
 
 
 def spatial_kernel(qkv_ref, residual_ref, out_ref):
@@ -123,6 +132,7 @@
         ],
         out_specs=pl.BlockSpec((tokens, cols), lambda j: (0, j)),
         out_shape=jax.ShapeDtypeStruct((tokens, width), F32),
+        compiler_params=MODEST,
         name="spatial",
     )(qkv, residual)
 
@@ -158,6 +168,7 @@
             out_specs=pl.BlockSpec((frames, tokens, cols), lambda j, s: (0, 0, j)),
         ),
         out_shape=jax.ShapeDtypeStruct((frames, tokens, width), BF16),
+        compiler_params=MODEST,
         name="temporal",
     )(places, *pieces)
 
@@ -178,9 +189,10 @@
         weigh_kernel,
         in_specs=[VMEM_SPEC] * (3 + len(queries)),
         out_specs=VMEM_SPEC,
-        out_shape=jax.ShapeDtypeStruct((width // HDIM, len(queries), tokens, rows), BF16),
+        out_shape=pltpu.VMEM((width // HDIM, len(queries), tokens, rows), BF16),
+        compiler_params=MODEST,
         name="cross_weights",
-    )(bias, kept, come, *queries)
+    )(*on_chip(bias, kept, come, *queries))
 
 
 def value_kernel(weight_ref, kept_ref, come_ref, *out_refs):
@@ -199,9 +211,10 @@
         value_kernel,
         in_specs=[VMEM_SPEC] * 3,
         out_specs=[VMEM_SPEC] * count,
-        out_shape=[jax.ShapeDtypeStruct((tokens, width), F32 if j == 0 else BF16) for j in range(count)],
+        out_shape=[pltpu.VMEM((tokens, width), F32 if j == 0 else BF16) for j in range(count)],
+        compiler_params=MODEST,
         name="cross_values",
-    )(weights, kept, come)
+    )(*on_chip(weights, kept, come))
 
 
 def final_kernel(scalar_ref, base_ref, temporal_ref, *refs):
@@ -219,8 +232,9 @@
         in_specs=[SMEM_SPEC] + [VMEM_SPEC] * (2 + len(pieces)),
         out_specs=VMEM_SPEC,
         out_shape=jax.ShapeDtypeStruct(base.shape, BF16),
+        compiler_params=MODEST,
         name="final",
-    )(place.reshape(1), base, temporal, *pieces)
+    )(place.reshape(1), *on_chip(base, temporal, *pieces))
 
 
 def temporal_plan(seq):
@@ -276,16 +290,17 @@
                 weights[kind].append(lax.ppermute(part, ("grp", "seq"), pairs))
 
     def slot(k):
-        index = jnp.take(assignment, group ^ k)
+        index = lax.dynamic_index_in_dim(assignment, group ^ k, keepdims=False)
         return lax.dynamic_index_in_dim(parts, index, 1, keepdims=False).reshape(rows, feats)
 
     wanted = jnp.stack([slot(0)] + [swap(slot(k), "grp", k) for k in range(1, grp)])
-    n_pairs = [(s, h) for s in range(seq) for h in range(sides)]
     states = []
     for k in range(sides):
-        for c in range(2):
-            pairs = [(s * sides + h, (s ^ c) * sides + (h ^ k)) for s, h in n_pairs]
-            states.append(wanted if k + c == 0 else lax.ppermute(wanted, ("seq", "hd"), pairs))
+        if k:
+            other = swap(wanted, "hd", k)
+        else:
+            other = wanted
+        states += [other, swap(other, "seq", 1)]
 
     quarter = width // 4
     query = cross_query[0, 0]
@@ -309,7 +324,8 @@
     row = jnp.arange(rows * sides)
     which, source, inner = row // rows, (row % rows) // rows_side, row % rows_side
     position = source * rows_here + (which ^ side) * rows_side + inner
-    length = jnp.take(prompt_lengths, jnp.take(assignment, group))
+    served = lax.dynamic_index_in_dim(assignment, group, keepdims=False)
+    length = lax.dynamic_index_in_dim(prompt_lengths, served, keepdims=False)
     bias = jnp.where(position < length, 0.0, -1e9).astype(F32)[None]
 
     base = spatial_attention(qkv, residual[0, 0])

time: 171 us -> 174 us (1.018)
  local copies, waits for them, and re-layouts: 13.5 us -> 29 us
  Pallas kernels: 34.8 us -> 23.7 us
  starting transfers between devices: 46.5 us -> 38.7 us
  waiting for transfers between devices: 70.4 us -> 72.9 us
  between operations: 2.07 us -> 4.12 us
    unnamed x47 -> x51, local copies, waits for them, and re-layouts: 4.6 us -> 16.7 us
    ppermute x12 -> x15, waiting for transfers between devices: 37.4 us -> 41.1 us  [swap(): return lax.ppermute(value, axis, pairs)]
    ppermute x3 -> x0, starting transfers between devices: 2.83 us -> none  [block(): lax.ppermute(wanted, ('seq', 'hd'), pairs)]
    ppermute x12 -> x15, starting transfers between devices: 17 us -> 14.3 us  [swap(): return lax.ppermute(value, axis, pairs)]
    pallas_call x2, Pallas kernels: 7.68 us -> 5.35 us  [project(): pl.pallas_call(functools.partial(project_kernel, n_rows), in_specs=[SMEM_...]
    pallas_call x1, Pallas kernels: 3.92 us -> 1.69 us  [cross_values(): pl.pallas_call(value_kernel, in_specs=[VMEM_SPEC] * 3, out_specs=[VMEM_SP...]
    all_to_all x1, starting transfers between devices: 6.03 us -> 3.83 us  [block(): lax.all_to_all(temporal, 'seq', 0, 0, tiled=True).reshape(tokens, width)]
    pallas_call x1, Pallas kernels: 5.23 us -> 3.21 us  [cross_weights(): pl.pallas_call(weigh_kernel, in_specs=[VMEM_SPEC] * (3 + len(queries)), o...]
  transfers between devices with their start and end apart: 28 -> 28, of which waited for: 11 -> 12; matrix products, arithmetic and copies ran while one was open for 8% -> 11% of each run, Pallas kernels for 18% -> 12%
where the time goes in v3:
time: 174 us; the launch traced here: 172 us
  waiting for transfers between devices  72.9 us (42%)
  starting transfers between devices  38.7 us (22%)
  local copies, waits for them, and re-layouts  29 us (17%)
  Pallas kernels  23.7 us (14%)
  between operations  4.12 us (2%)
  other arithmetic  3.92 us (2%)
    ppermute x15, waiting for transfers between devices, swap(): return lax.ppermute(value, axis, pairs)  41.1 us
    ppermute x7, waiting for transfers between devices, block(): pieces.append(lax.ppermute(blocks[number], 'seq', pairs))  31 us
    unnamed x51, local copies, waits for them, and re-layouts  16.7 us
    ppermute x15, starting transfers between devices, swap(): return lax.ppermute(value, axis, pairs)  14.3 us
    ppermute x7, starting transfers between devices, block(): pieces.append(lax.ppermute(blocks[number], 'seq', pairs))  9.61 us
    all_to_all x1, starting transfers between devices, block(): parts = lax.all_to_all(parts, 'seq', 0, 0, tiled=True)  6.49 us
    pallas_call x1, Pallas kernels, temporal_attention(): pl.pallas_call(functools.partial(temporal_kernel, frames), grid_spec=pltp...  5.92 us
    pallas_call x2, Pallas kernels, project(): pl.pallas_call(functools.partial(project_kernel, n_rows), in_specs=[SMEM_...  5.35 us
  transfers between devices with their start and end apart: 28, of which 12 were waited for; matrix products, arithmetic and copies ran while one was open for 11% of the time, Pallas kernels for 12%

profile of v3, /device:TPU:0, one launch (start us, length us, event | category | flops | bytes accessed | tf_op | source)
XLA Modules:
  0.0 172.4 jit_solution(2912200864780783486)
XLA Ops:
  0.0 1.0 copy-done.14
  1.8 6.5 %all-to-all-start.1 = ((bf16[8,2,32,256]{3,2,1,0:T(8,128)(2,1)}), bf16[8,2,32,256]{3,2,1,0:T(8,128)(2,1)S(1)}, u32[]{:S(2)}, u32[]{:S(2)}) async-start(bf16[8,2,32,256]{3,2,1,0:T(8,128)(2,1)} %prompt_blocks.1), calls=%async_computation.1 | async-start | bytes 524288 | tf_op jit(solution)/shard_map/all_to_all | solution.py:258
  8.3 2.1 %dynamic-slice_bitcast_fusion.4 = (bf16[3,32,1536]{2,1,0:T(8,128)(2,1)}, bf16[3,32,1536]{2,1,0:T(8,128)(2,1)}, bf16[3,32,1536]{2,1,0:T(8,128)(2,1)}) fusion(bf16[1,1,256,3,1536]{4,2,3,1,0:T(8,128)(2,1)} %param.7, s32[]{:T(128)S(6)} %select_n.151, s32[]{:T(128)S(6)} %select_n.149, s32[]{:T(128)S(6)} %select_n.150), kind=kLoop, calls=%fused_computation.9 | loop fusion | bytes 1769484 | tf_op jit(solution)/shard_map/dynamic_slice | solution.py:270
  10.4 1.2 constant_dynamic-slice_fusion.3
  11.5 3.5 %collective-permute-start.2 = (bf16[3,32,1536]{2,1,0:T(8,128)(2,1)}, bf16[3,32,1536]{2,1,0:T(8,128)(2,1)S(1)}, u32[]{:S(2)}, u32[]{:S(2)}) collective-permute-start(bf16[3,32,1536]{2,1,0:T(8,128)(2,1)} %get-tuple-element.35), channel_id=1, source_target_pairs={{0,14},{2,4},{4,10},{6,0},{8,6},{10,12},{12,2},{14,8},{1,15},{3,5}... | collective-permute-start | bytes 884744 | tf_op jit(solution)/shard_map/ppermute | solution.py:276
  18.3 2.7 %copy.10 = bf16[256,2,1536]{2,0,1:T(8,128)(2,1)} copy(bf16[256,2,1536]{2,1,0:T(2,128)(2,1)} %param.11) | data formatting | bytes 3145728 | tf_op args[4]
  22.4 1.6 collective-permute-start.7
  24.0 2.1 %constant_dynamic-slice_fusion = bf16[2,256,768]{2,1,0:T(8,128)(2,1)} fusion(bf16[2,256,1536]{2,1,0:T(8,128)(2,1)} %bitcast.62, s32[]{:T(128)S(6)} %select_n.170), kind=kLoop, calls=%fused_computation.22 | loop fusion | bytes 1572868 | tf_op jit(solution)/shard_map/dynamic_slice | solution.py:281
  26.1 1.1 collective-permute-start.4
  27.5 1.6 collective-permute-start.5
  29.9 1.5 collective-permute-start.9
  31.4 2.4 %dynamic-slice_bitcast_fusion = (bf16[256,768]{1,0:T(8,128)(2,1)}, bf16[256,768]{1,0:T(8,128)(2,1)}, bf16[256,768]{1,0:T(8,128)(2,1)S(1)}, bf16[256,768]{1,0:T(8,128)(2,1)}) fusion(bf16[2,256,1536]{2,1,0:T(8,128)(2,1)} %bitcast.63, s32[]{:T(128)S(6)} %add.152, s32[]{:T(128)S(6)} %select_n.170, s32[]{:T(128)S(6)} %select_n.169), kind=kLoop, calls=%fused_computation.3 | loop fusion | bytes 3145740 | tf_op jit(solution)/shard_map/squeeze | solution.py:288
  33.8 3.8 %collective-permute-done.3.refs_4_ = bf16[3,32,1536]{2,1,0:T(8,128)(2,1)} collective-permute-done((bf16[3,32,1536]{2,1,0:T(8,128)(2,1)}, bf16[3,32,1536]{2,1,0:T(8,128)(2,1)}, u32[]{:S(2)}, u32[]{:S(2)}) %collective-permute-start.3) | collective-permute-done | bytes 294944 | tf_op jit(solution)/shard_map/ppermute | solution.py:276
  38.1 14.8 %collective-permute-done.4.refs_5_ = bf16[3,32,1536]{2,1,0:T(8,128)(2,1)} collective-permute-done((bf16[3,32,1536]{2,1,0:T(8,128)(2,1)}, bf16[3,32,1536]{2,1,0:T(8,128)(2,1)}, u32[]{:S(2)}, u32[]{:S(2)}) %collective-permute-start.4) | collective-permute-done | bytes 294944 | tf_op jit(solution)/shard_map/ppermute | solution.py:276
  53.0 1.5 collective-permute-start.13
  54.5 5.5 %collective-permute-done.5.refs_6_ = bf16[3,32,1536]{2,1,0:T(8,128)(2,1)S(1)} collective-permute-done((bf16[3,32,1536]{2,1,0:T(8,128)(2,1)}, bf16[3,32,1536]{2,1,0:T(8,128)(2,1)S(1)}, u32[]{:S(2)}, u32[]{:S(2)}) %collective-permute-start.5) | collective-permute-done | bytes 294944 | tf_op jit(solution)/shard_map/ppermute | solution.py:276
  63.5 1.7 collective-permute-start.19
  65.9 3.4 %collective-permute-start = (bf16[3,32,1536]{2,1,0:T(8,128)(2,1)}, bf16[3,32,1536]{2,1,0:T(8,128)(2,1)}, u32[]{:S(2)}, u32[]{:S(2)}) collective-permute-start(bf16[3,32,1536]{2,1,0:T(8,128)(2,1)} %get-tuple-element.16), channel_id=1, source_target_pairs={{0,12},{2,6},{4,8},{6,2},{8,4},{10,14},{12,0},{14,10},{1,13},{3,7}... | collective-permute-start | bytes 884744 | tf_op jit(solution)/shard_map/ppermute | solution.py:276
  69.2 1.9 %slice_bitcast_fusion = (bf16[256,768]{1,0:T(8,128)(2,1)}, bf16[256,768]{1,0:T(8,128)(2,1)S(1)}) fusion(bf16[2,256,768]{2,1,0:T(8,128)(2,1)} %collective-permute-done.11), kind=kLoop, calls=%fused_computation.4 | loop fusion | bytes 1572864 | tf_op jit(solution)/shard_map/squeeze | solution.py:286
  71.1 2.6 %project.2 = (f32[512,384]{1,0:T(8,128)S(1)}, bf16[512,384]{1,0:T(8,128)(2,1)}) custom-call(s32[1]{0:T(128)} %bitcast.22.scalar_ref, bf16[2,256,256]{2,1,0:T(8,128)(2,1)S(1)} %pad_maximum_fusion.refs_0_, bf16[2,256,256]{2,1,0:T(8,128)(2,1)} %collective-permute-done.8.refs_1_, bf16[2,256,256]{2,1,0:T(8,128)(2,1)S(1)} %copy-done.9, ...), custom_call_target="tpu_custom_call" | custom-call | tf_op jit(solution)/shard_map/project/pallas_call | solution.py:105
  74.7 2.0 %collective-permute-start.14 = (bf16[512,384]{1,0:T(8,128)(2,1)}, bf16[512,384]{1,0:T(8,128)(2,1)}, u32[]{:S(2)}, u32[]{:S(2)}) collective-permute-start(bf16[512,384]{1,0:T(8,128)(2,1)} %get-tuple-element.20), channel_id=1, source_target_pairs={{0,4},{2,6},{4,0},{6,2},{8,12},{10,14},{12,8},{14,10},{1,5},{3,7},... | collective-permute-start | bytes 1179656 | tf_op jit(solution)/shard_map/ppermute | solution.py:22
  76.8 1.2 collective-permute-done.refs_1_
  78.0 5.7 %collective-permute-done.1.refs_2_ = bf16[3,32,1536]{2,1,0:T(8,128)(2,1)} collective-permute-done((bf16[3,32,1536]{2,1,0:T(8,128)(2,1)}, bf16[3,32,1536]{2,1,0:T(8,128)(2,1)}, u32[]{:S(2)}, u32[]{:S(2)}) %collective-permute-start.1) | collective-permute-done | bytes 294944 | tf_op jit(solution)/shard_map/ppermute | solution.py:276
  83.7 1.0 copy-done.7
  84.6 1.0 copy-done.20
  85.6 1.0 copy-done.22
  86.5 5.9 %temporal.1 = bf16[8,32,1536]{2,1,0:T(8,128)(2,1)S(1)} custom-call(s32[8]{0:T(128)S(1)} %stack.41.scalar_ref, bf16[3,32,1536]{2,1,0:T(8,128)(2,1)S(1)} %copy-done.7, bf16[3,32,1536]{2,1,0:T(8,128)(2,1)} %collective-permute-done.refs_1_, bf16[3,32,1536]{2,1,0:T(8,128)(2,1)} %collective-permute-done.1.refs_2_, bf16[3,32,1536]{2,1,0:T(8,128)(2,1)S(1)} %copy-done.20, ...), custom_call_target="tpu_custom_call" | custom-call | tf_op jit(solution)/shard_map/temporal/pallas_call | solution.py:162
  93.4 3.8 %all-to-all-start = ((bf16[8,32,1536]{2,1,0:T(8,128)(2,1)}), bf16[8,32,1536]{2,1,0:T(8,128)(2,1)S(1)}, u32[]{:S(2)}, u32[]{:S(2)}) async-start(bf16[8,32,1536]{2,1,0:T(8,128)(2,1)} %copy-done.4), calls=%async_computation | async-start | bytes 1572864 | tf_op jit(solution)/shard_map/all_to_all | solution.py:333
  97.2 1.0 copy-done.6
  98.2 0.9 copy-done.10
  99.2 2.7 %project.3 = (f32[512,384]{1,0:T(8,128)S(1)}, bf16[512,384]{1,0:T(8,128)(2,1)S(1)}) custom-call(s32[1]{0:T(128)} %bitcast.22.scalar_ref, bf16[2,256,256]{2,1,0:T(8,128)(2,1)S(1)} %pad_maximum_fusion.refs_0_, bf16[2,256,256]{2,1,0:T(8,128)(2,1)} %collective-permute-done.8.refs_1_, bf16[2,256,256]{2,1,0:T(8,128)(2,1)S(1)} %copy-done.10, ...), custom_call_target="tpu_custom_call" | custom-call | tf_op jit(solution)/shard_map/project/pallas_call | solution.py:105
  101.9 2.1 %collective-permute-start.21 = (bf16[512,384]{1,0:T(8,128)(2,1)S(1)}, bf16[512,384]{1,0:T(8,128)(2,1)S(1)}, u32[]{:S(2)}, u32[]{:S(2)}) collective-permute-start(bf16[512,384]{1,0:T(8,128)(2,1)S(1)} %get-tuple-element.22), channel_id=1, source_target_pairs={{0,4},{2,6},{4,0},{6,2},{8,12},{10,14},{12,8},{14,10},{1,5},{3,7},... | collective-permute-start | bytes 1179656 | tf_op jit(solution)/shard_map/ppermute | solution.py:22
  104.0 2.1 %fusion.5 = (bf16[512,384]{1,0:T(8,128)(2,1)}, f32[512,384]{1,0:T(8,128)}) fusion(f32[512,384]{1,0:T(8,128)S(1)} %copy-done.13, bf16[512,384]{1,0:T(8,128)(2,1)} %collective-permute-done.14), kind=kLoop, calls=%fused_computation.40 | loop fusion | flops 589824 | bytes 2359296 | tf_op jit(solution)/shard_map/convert_element_type | solution.py:318
  106.1 2.4 %collective-permute-start.15 = (bf16[512,384]{1,0:T(8,128)(2,1)}, bf16[512,384]{1,0:T(8,128)(2,1)}, u32[]{:S(2)}, u32[]{:S(2)}) collective-permute-start(bf16[512,384]{1,0:T(8,128)(2,1)} %get-tuple-element.29), channel_id=1, source_target_pairs={{0,8},{2,10},{4,12},{6,14},{8,0},{10,2},{12,4},{14,6},{1,9},{3,11}... | collective-permute-start | bytes 1179656 | tf_op jit(solution)/shard_map/ppermute | solution.py:22
  108.5 18.3 %collective-permute-done.21 = bf16[512,384]{1,0:T(8,128)(2,1)S(1)} collective-permute-done((bf16[512,384]{1,0:T(8,128)(2,1)S(1)}, bf16[512,384]{1,0:T(8,128)(2,1)S(1)}, u32[]{:S(2)}, u32[]{:S(2)}) %collective-permute-start.21) | collective-permute-done | bytes 393248 | tf_op jit(solution)/shard_map/ppermute | solution.py:22
  126.7 1.1 fusion.4
  127.9 1.4 dynamic-slice_bitcast_fusion.7
  129.3 2.0 %collective-permute-start.17 = (bf16[256,384]{1,0:T(8,128)(2,1)S(1)}, bf16[256,384]{1,0:T(8,128)(2,1)S(1)}, u32[]{:S(2)}, u32[]{:S(2)}) collective-permute-start(bf16[256,384]{1,0:T(8,128)(2,1)S(1)} %get-tuple-element.48), channel_id=1, source_target_pairs={{0,4},{2,6},{4,0},{6,2},{8,12},{10,14},{12,8},{14,10},{1,5},{3,7},... | collective-permute-start | bytes 589832 | tf_op jit(solution)/shard_map/ppermute | solution.py:22
  132.6 9.2 %collective-permute-done.17.refs_2_ = bf16[256,384]{1,0:T(8,128)(2,1)S(1)} collective-permute-done((bf16[256,384]{1,0:T(8,128)(2,1)S(1)}, bf16[256,384]{1,0:T(8,128)(2,1)S(1)}, u32[]{:S(2)}, u32[]{:S(2)}) %collective-permute-start.17) | collective-permute-done | bytes 196640 | tf_op jit(solution)/shard_map/ppermute | solution.py:22
  141.8 10.6 %collective-permute-done.18.refs_3_ = bf16[256,384]{1,0:T(8,128)(2,1)S(1)} collective-permute-done((bf16[256,384]{1,0:T(8,128)(2,1)S(1)}, bf16[256,384]{1,0:T(8,128)(2,1)S(1)}, u32[]{:S(2)}, u32[]{:S(2)}) %collective-permute-start.18) | collective-permute-done | bytes 196640 | tf_op jit(solution)/shard_map/ppermute | solution.py:22
  152.3 3.2 %cross_weights.1.weight_ref = bf16[3,4,256,512]{3,2,1,0:T(8,128)(2,1)S(1)} custom-call(f32[1,512]{1,0:T(1,128)S(1)} %compare_select_fusion.bias_ref, f32[512,384]{1,0:T(8,128)S(1)} %copy-done.3, bf16[512,384]{1,0:T(8,128)(2,1)} %collective-permute-done.15.come_ref, bf16[256,384]{1,0:T(8,128)(2,1)S(1)} %get-tuple-element.47.refs_0_, ...), custom_call_target="tpu_custom_call" | custom-call | tf_op jit(solution)/shard_map/cross_weights/pallas_call | solution.py:188
  155.6 1.7 cross_values.1
  158.2 2.0 %collective-permute-start.25 = (bf16[256,384]{1,0:T(8,128)(2,1)}, bf16[256,384]{1,0:T(8,128)(2,1)}, u32[]{:S(2)}, u32[]{:S(2)}) collective-permute-start(bf16[256,384]{1,0:T(8,128)(2,1)} %get-tuple-element.26), channel_id=1, source_target_pairs={{0,6},{2,4},{4,2},{6,0},{8,14},{10,12},{12,10},{14,8},{1,7},{3,5},... | collective-permute-start | bytes 589832 | tf_op jit(solution)/shard_map/ppermute | solution.py:22
  160.2 4.5 %spatial.1.base_ref = f32[256,1536]{1,0:T(8,128)S(1)} custom-call(bf16[3,256,1536]{2,1,0:T(8,128)(2,1)S(1)} %bitcast.59, bf16[256,1536]{1,0:T(8,128)(2,1)S(1)} %bitcast.61), custom_call_target="tpu_custom_call" | custom-call | tf_op jit(solution)/shard_map/spatial/pallas_call | solution.py:126
  164.7 1.2 copy-done.1
  166.1 2.5 %collective-permute-done.25.refs_3_ = bf16[256,384]{1,0:T(8,128)(2,1)} collective-permute-done((bf16[256,384]{1,0:T(8,128)(2,1)}, bf16[256,384]{1,0:T(8,128)(2,1)}, u32[]{:S(2)}, u32[]{:S(2)}) %collective-permute-start.25) | collective-permute-done | bytes 196640 | tf_op jit(solution)/shard_map/ppermute | solution.py:22
  168.7 1.4 copy-done.2
  170.1 2.3 %final.1 = bf16[256,1536]{1,0:T(8,128)(2,1)} custom-call(s32[1]{0:T(128)} %bitcast.scalar_ref, f32[256,1536]{1,0:T(8,128)S(1)} %copy-done.2, bf16[256,1536]{1,0:T(8,128)(2,1)S(1)} %bitcast.60, f32[256,384]{1,0:T(8,128)S(1)} %copy-done.16, bf16[256,384]{1,0:T(8,128)(2,1)} %collective-permute-done.23.refs_1_, ...), custom_call_target="tpu_custom_call" | custom-call | tf_op jit(solution)/shard_map/final/pallas_call | solution.py:230
  (81 shorter events, 11.7 us)
Async XLA Ops:
  0.0 1.0 copy-start.14
  1.0 9.3 %copy-start = (bf16[1,1,256,3,1536]{4,2,3,1,0:T(8,128)(2,1)S(1)}, bf16[1,1,256,3,1536]{4,2,3,1,0:T(8,128)(2,1)}, u32[]{:S(2)}) copy-start(bf16[1,1,256,3,1536]{4,2,3,1,0:T(8,128)(2,1)} %param.7) | copy-start | bytes 7077892
  1.8 20.6 %all-to-all-start.1 = ((bf16[8,2,32,256]{3,2,1,0:T(8,128)(2,1)}), bf16[8,2,32,256]{3,2,1,0:T(8,128)(2,1)S(1)}, u32[]{:S(2)}, u32[]{:S(2)}) async-start(bf16[8,2,32,256]{3,2,1,0:T(8,128)(2,1)} %prompt_blocks.1), calls=%async_computation.1 | async-start | bytes 524288 | tf_op jit(solution)/shard_map/all_to_all | solution.py:258
  10.4 4.7 %copy-start.23 = (s32[2]{0:T(128)S(1)}, s32[2]{0:T(128)}, u32[]{:S(2)}) copy-start(s32[2]{0:T(128)} %param.13) | copy-start | bytes 28
  11.5 17.6 %collective-permute-start.2 = (bf16[3,32,1536]{2,1,0:T(8,128)(2,1)}, bf16[3,32,1536]{2,1,0:T(8,128)(2,1)S(1)}, u32[]{:S(2)}, u32[]{:S(2)}) collective-permute-start(bf16[3,32,1536]{2,1,0:T(8,128)(2,1)} %get-tuple-element.35), channel_id=1, source_target_pairs={{0,14},{2,4},{4,10},{6,0},{8,6},{10,12},{12,2},{14,8},{1,15},{3,5}... | collective-permute-start | bytes 884744 | tf_op jit(solution)/shard_map/ppermute | solution.py:276
  22.4 5.0 %collective-permute-start.7 = (bf16[256,256]{1,0:T(8,128)(2,1)S(1)}, bf16[256,256]{1,0:T(8,128)(2,1)S(1)}, u32[]{:S(2)}, u32[]{:S(2)}) collective-permute-start(bf16[256,256]{1,0:T(8,128)(2,1)S(1)} %bitcast.66), channel_id=1, source_target_pairs={{0,16},{16,0},{1,17},{17,1},{2,18},{18,2},{3,19},{19,3},{4,20},{20... | collective-permute-start | bytes 393224 | tf_op jit(solution)/shard_map/ppermute | solution.py:22
  26.1 39.1 %collective-permute-start.11 = (bf16[2,256,768]{2,1,0:T(8,128)(2,1)}, bf16[2,256,768]{2,1,0:T(8,128)(2,1)}, u32[]{:S(2)}, u32[]{:S(2)}) collective-permute-start(bf16[2,256,768]{2,1,0:T(8,128)(2,1)} %constant_dynamic-slice_fusion), channel_id=1, source_target_pairs={{0,2},{2,0},{4,6},{6,4},{8,10},{10,8},{12,14},{14,12},{1,3},{3,1},... | collective-permute-start | bytes 2359304 | tf_op jit(solution)/shard_map/ppermute | solution.py:22
  26.1 11.5 %collective-permute-start.3 = (bf16[3,32,1536]{2,1,0:T(8,128)(2,1)}, bf16[3,32,1536]{2,1,0:T(8,128)(2,1)}, u32[]{:S(2)}, u32[]{:S(2)}) collective-permute-start(bf16[3,32,1536]{2,1,0:T(8,128)(2,1)} %get-tuple-element.34), channel_id=1, source_target_pairs={{0,6},{2,12},{4,2},{6,8},{8,14},{10,4},{12,10},{14,0},{1,7},{3,13}... | collective-permute-start | bytes 884744 | tf_op jit(solution)/shard_map/ppermute | solution.py:276
  26.1 26.9 %collective-permute-start.4 = (bf16[3,32,1536]{2,1,0:T(8,128)(2,1)}, bf16[3,32,1536]{2,1,0:T(8,128)(2,1)}, u32[]{:S(2)}, u32[]{:S(2)}) collective-permute-start(bf16[3,32,1536]{2,1,0:T(8,128)(2,1)} %get-tuple-element.33), channel_id=1, source_target_pairs={{0,8},{2,10},{4,12},{6,14},{8,0},{10,2},{12,4},{14,6},{1,9},{3,11}... | collective-permute-start | bytes 884744 | tf_op jit(solution)/shard_map/ppermute | solution.py:276
  27.5 32.5 %collective-permute-start.5 = (bf16[3,32,1536]{2,1,0:T(8,128)(2,1)}, bf16[3,32,1536]{2,1,0:T(8,128)(2,1)S(1)}, u32[]{:S(2)}, u32[]{:S(2)}) collective-permute-start(bf16[3,32,1536]{2,1,0:T(8,128)(2,1)} %get-tuple-element.32), channel_id=1, source_target_pairs={{0,10},{2,8},{4,14},{6,12},{8,2},{10,0},{12,6},{14,4},{1,11},{3,9}... | collective-permute-start | bytes 884744 | tf_op jit(solution)/shard_map/ppermute | solution.py:276
  29.9 30.8 %collective-permute-start.9 = (bf16[2,256,256]{2,1,0:T(8,128)(2,1)S(1)}, bf16[2,256,256]{2,1,0:T(8,128)(2,1)S(1)}, u32[]{:S(2)}, u32[]{:S(2)}) collective-permute-start(bf16[2,256,256]{2,1,0:T(8,128)(2,1)S(1)} %pad_maximum_fusion.refs_0_), channel_id=1, source_target_pairs={{0,1},{1,0},{2,3},{3,2},{4,5},{5,4},{6,7},{7,6},{8,9},{9,8},{10,11... | collective-permute-start | bytes 786440 | tf_op jit(solution)/shard_map/ppermute | solution.py:22
  37.6 24.3 %collective-permute-start.12 = (bf16[256,768]{1,0:T(8,128)(2,1)S(1)}, bf16[256,768]{1,0:T(8,128)(2,1)S(1)}, u32[]{:S(2)}, u32[]{:S(2)}) collective-permute-start(bf16[256,768]{1,0:T(8,128)(2,1)S(1)} %get-tuple-element.41.refs_4_), channel_id=1, source_target_pairs={{0,16},{2,18},{4,20},{6,22},{8,24},{10,26},{12,28},{14,30},{16,0},... | collective-permute-start | bytes 1179656 | tf_op jit(solution)/shard_map/ppermute | solution.py:290
  53.0 10.5 %collective-permute-start.13 = (bf16[256,768]{1,0:T(8,128)(2,1)}, bf16[256,768]{1,0:T(8,128)(2,1)}, u32[]{:S(2)}, u32[]{:S(2)}) collective-permute-start(bf16[256,768]{1,0:T(8,128)(2,1)} %get-tuple-element.40), channel_id=1, source_target_pairs={{0,18},{2,16},{4,22},{6,20},{8,26},{10,24},{12,30},{14,28},{16,2},... | collective-permute-start | bytes 1179656 | tf_op jit(solution)/shard_map/ppermute | solution.py:290
  60.7 5.2 %collective-permute-start.8 = (bf16[2,256,256]{2,1,0:T(8,128)(2,1)S(1)}, bf16[2,256,256]{2,1,0:T(8,128)(2,1)}, u32[]{:S(2)}, u32[]{:S(2)}) collective-permute-start(bf16[2,256,256]{2,1,0:T(8,128)(2,1)S(1)} %pad_maximum_fusion.refs_0_), channel_id=1, source_target_pairs={{0,2},{2,0},{4,6},{6,4},{8,10},{10,8},{12,14},{14,12},{1,3},{3,1},... | collective-permute-start | bytes 786440 | tf_op jit(solution)/shard_map/ppermute | solution.py:22
  60.7 8.6 %collective-permute-start.10 = (bf16[2,256,256]{2,1,0:T(8,128)(2,1)S(1)}, bf16[2,256,256]{2,1,0:T(8,128)(2,1)}, u32[]{:S(2)}, u32[]{:S(2)}) collective-permute-start(bf16[2,256,256]{2,1,0:T(8,128)(2,1)S(1)} %collective-permute-done.9.refs_2_), channel_id=1, source_target_pairs={{0,2},{2,0},{4,6},{6,4},{8,10},{10,8},{12,14},{14,12},{1,3},{3,1},... | collective-permute-start | bytes 786440 | tf_op jit(solution)/shard_map/ppermute | solution.py:22
  62.7 12.0 %collective-permute-start.6 = (bf16[3,32,1536]{2,1,0:T(8,128)(2,1)}, bf16[3,32,1536]{2,1,0:T(8,128)(2,1)}, u32[]{:S(2)}, u32[]{:S(2)}) collective-permute-start(bf16[3,32,1536]{2,1,0:T(8,128)(2,1)} %get-tuple-element.31), channel_id=1, source_target_pairs={{0,2},{2,0},{4,6},{6,4},{8,10},{10,8},{12,14},{14,12},{1,3},{3,1},... | collective-permute-start | bytes 884744 | tf_op jit(solution)/shard_map/ppermute | solution.py:276
  62.7 8.5 %copy-start.9 = (bf16[2,256,256]{2,1,0:T(8,128)(2,1)S(1)}, bf16[2,256,256]{2,1,0:T(8,128)(2,1)}, u32[]{:S(2)}) copy-start(bf16[2,256,256]{2,1,0:T(8,128)(2,1)} %copy-done.8) | copy-start | bytes 786436
  62.7 8.5 %copy-start.18 = (bf16[256,768]{1,0:T(8,128)(2,1)S(1)}, bf16[256,768]{1,0:T(8,128)(2,1)}, u32[]{:S(2)}) copy-start(bf16[256,768]{1,0:T(8,128)(2,1)} %copy-done.17) | copy-start | bytes 1179652
  63.5 33.7 %collective-permute-start.19 = (bf16[256,768]{1,0:T(8,128)(2,1)}, bf16[256,768]{1,0:T(8,128)(2,1)}, u32[]{:S(2)}, u32[]{:S(2)}) collective-permute-start(bf16[256,768]{1,0:T(8,128)(2,1)} %get-tuple-element.42.refs_4_), channel_id=1, source_target_pairs={{0,16},{2,18},{4,20},{6,22},{8,24},{10,26},{12,28},{14,30},{16,0},... | collective-permute-start | bytes 1179656 | tf_op jit(solution)/shard_map/ppermute | solution.py:290
  65.1 32.1 %collective-permute-start.20 = (bf16[256,768]{1,0:T(8,128)(2,1)}, bf16[256,768]{1,0:T(8,128)(2,1)}, u32[]{:S(2)}, u32[]{:S(2)}) collective-permute-start(bf16[256,768]{1,0:T(8,128)(2,1)} %get-tuple-element.39), channel_id=1, source_target_pairs={{0,18},{2,16},{4,22},{6,20},{8,26},{10,24},{12,30},{14,28},{16,2},... | collective-permute-start | bytes 1179656 | tf_op jit(solution)/shard_map/ppermute | solution.py:290
  65.9 12.1 %collective-permute-start = (bf16[3,32,1536]{2,1,0:T(8,128)(2,1)}, bf16[3,32,1536]{2,1,0:T(8,128)(2,1)}, u32[]{:S(2)}, u32[]{:S(2)}) collective-permute-start(bf16[3,32,1536]{2,1,0:T(8,128)(2,1)} %get-tuple-element.16), channel_id=1, source_target_pairs={{0,12},{2,6},{4,8},{6,2},{8,4},{10,14},{12,0},{14,10},{1,13},{3,7}... | collective-permute-start | bytes 884744 | tf_op jit(solution)/shard_map/ppermute | solution.py:276
  69.2 14.4 %collective-permute-start.1 = (bf16[3,32,1536]{2,1,0:T(8,128)(2,1)}, bf16[3,32,1536]{2,1,0:T(8,128)(2,1)}, u32[]{:S(2)}, u32[]{:S(2)}) collective-permute-start(bf16[3,32,1536]{2,1,0:T(8,128)(2,1)} %get-tuple-element.17), channel_id=1, source_target_pairs={{0,4},{2,14},{4,0},{6,10},{8,12},{10,6},{12,8},{14,2},{1,5},{3,15}... | collective-permute-start | bytes 884744 | tf_op jit(solution)/shard_map/ppermute | solution.py:276
  73.8 0.9 copy-start.12
  74.7 29.3 %collective-permute-start.14 = (bf16[512,384]{1,0:T(8,128)(2,1)}, bf16[512,384]{1,0:T(8,128)(2,1)}, u32[]{:S(2)}, u32[]{:S(2)}) collective-permute-start(bf16[512,384]{1,0:T(8,128)(2,1)} %get-tuple-element.20), channel_id=1, source_target_pairs={{0,4},{2,6},{4,0},{6,2},{8,12},{10,14},{12,8},{14,10},{1,5},{3,7},... | collective-permute-start | bytes 1179656 | tf_op jit(solution)/shard_map/ppermute | solution.py:22
  83.7 1.0 copy-start.7
  84.6 1.0 copy-start.20
  85.6 1.0 copy-start.22
  92.5 0.9 copy-start.4
  93.4 72.5 %all-to-all-start = ((bf16[8,32,1536]{2,1,0:T(8,128)(2,1)}), bf16[8,32,1536]{2,1,0:T(8,128)(2,1)S(1)}, u32[]{:S(2)}, u32[]{:S(2)}) async-start(bf16[8,32,1536]{2,1,0:T(8,128)(2,1)} %copy-done.4), calls=%async_computation | async-start | bytes 1572864 | tf_op jit(solution)/shard_map/all_to_all | solution.py:333
  97.2 1.0 copy-start.6
  98.2 0.9 copy-start.10
  99.2 4.8 %copy-start.13 = (f32[512,384]{1,0:T(8,128)S(1)}, f32[512,384]{1,0:T(8,128)}, u32[]{:S(2)}) copy-start(f32[512,384]{1,0:T(8,128)} %copy-done.12) | copy-start | bytes 2359300
  101.9 24.8 %collective-permute-start.21 = (bf16[512,384]{1,0:T(8,128)(2,1)S(1)}, bf16[512,384]{1,0:T(8,128)(2,1)S(1)}, u32[]{:S(2)}, u32[]{:S(2)}) collective-permute-start(bf16[512,384]{1,0:T(8,128)(2,1)S(1)} %get-tuple-element.22), channel_id=1, source_target_pairs={{0,4},{2,6},{4,0},{6,2},{8,12},{10,14},{12,8},{14,10},{1,5},{3,7},... | collective-permute-start | bytes 1179656 | tf_op jit(solution)/shard_map/ppermute | solution.py:22
  106.1 46.3 %collective-permute-start.15 = (bf16[512,384]{1,0:T(8,128)(2,1)}, bf16[512,384]{1,0:T(8,128)(2,1)}, u32[]{:S(2)}, u32[]{:S(2)}) collective-permute-start(bf16[512,384]{1,0:T(8,128)(2,1)} %get-tuple-element.29), channel_id=1, source_target_pairs={{0,8},{2,10},{4,12},{6,14},{8,0},{10,2},{12,4},{14,6},{1,9},{3,11}... | collective-permute-start | bytes 1179656 | tf_op jit(solution)/shard_map/ppermute | solution.py:22
  126.7 4.7 %copy-start.24 = (s32[2]{0:T(128)S(1)}, s32[2]{0:T(128)}, u32[]{:S(2)}) copy-start(s32[2]{0:T(128)} %param.12) | copy-start | bytes 28
  127.9 27.7 %collective-permute-start.22 = (bf16[512,384]{1,0:T(8,128)(2,1)}, bf16[512,384]{1,0:T(8,128)(2,1)S(1)}, u32[]{:S(2)}, u32[]{:S(2)}) collective-permute-start(bf16[512,384]{1,0:T(8,128)(2,1)} %get-tuple-element.27), channel_id=1, source_target_pairs={{0,8},{2,10},{4,12},{6,14},{8,0},{10,2},{12,4},{14,6},{1,9},{3,11}... | collective-permute-start | bytes 1179656 | tf_op jit(solution)/shard_map/ppermute | solution.py:22
  127.9 24.5 %copy-start.3 = (f32[512,384]{1,0:T(8,128)S(1)}, f32[512,384]{1,0:T(8,128)}, u32[]{:S(2)}) copy-start(f32[512,384]{1,0:T(8,128)} %get-tuple-element.30.kept_ref) | copy-start | bytes 2359300
  129.2 3.4 %collective-permute-start.16 = (bf16[256,384]{1,0:T(8,128)(2,1)S(1)}, bf16[256,384]{1,0:T(8,128)(2,1)S(1)}, u32[]{:S(2)}, u32[]{:S(2)}) collective-permute-start(bf16[256,384]{1,0:T(8,128)(2,1)S(1)} %get-tuple-element.46), channel_id=1, source_target_pairs={{0,2},{2,0},{4,6},{6,4},{8,10},{10,8},{12,14},{14,12},{1,3},{3,1},... | collective-permute-start | bytes 589832 | tf_op jit(solution)/shard_map/ppermute | solution.py:22
  129.3 12.5 %collective-permute-start.17 = (bf16[256,384]{1,0:T(8,128)(2,1)S(1)}, bf16[256,384]{1,0:T(8,128)(2,1)S(1)}, u32[]{:S(2)}, u32[]{:S(2)}) collective-permute-start(bf16[256,384]{1,0:T(8,128)(2,1)S(1)} %get-tuple-element.48), channel_id=1, source_target_pairs={{0,4},{2,6},{4,0},{6,2},{8,12},{10,14},{12,8},{14,10},{1,5},{3,7},... | collective-permute-start | bytes 589832 | tf_op jit(solution)/shard_map/ppermute | solution.py:22
  131.4 21.0 %collective-permute-start.18 = (bf16[256,384]{1,0:T(8,128)(2,1)S(1)}, bf16[256,384]{1,0:T(8,128)(2,1)S(1)}, u32[]{:S(2)}, u32[]{:S(2)}) collective-permute-start(bf16[256,384]{1,0:T(8,128)(2,1)S(1)} %get-tuple-element.45), channel_id=1, source_target_pairs={{0,6},{2,4},{4,2},{6,0},{8,14},{10,12},{12,10},{14,8},{1,7},{3,5},... | collective-permute-start | bytes 589832 | tf_op jit(solution)/shard_map/ppermute | solution.py:22
  152.3 3.2 %copy-start.5 = (f32[512,384]{1,0:T(8,128)S(1)}, f32[512,384]{1,0:T(8,128)}, u32[]{:S(2)}) copy-start(f32[512,384]{1,0:T(8,128)} %get-tuple-element.28.kept_ref) | copy-start | bytes 2359300
  155.6 4.6 %copy-start.11 = (bf16[1,1,256,1536]{3,2,1,0:T(8,128)(2,1)S(1)}, bf16[1,1,256,1536]{3,2,1,0:T(8,128)(2,1)}, u32[]{:S(2)}) copy-start(bf16[1,1,256,1536]{3,2,1,0:T(8,128)(2,1)} %param.9) | copy-start | bytes 2359300
  158.0 8.1 %collective-permute-start.23 = (bf16[256,384]{1,0:T(8,128)(2,1)}, bf16[256,384]{1,0:T(8,128)(2,1)}, u32[]{:S(2)}, u32[]{:S(2)}) collective-permute-start(bf16[256,384]{1,0:T(8,128)(2,1)} %get-tuple-element.24), channel_id=1, source_target_pairs={{0,4},{2,6},{4,0},{6,2},{8,12},{10,14},{12,8},{14,10},{1,5},{3,7},... | collective-permute-start | bytes 589832 | tf_op jit(solution)/shard_map/ppermute | solution.py:22
  158.0 8.1 %collective-permute-start.24 = (bf16[256,384]{1,0:T(8,128)(2,1)}, bf16[256,384]{1,0:T(8,128)(2,1)}, u32[]{:S(2)}, u32[]{:S(2)}) collective-permute-start(bf16[256,384]{1,0:T(8,128)(2,1)} %get-tuple-element.25), channel_id=1, source_target_pairs={{0,2},{2,0},{4,6},{6,4},{8,10},{10,8},{12,14},{14,12},{1,3},{3,1},... | collective-permute-start | bytes 589832 | tf_op jit(solution)/shard_map/ppermute | solution.py:22
  158.2 10.5 %collective-permute-start.25 = (bf16[256,384]{1,0:T(8,128)(2,1)}, bf16[256,384]{1,0:T(8,128)(2,1)}, u32[]{:S(2)}, u32[]{:S(2)}) collective-permute-start(bf16[256,384]{1,0:T(8,128)(2,1)} %get-tuple-element.26), channel_id=1, source_target_pairs={{0,6},{2,4},{4,2},{6,0},{8,14},{10,12},{12,10},{14,8},{1,7},{3,5},... | collective-permute-start | bytes 589832 | tf_op jit(solution)/shard_map/ppermute | solution.py:22
  160.2 8.5 %copy-start.16 = (f32[256,384]{1,0:T(8,128)S(1)}, f32[256,384]{1,0:T(8,128)}, u32[]{:S(2)}) copy-start(f32[256,384]{1,0:T(8,128)} %copy-done.15) | copy-start | bytes 1179652
  164.7 1.2 copy-start.1
  168.7 1.4 copy-start.2
  (5 other events, 3.7 us)

commit v4 on v3

--- a/solution.py
+++ b/solution.py
@@ -15,6 +15,13 @@
 
 
 MODEST = pltpu.CompilerParams(vmem_limit_bytes=24 << 20)
+
+VMEM_SPEC = pl.BlockSpec(memory_space=pltpu.VMEM)
+SMEM_SPEC = pl.BlockSpec(memory_space=pltpu.SMEM)
+
+
+def on_chip(*values):
+    return [pltpu.with_memory_space_constraint(v, pltpu.VMEM) for v in values]
 
 
 def swap(value, axis, bits):
@@ -68,6 +75,30 @@
     )(side.reshape(1), states)
 
 
+def pick_kernel(assignment_ref, group_ref, parts_ref, *out_refs):
+    blocks, _, rows, _ = parts_ref.shape
+    for k, out_ref in enumerate(out_refs):
+        slot = assignment_ref[group_ref[0] ^ k]
+        for j in range(blocks):
+            out_ref[j * rows : (j + 1) * rows, :] = parts_ref[j, slot]
+
+
+def pick_slots(assignment, group, parts, n_grp):
+    blocks, _, rows, feats = parts.shape
+    if feats % HDIM:
+        slots = [lax.dynamic_index_in_dim(assignment, group ^ k, keepdims=False) for k in range(n_grp)]
+        cut = [lax.dynamic_index_in_dim(parts, slot, 1, keepdims=False) for slot in slots]
+        return [c.reshape(blocks * rows, feats) for c in cut]
+    return pl.pallas_call(
+        pick_kernel,
+        in_specs=[SMEM_SPEC, SMEM_SPEC, VMEM_SPEC],
+        out_specs=[VMEM_SPEC] * n_grp,
+        out_shape=[pltpu.VMEM((blocks * rows, feats), BF16)] * n_grp,
+        compiler_params=MODEST,
+        name="pick_slots",
+    )(assignment, group.reshape(1), *on_chip(parts))
+
+
 def project_kernel(n_rows, scalar_ref, *refs):
     near = scalar_ref[0]
     state_refs = refs[: 2 * n_rows]
@@ -90,14 +121,6 @@
         kept_ref[i * rows : (i + 1) * rows, :] = product(i, near * cols)
 
 
-VMEM_SPEC = pl.BlockSpec(memory_space=pltpu.VMEM)
-SMEM_SPEC = pl.BlockSpec(memory_space=pltpu.SMEM)
-
-
-def on_chip(*values):
-    return [pltpu.with_memory_space_constraint(v, pltpu.VMEM) for v in values]
-
-
 def project(states, weights, near):
     _, rows, _ = states[0].shape
     n_rows = len(states) // 2
@@ -106,10 +129,10 @@
         functools.partial(project_kernel, n_rows),
         in_specs=[SMEM_SPEC] + [VMEM_SPEC] * (len(states) + len(weights)),
         out_specs=[VMEM_SPEC] * 2,
-        out_shape=[pltpu.VMEM(shape, F32), pltpu.VMEM(shape, BF16)],
+        out_shape=[jax.ShapeDtypeStruct(shape, F32), pltpu.VMEM(shape, BF16)],
         compiler_params=MODEST,
         name="project",
-    )(near.reshape(1), *on_chip(*states, *weights))
+    )(near.reshape(1), *states, *weights[:2], *on_chip(*weights[2:]))
 
 
 def spatial_kernel(qkv_ref, residual_ref, out_ref):
@@ -131,7 +154,7 @@
             pl.BlockSpec((tokens, cols), lambda j: (0, j)),
         ],
         out_specs=pl.BlockSpec((tokens, cols), lambda j: (0, j)),
-        out_shape=jax.ShapeDtypeStruct((tokens, width), F32),
+        out_shape=pltpu.HBM((tokens, width), F32),
         compiler_params=MODEST,
         name="spatial",
     )(qkv, residual)
@@ -192,7 +215,7 @@
         out_shape=pltpu.VMEM((width // HDIM, len(queries), tokens, rows), BF16),
         compiler_params=MODEST,
         name="cross_weights",
-    )(*on_chip(bias, kept, come, *queries))
+    )(bias, kept, *on_chip(come), *queries)
 
 
 def value_kernel(weight_ref, kept_ref, come_ref, *out_refs):
@@ -211,30 +234,38 @@
         value_kernel,
         in_specs=[VMEM_SPEC] * 3,
         out_specs=[VMEM_SPEC] * count,
-        out_shape=[pltpu.VMEM((tokens, width), F32 if j == 0 else BF16) for j in range(count)],
+        out_shape=[pltpu.VMEM((tokens, width), F32)]
+        + [pltpu.VMEM((tokens, width), BF16)] * (count - 1),
         compiler_params=MODEST,
         name="cross_values",
-    )(*on_chip(weights, kept, come))
-
-
-def final_kernel(scalar_ref, base_ref, temporal_ref, *refs):
+    )(*on_chip(weights), kept, *on_chip(come))
+
+
+def gather_kernel(scalar_ref, base_ref, *refs):
     piece_refs, out_ref = refs[:-1], refs[-1]
-    cols = piece_refs[0].shape[1]
     for j, piece_ref in enumerate(piece_refs):
-        at = pl.ds(pl.multiple_of((scalar_ref[0] ^ j) * cols, HDIM), cols)
-        total = base_ref[:, at] + temporal_ref[:, at].astype(F32)
-        out_ref[:, at] = (total + piece_ref[...].astype(F32)).astype(BF16)
-
-
-def final_sum(place, base, temporal, pieces):
-    return pl.pallas_call(
-        final_kernel,
-        in_specs=[SMEM_SPEC] + [VMEM_SPEC] * (2 + len(pieces)),
-        out_specs=VMEM_SPEC,
-        out_shape=jax.ShapeDtypeStruct(base.shape, BF16),
-        compiler_params=MODEST,
-        name="final",
-    )(place.reshape(1), *on_chip(base, temporal, *pieces))
+
+        @pl.when(pl.program_id(0) == j)
+        def _(piece_ref=piece_ref):
+            out_ref[...] = base_ref[...] + piece_ref[...].astype(F32)
+
+
+def gather_results(place, base, pieces):
+    tokens, width = base.shape
+    cols = width // len(pieces)
+    side = pl.BlockSpec((tokens, cols), lambda j, s: (0, j ^ s[0]))
+    return pl.pallas_call(
+        gather_kernel,
+        grid_spec=pltpu.PrefetchScalarGridSpec(
+            num_scalar_prefetch=1,
+            grid=(len(pieces),),
+            in_specs=[side] + [VMEM_SPEC] * len(pieces),
+            out_specs=side,
+        ),
+        out_shape=jax.ShapeDtypeStruct(base.shape, F32),
+        compiler_params=MODEST,
+        name="gather_results",
+    )(place.reshape(1), base, *on_chip(*pieces))
 
 
 def temporal_plan(seq):
@@ -277,23 +308,25 @@
 
     half = width // 2
     planes = lax.optimization_barrier(kv_weight.transpose(1, 0, 2))
-    mine = lax.dynamic_slice_in_dim(planes, core * half, half, 2)
-    theirs = lax.dynamic_slice_in_dim(planes, (1 - core) * half, half, 2)
-    come = swap(theirs, "seq", 1)
-    across = [(g, s) for g in range(grp) for s in range(seq)]
-    weights = []
+    across = [(g, q) for g in range(grp) for q in range(seq)]
+
+    def halves(source, kind):
+        cut = (lax.dynamic_slice(source, (kind, 0, c * half), (1, feats, half)) for c in (core, 1 - core))
+        return tuple(c.reshape(feats, half) for c in cut)
+
+    keys = halves(planes, 0)
+    later, keys = lax.optimization_barrier((planes, keys))
+    weights = [keys, halves(later, 1)]
     for kind in range(2):
-        weights.append([mine[kind], come[kind]])
+        mine, theirs = weights[kind]
+        weights[kind] = [mine, swap(theirs, "seq", 1)]
         for k in range(1, grp):
-            for c, part in enumerate((mine[kind], theirs[kind])):
-                pairs = [(g * seq + s, (g ^ k) * seq + (s ^ c)) for g, s in across]
+            for c, part in enumerate((mine, theirs)):
+                pairs = [(g * seq + q, (g ^ k) * seq + (q ^ c)) for g, q in across]
                 weights[kind].append(lax.ppermute(part, ("grp", "seq"), pairs))
 
-    def slot(k):
-        index = lax.dynamic_index_in_dim(assignment, group ^ k, keepdims=False)
-        return lax.dynamic_index_in_dim(parts, index, 1, keepdims=False).reshape(rows, feats)
-
-    wanted = jnp.stack([slot(0)] + [swap(slot(k), "grp", k) for k in range(1, grp)])
+    slots = pick_slots(assignment, group, parts, grp)
+    wanted = jnp.stack([slots[0]] + [swap(slots[k], "grp", k) for k in range(1, grp)])
     states = []
     for k in range(sides):
         if k:
@@ -338,7 +371,8 @@
     for k in range(1, 4):
         results.append(swap(crossed[k], "seq", k))
     results[1], results[2] = results[2], results[1]
-    return final_sum(place, base, temporal, results)[None, None]
+    total = gather_results(place, base, results)
+    return (total + temporal.astype(F32)).astype(BF16)[None, None]
 
 
 def solution(mesh):

time: 174 us -> 169 us (0.971)
  waiting for transfers between devices: 72.9 us -> 68 us
  between operations: 4.12 us -> 2.05 us
  other arithmetic: 3.92 us -> 5.81 us
    ppermute x15 -> x16, waiting for transfers between devices: 41.1 us -> 34.6 us  [swap(): return lax.ppermute(value, axis, pairs)]
    unnamed x51 -> x61, local copies, waits for them, and re-layouts: 16.7 us -> 21.1 us
    squeeze x2 -> x0, local copies, waits for them, and re-layouts: 4.31 us -> none  [the longest x1 2.4 us: block(): theirs[kind]]
    ppermute x4, waiting for transfers between devices: 0.8 us -> 4.67 us  [block(): weights[kind].append(lax.ppermute(part, ('grp', 'seq'), pairs))]
    ppermute x7, waiting for transfers between devices: 31 us -> 28.7 us  [block(): pieces.append(lax.ppermute(blocks[number], 'seq', pairs))]
    broadcast_in_dim x0 -> x1, other arithmetic: none -> 2.19 us  [block(): return (total + temporal.astype(F32)).astype(BF16)[None, None]]
    dynamic_slice x3 -> x1, local copies, waits for them, and re-layouts: 2.74 us -> 0.64 us  [block(): served = lax.dynamic_index_in_dim(assignment, group, keepdims=False)]
    reshape x0 -> x2, local copies, waits for them, and re-layouts: none -> 1.99 us  [halves(): return tuple((c.reshape(feats, half) for c in cut))]
  transfers between devices with their start and end apart: 28 -> 29, of which waited for: 12 -> 10; matrix products, arithmetic and copies ran while one was open for 11% -> 9% of each run, Pallas kernels for 12% -> 13%
where the time goes in v4:
time: 169 us; the launch traced here: 168 us
  waiting for transfers between devices  68 us (40%)
  starting transfers between devices  39.2 us (23%)
  local copies, waits for them, and re-layouts  29.8 us (18%)
  Pallas kernels  23.2 us (14%)
  other arithmetic  5.81 us (3%)
  between operations  2.05 us (1%)
    ppermute x16, waiting for transfers between devices, swap(): return lax.ppermute(value, axis, pairs)  34.6 us
    ppermute x7, waiting for transfers between devices, block(): pieces.append(lax.ppermute(blocks[number], 'seq', pairs))  28.7 us
    unnamed x61, local copies, waits for them, and re-layouts  21.1 us
    ppermute x16, starting transfers between devices, swap(): return lax.ppermute(value, axis, pairs)  16.3 us
    ppermute x7, starting transfers between devices, block(): pieces.append(lax.ppermute(blocks[number], 'seq', pairs))  7.83 us
    pallas_call x1, Pallas kernels, temporal_attention(): pl.pallas_call(functools.partial(temporal_kernel, frames), grid_spec=pltp...  6.52 us
    all_to_all x1, starting transfers between devices, block(): parts = lax.all_to_all(parts, 'seq', 0, 0, tiled=True)  6.49 us
    pallas_call x1, Pallas kernels, spatial_attention(): pl.pallas_call(spatial_kernel, grid=(width // cols,), in_specs=[pl.BlockS...  5.24 us
  transfers between devices with their start and end apart: 29, of which 10 were waited for; matrix products, arithmetic and copies ran while one was open for 9% of the time, Pallas kernels for 13%

profile of v4, /device:TPU:0, one launch (start us, length us, event | category | flops | bytes accessed | tf_op | source)
XLA Modules:
  0.0 168.0 jit_solution(16633990729004827870)
XLA Ops:
  0.0 1.0 copy-done.16
  1.8 6.5 %all-to-all-start = ((bf16[8,2,32,256]{3,2,1,0:T(8,128)(2,1)}), bf16[8,2,32,256]{3,2,1,0:T(8,128)(2,1)S(1)}, u32[]{:S(2)}, u32[]{:S(2)}) async-start(bf16[8,2,32,256]{3,2,1,0:T(8,128)(2,1)} %prompt_blocks.1), calls=%async_computation | async-start | bytes 524288 | tf_op jit(solution)/shard_map/all_to_all | solution.py:289
  8.3 2.1 %dynamic-slice_bitcast_fusion.4 = (bf16[3,32,1536]{2,1,0:T(8,128)(2,1)}, bf16[3,32,1536]{2,1,0:T(8,128)(2,1)}, bf16[3,32,1536]{2,1,0:T(8,128)(2,1)}) fusion(bf16[1,1,256,3,1536]{4,2,3,1,0:T(8,128)(2,1)} %param.7, s32[]{:T(128)S(6)} %select_n.155, s32[]{:T(128)S(6)} %select_n.153, s32[]{:T(128)S(6)} %select_n.154), kind=kLoop, calls=%fused_computation.10 | loop fusion | bytes 1769484 | tf_op jit(solution)/shard_map/dynamic_slice | solution.py:301
  10.4 1.1 constant_dynamic-slice_fusion
  11.5 3.5 %collective-permute-start.22 = (bf16[3,32,1536]{2,1,0:T(8,128)(2,1)}, bf16[3,32,1536]{2,1,0:T(8,128)(2,1)S(1)}, u32[]{:S(2)}, u32[]{:S(2)}) collective-permute-start(bf16[3,32,1536]{2,1,0:T(8,128)(2,1)} %get-tuple-element.45), channel_id=1, source_target_pairs={{0,14},{2,4},{4,10},{6,0},{8,6},{10,12},{12,2},{14,8},{1,15},{3,5}... | collective-permute-start | bytes 884744 | tf_op jit(solution)/shard_map/ppermute | solution.py:307
  15.0 1.1 collective-permute-start.24
  16.2 1.6 collective-permute-start.25
  17.8 2.8 %copy.10 = bf16[256,2,1536]{2,0,1:T(8,128)(2,1)} copy(bf16[256,2,1536]{2,1,0:T(2,128)(2,1)} %param.11) | data formatting | bytes 3145728 | tf_op args[4]
  21.1 1.6 collective-permute-start
  22.7 1.2 dynamic-slice_bitcast_fusion.2
  23.9 3.6 %collective-permute-done.22.refs_3_ = bf16[3,32,1536]{2,1,0:T(8,128)(2,1)S(1)} collective-permute-done((bf16[3,32,1536]{2,1,0:T(8,128)(2,1)}, bf16[3,32,1536]{2,1,0:T(8,128)(2,1)S(1)}, u32[]{:S(2)}, u32[]{:S(2)}) %collective-permute-start.22) | collective-permute-done | bytes 294944 | tf_op jit(solution)/shard_map/ppermute | solution.py:307
  27.5 2.3 %collective-permute-done.23.refs_4_ = bf16[3,32,1536]{2,1,0:T(8,128)(2,1)} collective-permute-done((bf16[3,32,1536]{2,1,0:T(8,128)(2,1)}, bf16[3,32,1536]{2,1,0:T(8,128)(2,1)}, u32[]{:S(2)}, u32[]{:S(2)}) %collective-permute-start.23) | collective-permute-done | bytes 294944 | tf_op jit(solution)/shard_map/ppermute | solution.py:307
  29.8 1.5 collective-permute-start.5
  31.3 18.7 %collective-permute-done.24.refs_5_ = bf16[3,32,1536]{2,1,0:T(8,128)(2,1)} collective-permute-done((bf16[3,32,1536]{2,1,0:T(8,128)(2,1)}, bf16[3,32,1536]{2,1,0:T(8,128)(2,1)}, u32[]{:S(2)}, u32[]{:S(2)}) %collective-permute-start.24) | collective-permute-done | bytes 294944 | tf_op jit(solution)/shard_map/ppermute | solution.py:307
  50.0 1.5 collective-permute-start.2
  51.6 4.1 %collective-permute-done.25.refs_6_ = bf16[3,32,1536]{2,1,0:T(8,128)(2,1)} collective-permute-done((bf16[3,32,1536]{2,1,0:T(8,128)(2,1)}, bf16[3,32,1536]{2,1,0:T(8,128)(2,1)}, u32[]{:S(2)}, u32[]{:S(2)}) %collective-permute-start.25) | collective-permute-done | bytes 294944 | tf_op jit(solution)/shard_map/ppermute | solution.py:307
  55.6 1.3 collective-permute-start.6
  58.9 1.5 collective-permute-start.20
  62.0 4.7 %collective-permute-done.6.refs_7_ = bf16[256,768]{1,0:T(8,128)(2,1)S(1)} collective-permute-done((bf16[256,768]{1,0:T(8,128)(2,1)S(1)}, bf16[256,768]{1,0:T(8,128)(2,1)S(1)}, u32[]{:S(2)}, u32[]{:S(2)}) %collective-permute-start.6) | collective-permute-done | bytes 393248 | tf_op jit(solution)/shard_map/ppermute | solution.py:326
  68.7 1.5 collective-permute-start.13
  73.8 1.0 copy-done.18
  74.8 1.0 copy-done.20
  75.8 1.0 copy-done.22
  76.8 1.6 project.2
  79.3 1.0 copy-done.3
  80.3 1.0 copy-done.24
  81.3 1.0 copy-done.26
  82.2 6.5 %temporal.1 = bf16[8,32,1536]{2,1,0:T(8,128)(2,1)} custom-call(s32[8]{0:T(128)S(1)} %stack.47.scalar_ref, bf16[3,32,1536]{2,1,0:T(8,128)(2,1)S(1)} %copy-done.3, bf16[3,32,1536]{2,1,0:T(8,128)(2,1)} %collective-permute-done.20.refs_1_, bf16[3,32,1536]{2,1,0:T(8,128)(2,1)} %collective-permute-done.21.refs_2_, bf16[3,32,1536]{2,1,0:T(8,128)(2,1)S(1)} %copy-done.24, ...), custom_call_target="tpu_custom_call" | custom-call | tf_op jit(solution)/shard_map/temporal/pallas_call | solution.py:185
  88.7 4.3 %all-to-all-start.1 = ((bf16[8,32,1536]{2,1,0:T(8,128)(2,1)}), bf16[8,32,1536]{2,1,0:T(8,128)(2,1)}, u32[]{:S(2)}, u32[]{:S(2)}) async-start(bf16[8,32,1536]{2,1,0:T(8,128)(2,1)} %temporal.1), calls=%async_computation.1 | async-start | bytes 1572864 | tf_op jit(solution)/shard_map/all_to_all | solution.py:366
  95.0 2.6 %project.3 = (f32[512,384]{1,0:T(8,128)S(1)}, bf16[512,384]{1,0:T(8,128)(2,1)S(1)}) custom-call(s32[1]{0:T(128)} %bitcast.6.scalar_ref, bf16[2,256,256]{2,1,0:T(8,128)(2,1)S(1)} %pad_maximum_fusion.refs_0_, bf16[2,256,256]{2,1,0:T(8,128)(2,1)S(1)} %copy-done.9, bf16[2,256,256]{2,1,0:T(8,128)(2,1)S(1)} %copy-done.6, bf16[2,256,256]{2,1,0:T(8,128)(2,1)S(1)} %copy-done.12, ...), custom_call_target="tpu_custom_call" | custom-call | tf_op jit(solution)/shard_map/project/pallas_call | solution.py:128
  97.6 2.0 %collective-permute-start.15 = (bf16[512,384]{1,0:T(8,128)(2,1)S(1)}, bf16[512,384]{1,0:T(8,128)(2,1)S(1)}, u32[]{:S(2)}, u32[]{:S(2)}) collective-permute-start(bf16[512,384]{1,0:T(8,128)(2,1)S(1)} %get-tuple-element.29), channel_id=1, source_target_pairs={{0,4},{2,6},{4,0},{6,2},{8,12},{10,14},{12,8},{14,10},{1,5},{3,7},... | collective-permute-start | bytes 1179656 | tf_op jit(solution)/shard_map/ppermute | solution.py:29
  99.6 1.8 %fusion.7 = (bf16[512,384]{1,0:T(8,128)(2,1)}, f32[512,384]{1,0:T(8,128)S(1)}) fusion(f32[512,384]{1,0:T(8,128)S(1)} %copy-done.15, bf16[512,384]{1,0:T(8,128)(2,1)} %collective-permute-done.7), kind=kLoop, calls=%fused_computation.38 | loop fusion | flops 589824 | bytes 2359296 | tf_op jit(solution)/shard_map/convert_element_type | solution.py:351
  101.5 2.3 %collective-permute-start.8 = (bf16[512,384]{1,0:T(8,128)(2,1)}, bf16[512,384]{1,0:T(8,128)(2,1)}, u32[]{:S(2)}, u32[]{:S(2)}) collective-permute-start(bf16[512,384]{1,0:T(8,128)(2,1)} %get-tuple-element.39), channel_id=1, source_target_pairs={{0,8},{2,10},{4,12},{6,14},{8,0},{10,2},{12,4},{14,6},{1,9},{3,11}... | collective-permute-start | bytes 1179656 | tf_op jit(solution)/shard_map/ppermute | solution.py:29
  103.8 19.0 %collective-permute-done.15 = bf16[512,384]{1,0:T(8,128)(2,1)S(1)} collective-permute-done((bf16[512,384]{1,0:T(8,128)(2,1)S(1)}, bf16[512,384]{1,0:T(8,128)(2,1)S(1)}, u32[]{:S(2)}, u32[]{:S(2)}) %collective-permute-start.15) | collective-permute-done | bytes 393248 | tf_op jit(solution)/shard_map/ppermute | solution.py:29
  122.8 1.1 fusion.6
  123.9 2.1 %dynamic-slice_bitcast_fusion.7 = (bf16[256,384]{1,0:T(8,128)(2,1)}, bf16[256,384]{1,0:T(8,128)(2,1)}, bf16[256,384]{1,0:T(8,128)(2,1)S(1)}, bf16[256,384]{1,0:T(8,128)(2,1)}) fusion(bf16[1,1,256,1536]{3,2,1,0:T(8,128)(2,1)} %param.8, s32[]{:T(128)S(6)} %select_n.148, s32[]{:T(128)S(6)} %select_n.146, s32[]{:T(128)S(6)} %select_n.145, s32[]{:T(128)S(6)} %select_n.147), kind=kLoop, calls=%fused_computation.14 | loop fusion | bytes 1572880 | tf_op jit(solution)/shard_map/dynamic_slice | solution.py:342
  126.0 1.7 %collective-permute-start.10 = (bf16[256,384]{1,0:T(8,128)(2,1)}, bf16[256,384]{1,0:T(8,128)(2,1)S(1)}, u32[]{:S(2)}, u32[]{:S(2)}) collective-permute-start(bf16[256,384]{1,0:T(8,128)(2,1)} %get-tuple-element.56), channel_id=1, source_target_pairs={{0,4},{2,6},{4,0},{6,2},{8,12},{10,14},{12,8},{14,10},{1,5},{3,7},... | collective-permute-start | bytes 589832 | tf_op jit(solution)/shard_map/ppermute | solution.py:29
  131.9 6.1 %collective-permute-done.10.refs_2_ = bf16[256,384]{1,0:T(8,128)(2,1)S(1)} collective-permute-done((bf16[256,384]{1,0:T(8,128)(2,1)}, bf16[256,384]{1,0:T(8,128)(2,1)S(1)}, u32[]{:S(2)}, u32[]{:S(2)}) %collective-permute-start.10) | collective-permute-done | bytes 196640 | tf_op jit(solution)/shard_map/ppermute | solution.py:29
  138.0 3.4 %collective-permute-done.11.refs_3_ = bf16[256,384]{1,0:T(8,128)(2,1)} collective-permute-done((bf16[256,384]{1,0:T(8,128)(2,1)}, bf16[256,384]{1,0:T(8,128)(2,1)}, u32[]{:S(2)}, u32[]{:S(2)}) %collective-permute-start.11) | collective-permute-done | bytes 196640 | tf_op jit(solution)/shard_map/ppermute | solution.py:29
  141.4 3.4 %cross_weights.1.weight_ref = bf16[3,4,256,512]{3,2,1,0:T(8,128)(2,1)S(1)} custom-call(f32[1,512]{1,0:T(1,128)S(1)} %compare_select_fusion.bias_ref, f32[512,384]{1,0:T(8,128)S(1)} %get-tuple-element.40.kept_ref, bf16[512,384]{1,0:T(8,128)(2,1)} %collective-permute-done.8.come_ref, bf16[256,384]{1,0:T(8,128)(2,1)S(1)} %get-tuple-element.55.refs_0_, ...), custom_call_target="tpu_custom_call" | custom-call | tf_op jit(solution)/shard_map/cross_weights/pallas_call | solution.py:211
  144.8 3.0 %collective-permute-done.16.come_ref = bf16[512,384]{1,0:T(8,128)(2,1)} collective-permute-done((bf16[512,384]{1,0:T(8,128)(2,1)}, bf16[512,384]{1,0:T(8,128)(2,1)}, u32[]{:S(2)}, u32[]{:S(2)}) %collective-permute-start.16) | collective-permute-done | bytes 393248 | tf_op jit(solution)/shard_map/ppermute | solution.py:29
  147.9 2.0 %cross_values.1 = (f32[256,384]{1,0:T(8,128)S(1)}, bf16[256,384]{1,0:T(8,128)(2,1)S(1)}, bf16[256,384]{1,0:T(8,128)(2,1)S(1)}, bf16[256,384]{1,0:T(8,128)(2,1)S(1)}) custom-call(bf16[3,4,256,512]{3,2,1,0:T(8,128)(2,1)S(1)} %cross_weights.1.weight_ref, f32[512,384]{1,0:T(8,128)S(1)} %copy-done.2, bf16[512,384]{1,0:T(8,128)(2,1)} %collective-permute-done.16.come_ref), custom_call_target="tpu_custom_call" | custom-call | tf_op jit(solution)/shard_map/cross_values/pallas_call | solution.py:233
  149.9 4.0 %collective-permute-start.17 = (bf16[256,384]{1,0:T(8,128)(2,1)S(1)}, bf16[256,384]{1,0:T(8,128)(2,1)S(1)}, u32[]{:S(2)}, u32[]{:S(2)}) collective-permute-start(bf16[256,384]{1,0:T(8,128)(2,1)S(1)} %get-tuple-element.31), channel_id=1, source_target_pairs={{0,4},{2,6},{4,0},{6,2},{8,12},{10,14},{12,8},{14,10},{1,5},{3,7},... | collective-permute-start | bytes 589832 | tf_op jit(solution)/shard_map/ppermute | solution.py:29
  154.3 1.3 collective-permute-start.19
  155.6 5.2 %spatial.1.base_ref = f32[256,1536]{1,0:T(8,128)} custom-call(bf16[3,256,1536]{2,1,0:T(8,128)(2,1)S(1)} %bitcast.57, bf16[256,1536]{1,0:T(8,128)(2,1)S(1)} %bitcast.58), custom_call_target="tpu_custom_call" | custom-call | tf_op jit(solution)/shard_map/spatial/pallas_call | solution.py:149
  160.8 3.1 %collective-permute-done.19.refs_3_ = bf16[256,384]{1,0:T(8,128)(2,1)S(1)} collective-permute-done((bf16[256,384]{1,0:T(8,128)(2,1)S(1)}, bf16[256,384]{1,0:T(8,128)(2,1)S(1)}, u32[]{:S(2)}, u32[]{:S(2)}) %collective-permute-start.19) | collective-permute-done | bytes 196640 | tf_op jit(solution)/shard_map/ppermute | solution.py:29
  163.9 1.4 copy-done.1
  165.8 2.2 %fusion.1 = bf16[1,1,256,1536]{3,2,1,0:T(8,128)(2,1)} fusion(f32[256,1536]{1,0:T(8,128)S(1)} %gather_results.1, bf16[8,32,1536]{2,1,0:T(8,128)(2,1)} %all-to-all-done.1), kind=kLoop, calls=%fused_computation.3 | loop fusion | flops 1179648 | bytes 3145728 | tf_op jit(solution)/shard_map/broadcast_in_dim | solution.py:375
  (93 shorter events, 16.7 us)
Async XLA Ops:
  0.0 1.0 copy-start.16
  1.0 9.3 %copy-start = (bf16[1,1,256,3,1536]{4,2,3,1,0:T(8,128)(2,1)S(1)}, bf16[1,1,256,3,1536]{4,2,3,1,0:T(8,128)(2,1)}, u32[]{:S(2)}) copy-start(bf16[1,1,256,3,1536]{4,2,3,1,0:T(8,128)(2,1)} %param.7) | copy-start | bytes 7077892
  1.8 18.8 %all-to-all-start = ((bf16[8,2,32,256]{3,2,1,0:T(8,128)(2,1)}), bf16[8,2,32,256]{3,2,1,0:T(8,128)(2,1)S(1)}, u32[]{:S(2)}, u32[]{:S(2)}) async-start(bf16[8,2,32,256]{3,2,1,0:T(8,128)(2,1)} %prompt_blocks.1), calls=%async_computation | async-start | bytes 524288 | tf_op jit(solution)/shard_map/all_to_all | solution.py:289
  11.5 16.0 %collective-permute-start.22 = (bf16[3,32,1536]{2,1,0:T(8,128)(2,1)}, bf16[3,32,1536]{2,1,0:T(8,128)(2,1)S(1)}, u32[]{:S(2)}, u32[]{:S(2)}) collective-permute-start(bf16[3,32,1536]{2,1,0:T(8,128)(2,1)} %get-tuple-element.45), channel_id=1, source_target_pairs={{0,14},{2,4},{4,10},{6,0},{8,6},{10,12},{12,2},{14,8},{1,15},{3,5}... | collective-permute-start | bytes 884744 | tf_op jit(solution)/shard_map/ppermute | solution.py:307
  15.0 14.8 %collective-permute-start.23 = (bf16[3,32,1536]{2,1,0:T(8,128)(2,1)}, bf16[3,32,1536]{2,1,0:T(8,128)(2,1)}, u32[]{:S(2)}, u32[]{:S(2)}) collective-permute-start(bf16[3,32,1536]{2,1,0:T(8,128)(2,1)} %get-tuple-element.44), channel_id=1, source_target_pairs={{0,6},{2,12},{4,2},{6,8},{8,14},{10,4},{12,10},{14,0},{1,7},{3,13}... | collective-permute-start | bytes 884744 | tf_op jit(solution)/shard_map/ppermute | solution.py:307
  15.0 35.0 %collective-permute-start.24 = (bf16[3,32,1536]{2,1,0:T(8,128)(2,1)}, bf16[3,32,1536]{2,1,0:T(8,128)(2,1)}, u32[]{:S(2)}, u32[]{:S(2)}) collective-permute-start(bf16[3,32,1536]{2,1,0:T(8,128)(2,1)} %get-tuple-element.43), channel_id=1, source_target_pairs={{0,8},{2,10},{4,12},{6,14},{8,0},{10,2},{12,4},{14,6},{1,9},{3,11}... | collective-permute-start | bytes 884744 | tf_op jit(solution)/shard_map/ppermute | solution.py:307
  16.2 39.5 %collective-permute-start.25 = (bf16[3,32,1536]{2,1,0:T(8,128)(2,1)}, bf16[3,32,1536]{2,1,0:T(8,128)(2,1)}, u32[]{:S(2)}, u32[]{:S(2)}) collective-permute-start(bf16[3,32,1536]{2,1,0:T(8,128)(2,1)} %get-tuple-element.42), channel_id=1, source_target_pairs={{0,10},{2,8},{4,14},{6,12},{8,2},{10,0},{12,6},{14,4},{1,11},{3,9}... | collective-permute-start | bytes 884744 | tf_op jit(solution)/shard_map/ppermute | solution.py:307
  17.8 2.8 %copy-start.27 = (s32[2]{0:T(128)S(1)}, s32[2]{0:T(128)}, u32[]{:S(2)}) copy-start(s32[2]{0:T(128)} %assignment_ref.1) | copy-start | bytes 28
  20.6 40.6 %copy-start.28 = (bf16[256,2,1536]{2,0,1:T(8,128)(2,1)S(1)}, bf16[256,2,1536]{2,0,1:T(8,128)(2,1)}, u32[]{:S(2)}) copy-start(bf16[256,2,1536]{2,0,1:T(8,128)(2,1)} %copy.10) | copy-start | bytes 4718596
  21.1 8.7 %collective-permute-start = (bf16[256,256]{1,0:T(8,128)(2,1)S(1)}, bf16[256,256]{1,0:T(8,128)(2,1)S(1)}, u32[]{:S(2)}, u32[]{:S(2)}) collective-permute-start(bf16[256,256]{1,0:T(8,128)(2,1)S(1)} %get-tuple-element.22), channel_id=1, source_target_pairs={{0,16},{16,0},{1,17},{17,1},{2,18},{18,2},{3,19},{19,3},{4,20},{20... | collective-permute-start | bytes 393224 | tf_op jit(solution)/shard_map/ppermute | solution.py:29
  27.5 32.9 %copy-start.23 = (bf16[3,32,1536]{2,1,0:T(8,128)(2,1)}, bf16[3,32,1536]{2,1,0:T(8,128)(2,1)S(1)}, u32[]{:S(2)}) copy-start(bf16[3,32,1536]{2,1,0:T(8,128)(2,1)S(1)} %collective-permute-done.22.refs_3_) | copy-start | bytes 884740
  27.5 29.4 %collective-permute-start.26 = (bf16[3,32,1536]{2,1,0:T(8,128)(2,1)}, bf16[3,32,1536]{2,1,0:T(8,128)(2,1)S(1)}, u32[]{:S(2)}, u32[]{:S(2)}) collective-permute-start(bf16[3,32,1536]{2,1,0:T(8,128)(2,1)} %get-tuple-element.41), channel_id=1, source_target_pairs={{0,2},{2,0},{4,6},{6,4},{8,10},{10,8},{12,14},{14,12},{1,3},{3,1},... | collective-permute-start | bytes 884744 | tf_op jit(solution)/shard_map/ppermute | solution.py:307
  29.8 28.3 %collective-permute-start.4 = (bf16[256,768]{1,0:T(8,128)(2,1)S(1)}, bf16[256,768]{1,0:T(8,128)(2,1)S(1)}, u32[]{:S(2)}, u32[]{:S(2)}) collective-permute-start(bf16[256,768]{1,0:T(8,128)(2,1)S(1)} %get-tuple-element.24), channel_id=1, source_target_pairs={{0,2},{2,0},{4,6},{6,4},{8,10},{10,8},{12,14},{14,12},{1,3},{3,1},... | collective-permute-start | bytes 1179656 | tf_op jit(solution)/shard_map/ppermute | solution.py:29
  29.8 30.6 %collective-permute-start.5 = (bf16[256,768]{1,0:T(8,128)(2,1)S(1)}, bf16[256,768]{1,0:T(8,128)(2,1)S(1)}, u32[]{:S(2)}, u32[]{:S(2)}) collective-permute-start(bf16[256,768]{1,0:T(8,128)(2,1)S(1)} %get-tuple-element.23.refs_4_), channel_id=1, source_target_pairs={{0,16},{2,18},{4,20},{6,22},{8,24},{10,26},{12,28},{14,30},{16,0},... | collective-permute-start | bytes 1179656 | tf_op jit(solution)/shard_map/ppermute | solution.py:326
  50.0 7.9 %collective-permute-start.2 = (bf16[2,256,256]{2,1,0:T(8,128)(2,1)S(1)}, bf16[2,256,256]{2,1,0:T(8,128)(2,1)S(1)}, u32[]{:S(2)}, u32[]{:S(2)}) collective-permute-start(bf16[2,256,256]{2,1,0:T(8,128)(2,1)S(1)} %pad_maximum_fusion.refs_0_), channel_id=1, source_target_pairs={{0,1},{1,0},{2,3},{3,2},{4,5},{5,4},{6,7},{7,6},{8,9},{9,8},{10,11... | collective-permute-start | bytes 786440 | tf_op jit(solution)/shard_map/ppermute | solution.py:29
  55.6 11.0 %collective-permute-start.6 = (bf16[256,768]{1,0:T(8,128)(2,1)S(1)}, bf16[256,768]{1,0:T(8,128)(2,1)S(1)}, u32[]{:S(2)}, u32[]{:S(2)}) collective-permute-start(bf16[256,768]{1,0:T(8,128)(2,1)S(1)} %get-tuple-element.24), channel_id=1, source_target_pairs={{0,18},{2,16},{4,22},{6,20},{8,26},{10,24},{12,30},{14,28},{16,2},... | collective-permute-start | bytes 1179656 | tf_op jit(solution)/shard_map/ppermute | solution.py:326
  57.6 10.4 %collective-permute-start.1 = (bf16[2,256,256]{2,1,0:T(8,128)(2,1)S(1)}, bf16[2,256,256]{2,1,0:T(8,128)(2,1)S(1)}, u32[]{:S(2)}, u32[]{:S(2)}) collective-permute-start(bf16[2,256,256]{2,1,0:T(8,128)(2,1)S(1)} %pad_maximum_fusion.refs_0_), channel_id=1, source_target_pairs={{0,2},{2,0},{4,6},{6,4},{8,10},{10,8},{12,14},{14,12},{1,3},{3,1},... | collective-permute-start | bytes 786440 | tf_op jit(solution)/shard_map/ppermute | solution.py:29
  58.0 10.1 %copy-start.4 = (bf16[2,256,256]{2,1,0:T(8,128)(2,1)}, bf16[2,256,256]{2,1,0:T(8,128)(2,1)S(1)}, u32[]{:S(2)}) copy-start(bf16[2,256,256]{2,1,0:T(8,128)(2,1)S(1)} %collective-permute-done.2.refs_2_) | copy-start | bytes 786436
  58.0 12.3 %collective-permute-start.3 = (bf16[2,256,256]{2,1,0:T(8,128)(2,1)S(1)}, bf16[2,256,256]{2,1,0:T(8,128)(2,1)S(1)}, u32[]{:S(2)}, u32[]{:S(2)}) collective-permute-start(bf16[2,256,256]{2,1,0:T(8,128)(2,1)S(1)} %collective-permute-done.2.refs_2_), channel_id=1, source_target_pairs={{0,2},{2,0},{4,6},{6,4},{8,10},{10,8},{12,14},{14,12},{1,3},{3,1},... | collective-permute-start | bytes 786440 | tf_op jit(solution)/shard_map/ppermute | solution.py:29
  58.9 20.3 %collective-permute-start.20 = (bf16[3,32,1536]{2,1,0:T(8,128)(2,1)}, bf16[3,32,1536]{2,1,0:T(8,128)(2,1)}, u32[]{:S(2)}, u32[]{:S(2)}) collective-permute-start(bf16[3,32,1536]{2,1,0:T(8,128)(2,1)} %get-tuple-element.34), channel_id=1, source_target_pairs={{0,12},{2,6},{4,8},{6,2},{8,4},{10,14},{12,0},{14,10},{1,13},{3,7}... | collective-permute-start | bytes 884744 | tf_op jit(solution)/shard_map/ppermute | solution.py:307
  61.2 18.1 %collective-permute-start.21 = (bf16[3,32,1536]{2,1,0:T(8,128)(2,1)}, bf16[3,32,1536]{2,1,0:T(8,128)(2,1)}, u32[]{:S(2)}, u32[]{:S(2)}) collective-permute-start(bf16[3,32,1536]{2,1,0:T(8,128)(2,1)} %get-tuple-element.35), channel_id=1, source_target_pairs={{0,4},{2,14},{4,0},{6,10},{8,12},{10,6},{12,8},{14,2},{1,5},{3,15}... | collective-permute-start | bytes 884744 | tf_op jit(solution)/shard_map/ppermute | solution.py:307
  67.4 25.7 %collective-permute-start.12 = (bf16[256,768]{1,0:T(8,128)(2,1)}, bf16[256,768]{1,0:T(8,128)(2,1)}, u32[]{:S(2)}, u32[]{:S(2)}) collective-permute-start(bf16[256,768]{1,0:T(8,128)(2,1)} %get-tuple-element.49), channel_id=1, source_target_pairs={{0,2},{2,0},{4,6},{6,4},{8,10},{10,8},{12,14},{14,12},{1,3},{3,1},... | collective-permute-start | bytes 1179656 | tf_op jit(solution)/shard_map/ppermute | solution.py:29
  68.7 24.4 %collective-permute-start.13 = (bf16[256,768]{1,0:T(8,128)(2,1)S(1)}, bf16[256,768]{1,0:T(8,128)(2,1)}, u32[]{:S(2)}, u32[]{:S(2)}) collective-permute-start(bf16[256,768]{1,0:T(8,128)(2,1)S(1)} %get-tuple-element.50.refs_4_), channel_id=1, source_target_pairs={{0,16},{2,18},{4,20},{6,22},{8,24},{10,26},{12,28},{14,30},{16,0},... | collective-permute-start | bytes 1179656 | tf_op jit(solution)/shard_map/ppermute | solution.py:326
  70.9 22.2 %collective-permute-start.14 = (bf16[256,768]{1,0:T(8,128)(2,1)}, bf16[256,768]{1,0:T(8,128)(2,1)}, u32[]{:S(2)}, u32[]{:S(2)}) collective-permute-start(bf16[256,768]{1,0:T(8,128)(2,1)} %get-tuple-element.49), channel_id=1, source_target_pairs={{0,18},{2,16},{4,22},{6,20},{8,26},{10,24},{12,30},{14,28},{16,2},... | collective-permute-start | bytes 1179656 | tf_op jit(solution)/shard_map/ppermute | solution.py:326
  73.8 1.0 copy-start.18
  74.8 1.0 copy-start.20
  75.8 1.0 copy-start.22
  79.2 20.4 %collective-permute-start.7 = (bf16[512,384]{1,0:T(8,128)(2,1)}, bf16[512,384]{1,0:T(8,128)(2,1)}, u32[]{:S(2)}, u32[]{:S(2)}) collective-permute-start(bf16[512,384]{1,0:T(8,128)(2,1)} %get-tuple-element.26), channel_id=1, source_target_pairs={{0,4},{2,6},{4,0},{6,2},{8,12},{10,14},{12,8},{14,10},{1,5},{3,7},... | collective-permute-start | bytes 1179656 | tf_op jit(solution)/shard_map/ppermute | solution.py:29
  79.3 1.0 copy-start.3
  80.3 1.0 copy-start.24
  81.3 1.0 copy-start.26
  88.7 4.4 %copy-start.6 = (bf16[2,256,256]{2,1,0:T(8,128)(2,1)S(1)}, bf16[2,256,256]{2,1,0:T(8,128)(2,1)}, u32[]{:S(2)}) copy-start(bf16[2,256,256]{2,1,0:T(8,128)(2,1)} %copy-done.4) | copy-start | bytes 786436
  88.7 77.1 %all-to-all-start.1 = ((bf16[8,32,1536]{2,1,0:T(8,128)(2,1)}), bf16[8,32,1536]{2,1,0:T(8,128)(2,1)}, u32[]{:S(2)}, u32[]{:S(2)}) async-start(bf16[8,32,1536]{2,1,0:T(8,128)(2,1)} %temporal.1), calls=%async_computation.1 | async-start | bytes 1572864 | tf_op jit(solution)/shard_map/all_to_all | solution.py:366
  93.1 1.0 copy-start.9
  95.0 4.6 %copy-start.15 = (f32[512,384]{1,0:T(8,128)S(1)}, f32[512,384]{1,0:T(8,128)}, u32[]{:S(2)}) copy-start(f32[512,384]{1,0:T(8,128)} %copy-done.14) | copy-start | bytes 2359300
  97.6 25.2 %collective-permute-start.15 = (bf16[512,384]{1,0:T(8,128)(2,1)S(1)}, bf16[512,384]{1,0:T(8,128)(2,1)S(1)}, u32[]{:S(2)}, u32[]{:S(2)}) collective-permute-start(bf16[512,384]{1,0:T(8,128)(2,1)S(1)} %get-tuple-element.29), channel_id=1, source_target_pairs={{0,4},{2,6},{4,0},{6,2},{8,12},{10,14},{12,8},{14,10},{1,5},{3,7},... | collective-permute-start | bytes 1179656 | tf_op jit(solution)/shard_map/ppermute | solution.py:29
  101.5 40.0 %collective-permute-start.8 = (bf16[512,384]{1,0:T(8,128)(2,1)}, bf16[512,384]{1,0:T(8,128)(2,1)}, u32[]{:S(2)}, u32[]{:S(2)}) collective-permute-start(bf16[512,384]{1,0:T(8,128)(2,1)} %get-tuple-element.39), channel_id=1, source_target_pairs={{0,8},{2,10},{4,12},{6,14},{8,0},{10,2},{12,4},{14,6},{1,9},{3,11}... | collective-permute-start | bytes 1179656 | tf_op jit(solution)/shard_map/ppermute | solution.py:29
  122.8 7.9 %copy-start.29 = (s32[2]{0:T(128)S(1)}, s32[2]{0:T(128)}, u32[]{:S(2)}) copy-start(s32[2]{0:T(128)} %param.12) | copy-start | bytes 28
  123.9 24.0 %collective-permute-start.16 = (bf16[512,384]{1,0:T(8,128)(2,1)}, bf16[512,384]{1,0:T(8,128)(2,1)}, u32[]{:S(2)}, u32[]{:S(2)}) collective-permute-start(bf16[512,384]{1,0:T(8,128)(2,1)} %get-tuple-element.37), channel_id=1, source_target_pairs={{0,8},{2,10},{4,12},{6,14},{8,0},{10,2},{12,4},{14,6},{1,9},{3,11}... | collective-permute-start | bytes 1179656 | tf_op jit(solution)/shard_map/ppermute | solution.py:29
  126.0 12.0 %collective-permute-start.10 = (bf16[256,384]{1,0:T(8,128)(2,1)}, bf16[256,384]{1,0:T(8,128)(2,1)S(1)}, u32[]{:S(2)}, u32[]{:S(2)}) collective-permute-start(bf16[256,384]{1,0:T(8,128)(2,1)} %get-tuple-element.56), channel_id=1, source_target_pairs={{0,4},{2,6},{4,0},{6,2},{8,12},{10,14},{12,8},{14,10},{1,5},{3,7},... | collective-permute-start | bytes 589832 | tf_op jit(solution)/shard_map/ppermute | solution.py:29
  127.7 13.7 %collective-permute-start.11 = (bf16[256,384]{1,0:T(8,128)(2,1)}, bf16[256,384]{1,0:T(8,128)(2,1)}, u32[]{:S(2)}, u32[]{:S(2)}) collective-permute-start(bf16[256,384]{1,0:T(8,128)(2,1)} %get-tuple-element.53), channel_id=1, source_target_pairs={{0,6},{2,4},{4,2},{6,0},{8,14},{10,12},{12,10},{14,8},{1,7},{3,5},... | collective-permute-start | bytes 589832 | tf_op jit(solution)/shard_map/ppermute | solution.py:29
  127.7 13.7 %collective-permute-start.9 = (bf16[256,384]{1,0:T(8,128)(2,1)}, bf16[256,384]{1,0:T(8,128)(2,1)}, u32[]{:S(2)}, u32[]{:S(2)}) collective-permute-start(bf16[256,384]{1,0:T(8,128)(2,1)} %get-tuple-element.54), channel_id=1, source_target_pairs={{0,2},{2,0},{4,6},{6,4},{8,10},{10,8},{12,14},{14,12},{1,3},{3,1},... | collective-permute-start | bytes 589832 | tf_op jit(solution)/shard_map/ppermute | solution.py:29
  141.4 6.5 %copy-start.2 = (f32[512,384]{1,0:T(8,128)S(1)}, f32[512,384]{1,0:T(8,128)}, u32[]{:S(2)}) copy-start(f32[512,384]{1,0:T(8,128)} %get-tuple-element.38.kept_ref) | copy-start | bytes 2359300
  147.9 7.7 %copy-start.13 = (bf16[1,1,256,1536]{3,2,1,0:T(8,128)(2,1)S(1)}, bf16[1,1,256,1536]{3,2,1,0:T(8,128)(2,1)}, u32[]{:S(2)}) copy-start(bf16[1,1,256,1536]{3,2,1,0:T(8,128)(2,1)} %param.9) | copy-start | bytes 2359300
  149.9 10.9 %collective-permute-start.17 = (bf16[256,384]{1,0:T(8,128)(2,1)S(1)}, bf16[256,384]{1,0:T(8,128)(2,1)S(1)}, u32[]{:S(2)}, u32[]{:S(2)}) collective-permute-start(bf16[256,384]{1,0:T(8,128)(2,1)S(1)} %get-tuple-element.31), channel_id=1, source_target_pairs={{0,4},{2,6},{4,0},{6,2},{8,12},{10,14},{12,8},{14,10},{1,5},{3,7},... | collective-permute-start | bytes 589832 | tf_op jit(solution)/shard_map/ppermute | solution.py:29
  153.9 6.9 %collective-permute-start.18 = (bf16[256,384]{1,0:T(8,128)(2,1)S(1)}, bf16[256,384]{1,0:T(8,128)(2,1)S(1)}, u32[]{:S(2)}, u32[]{:S(2)}) collective-permute-start(bf16[256,384]{1,0:T(8,128)(2,1)S(1)} %get-tuple-element.32), channel_id=1, source_target_pairs={{0,2},{2,0},{4,6},{6,4},{8,10},{10,8},{12,14},{14,12},{1,3},{3,1},... | collective-permute-start | bytes 589832 | tf_op jit(solution)/shard_map/ppermute | solution.py:29
  154.3 9.6 %collective-permute-start.19 = (bf16[256,384]{1,0:T(8,128)(2,1)S(1)}, bf16[256,384]{1,0:T(8,128)(2,1)S(1)}, u32[]{:S(2)}, u32[]{:S(2)}) collective-permute-start(bf16[256,384]{1,0:T(8,128)(2,1)S(1)} %get-tuple-element.33), channel_id=1, source_target_pairs={{0,6},{2,4},{4,2},{6,0},{8,14},{10,12},{12,10},{14,8},{1,7},{3,5},... | collective-permute-start | bytes 589832 | tf_op jit(solution)/shard_map/ppermute | solution.py:29
  163.9 1.4 copy-start.1
  (11 other events, 9.0 us)

commit v5 on v4

--- a/solution.py
+++ b/solution.py
@@ -160,40 +160,43 @@
     )(qkv, residual)
 
 
-def temporal_kernel(frames, scalar_ref, *refs):
-    frame_refs, out_ref = refs[:frames], refs[frames]
+def temporal_kernel(plan, scalar_ref, *refs):
+    frames = len(plan[0])
+    frame_refs, out_refs = refs[:frames], refs[frames:]
     _, tokens, cols = frame_refs[0].shape
     rows = frames * tokens
     row_token = lax.rem(lax.broadcasted_iota(jnp.int32, (rows, rows), 0), tokens)
     col_token = lax.rem(lax.broadcasted_iota(jnp.int32, (rows, rows), 1), tokens)
     same = row_token == col_token
+    even = scalar_ref[0] == 0
     for head in range(cols // HDIM):
         at = lanes(head)
         query, key_rows, values = (
             jnp.concatenate([r[i, :, at] for r in frame_refs], axis=0) for i in range(3)
         )
         weights = softmax(jnp.where(same, scores_of(query, key_rows), -jnp.inf))
-        result = jnp.dot(weights, values, preferred_element_type=F32).astype(BF16)
-        for j in range(frames):
-            out_ref[scalar_ref[j], :, at] = result[j * tokens : (j + 1) * tokens]
-
-
-def temporal_attention(places, pieces):
-    frames = len(pieces)
+        result = jnp.dot(weights, values, preferred_element_type=F32)
+        parts = [result[j * tokens : (j + 1) * tokens] for j in range(frames)]
+        for out_ref, first, second in zip(out_refs, *plan):
+            part = parts[first] if first == second else jnp.where(even, parts[first], parts[second])
+            out_ref[:, at] = part.astype(BF16)
+
+
+def temporal_attention(core, plan, pieces):
     _, tokens, width = pieces[0].shape
     cols = block_cols(width)
     return pl.pallas_call(
-        functools.partial(temporal_kernel, frames),
+        functools.partial(temporal_kernel, plan),
         grid_spec=pltpu.PrefetchScalarGridSpec(
             num_scalar_prefetch=1,
             grid=(width // cols,),
-            in_specs=[pl.BlockSpec((3, tokens, cols), lambda j, s: (0, 0, j))] * frames,
-            out_specs=pl.BlockSpec((frames, tokens, cols), lambda j, s: (0, 0, j)),
+            in_specs=[pl.BlockSpec((3, tokens, cols), lambda j, s: (0, 0, j))] * len(pieces),
+            out_specs=[pl.BlockSpec((tokens, cols), lambda j, s: (0, j))] * len(pieces),
         ),
-        out_shape=jax.ShapeDtypeStruct((frames, tokens, width), BF16),
+        out_shape=[jax.ShapeDtypeStruct((tokens, width), BF16)] * len(pieces),
         compiler_params=MODEST,
         name="temporal",
-    )(places, *pieces)
+    )(core.reshape(1), *pieces)
 
 
 def weigh_kernel(bias_ref, kept_ref, come_ref, *refs):
@@ -262,10 +265,29 @@
             in_specs=[side] + [VMEM_SPEC] * len(pieces),
             out_specs=side,
         ),
-        out_shape=jax.ShapeDtypeStruct(base.shape, F32),
+        out_shape=pltpu.VMEM(base.shape, F32),
         compiler_params=MODEST,
         name="gather_results",
     )(place.reshape(1), base, *on_chip(*pieces))
+
+
+def final_kernel(scalar_ref, total_ref, *refs):
+    piece_refs, out_ref = refs[:-1], refs[-1]
+    rows = piece_refs[0].shape[0]
+    for k, piece_ref in enumerate(piece_refs):
+        at = pl.ds(pl.multiple_of((scalar_ref[0] ^ k) * rows, rows), rows)
+        out_ref[at, :] = (total_ref[at, :] + piece_ref[...].astype(F32)).astype(BF16)
+
+
+def final_sum(me, total, pieces):
+    return pl.pallas_call(
+        final_kernel,
+        in_specs=[SMEM_SPEC] + [VMEM_SPEC] * (1 + len(pieces)),
+        out_specs=VMEM_SPEC,
+        out_shape=jax.ShapeDtypeStruct(total.shape, BF16),
+        compiler_params=MODEST,
+        name="final",
+    )(me.reshape(1), *on_chip(total, *pieces))
 
 
 def temporal_plan(seq):
@@ -291,17 +313,14 @@
     qkv = latent_qkv[0, 0].transpose(1, 0, 2)
     share = tokens // seq
     steps = temporal_plan(seq)
-    pieces, sources = [lax.dynamic_slice_in_dim(qkv, me * share, share, 1)], [me]
+    pieces = [lax.dynamic_slice_in_dim(qkv, me * share, share, 1)]
     held = qkv
     for number, (even, odd) in enumerate(steps):
-        crossing = even & 1
         target = me ^ jnp.where(core == 0, even, odd)
         if number == 2:
             held, blocks = lax.optimization_barrier((qkv, blocks))
         block = lax.dynamic_slice_in_dim(held, target * share, share, 1)
         blocks = [block] if number == 0 else blocks + [block]
-        sender_core = core ^ crossing
-        sources.append(me ^ jnp.where(sender_core == 0, even, odd))
     for number, (even, odd) in enumerate(steps):
         pairs = [(i, i ^ (odd if i & 1 else even)) for i in range(seq)]
         pieces.append(lax.ppermute(blocks[number], "seq", pairs))
@@ -362,8 +381,14 @@
     bias = jnp.where(position < length, 0.0, -1e9).astype(F32)[None]
 
     base = spatial_attention(qkv, residual[0, 0])
-    temporal = temporal_attention(jnp.stack(sources).astype(jnp.int32), pieces)
-    temporal = lax.all_to_all(temporal, "seq", 0, 0, tiled=True).reshape(tokens, width)
+    plan = []
+    for here in range(2):
+        sources = [0] + [(odd if (here ^ even) & 1 else even) for even, odd in steps]
+        plan.append(tuple(sources.index(k) for k in range(seq)))
+    moved = temporal_attention(core, plan, pieces)
+    returned = [moved[0]]
+    for k in range(1, seq):
+        returned.append(swap(moved[k], "seq", k))
 
     shares = cross_weights(bias, *sums[0], queries)
     crossed = cross_values(shares, *sums[1])
@@ -372,7 +397,7 @@
         results.append(swap(crossed[k], "seq", k))
     results[1], results[2] = results[2], results[1]
     total = gather_results(place, base, results)
-    return (total + temporal.astype(F32)).astype(BF16)[None, None]
+    return final_sum(me, total, returned)[None, None]
 
 
 def solution(mesh):

time: 169 us -> 182 us (1.077)
  starting transfers between devices: 39.2 us -> 64.8 us
  local copies, waits for them, and re-layouts: 29.8 us -> 19.9 us
  other arithmetic: 5.81 us -> 3.84 us
    ppermute x7, starting transfers between devices: 7.83 us -> 32.8 us  [block(): pieces.append(lax.ppermute(blocks[number], 'seq', pairs))]
    ppermute x16 -> x23, waiting for transfers between devices: 34.6 us -> 23.8 us  [swap(): return lax.ppermute(value, axis, pairs)]
    ppermute x4, waiting for transfers between devices: 4.67 us -> 14.8 us  [block(): weights[kind].append(lax.ppermute(part, ('grp', 'seq'), pairs))]
    ppermute x7, waiting for transfers between devices: 28.7 us -> 20.6 us  [block(): pieces.append(lax.ppermute(blocks[number], 'seq', pairs))]
    unnamed x61 -> x51, local copies, waits for them, and re-layouts: 21.1 us -> 13.7 us
    all_to_all x1, waiting for transfers between devices: 0.01 us -> 7.33 us  [block(): parts = lax.all_to_all(parts, 'seq', 0, 0, tiled=True)]
    all_to_all x1 -> x0, starting transfers between devices: 4.34 us -> none  [block(): lax.all_to_all(temporal, 'seq', 0, 0, tiled=True).reshape(tokens, width)]
    ppermute x16 -> x23, starting transfers between devices: 16.3 us -> 19.4 us  [swap(): return lax.ppermute(value, axis, pairs)]
  transfers between devices with their start and end apart: 29 -> 35, of which waited for: 10 -> 15; matrix products, arithmetic and copies ran while one was open for 9% -> 6% of each run, Pallas kernels for 13% -> 11%
where the time goes in v5:
time: 182 us; the launch traced here: 180 us
  waiting for transfers between devices  66.5 us (37%)
  starting transfers between devices  64.8 us (36%)
  Pallas kernels  22.3 us (12%)
  local copies, waits for them, and re-layouts  19.9 us (11%)
  other arithmetic  3.84 us (2%)
  between operations  2.26 us (1%)
    ppermute x7, starting transfers between devices, block(): pieces.append(lax.ppermute(blocks[number], 'seq', pairs))  32.8 us
    ppermute x23, waiting for transfers between devices, swap(): return lax.ppermute(value, axis, pairs)  23.8 us
    ppermute x7, waiting for transfers between devices, block(): pieces.append(lax.ppermute(blocks[number], 'seq', pairs))  20.6 us
    ppermute x23, starting transfers between devices, swap(): return lax.ppermute(value, axis, pairs)  19.4 us
    ppermute x4, waiting for transfers between devices, block(): weights[kind].append(lax.ppermute(part, ('grp', 'seq'), pairs))  14.8 us
    unnamed x51, local copies, waits for them, and re-layouts  13.7 us
    all_to_all x1, waiting for transfers between devices, block(): parts = lax.all_to_all(parts, 'seq', 0, 0, tiled=True)  7.33 us
    all_to_all x1, starting transfers between devices, block(): parts = lax.all_to_all(parts, 'seq', 0, 0, tiled=True)  6.35 us
  transfers between devices with their start and end apart: 35, of which 15 were waited for; matrix products, arithmetic and copies ran while one was open for 6% of the time, Pallas kernels for 11%

profile of v5, /device:TPU:0, one launch (start us, length us, event | category | flops | bytes accessed | tf_op | source)
XLA Modules:
  0.0 179.5 jit_solution(2105869429202710554)
XLA Ops:
  0.0 1.0 copy-done.11
  1.8 6.4 %all-to-all-start = ((bf16[8,2,32,256]{3,2,1,0:T(8,128)(2,1)}), bf16[8,2,32,256]{3,2,1,0:T(8,128)(2,1)S(1)}, u32[]{:S(2)}, u32[]{:S(2)}) async-start(bf16[8,2,32,256]{3,2,1,0:T(8,128)(2,1)} %prompt_blocks.1), calls=%async_computation | async-start | bytes 524288 | tf_op jit(solution)/shard_map/all_to_all | solution.py:311
  8.1 1.6 copy.10
  10.5 7.3 %all-to-all-done.parts_ref = bf16[8,2,32,256]{3,2,1,0:T(8,128)(2,1)S(1)} async-done(((bf16[8,2,32,256]{3,2,1,0:T(8,128)(2,1)}), bf16[8,2,32,256]{3,2,1,0:T(8,128)(2,1)S(1)}, u32[]{:S(2)}, u32[]{:S(2)}) %all-to-all-start) | async-done | bytes 262176 | tf_op jit(solution)/shard_map/all_to_all | solution.py:311
  18.4 1.6 collective-permute-start
  20.7 1.2 collective-permute-start.14
  22.0 1.7 collective-permute-done
  23.7 1.6 collective-permute-start.2
  25.3 5.3 %collective-permute-done.2.refs_2_ = bf16[2,256,256]{2,1,0:T(8,128)(2,1)S(1)} collective-permute-done((bf16[2,256,256]{2,1,0:T(8,128)(2,1)S(1)}, bf16[2,256,256]{2,1,0:T(8,128)(2,1)S(1)}, u32[]{:S(2)}, u32[]{:S(2)}) %collective-permute-start.2) | collective-permute-done | bytes 262176 | tf_op jit(solution)/shard_map/ppermute | solution.py:29
  31.1 1.0 collective-permute-done.13.refs_6_
  32.2 2.4 %collective-permute-start.5 = (bf16[256,768]{1,0:T(8,128)(2,1)S(1)}, bf16[256,768]{1,0:T(8,128)(2,1)}, u32[]{:S(2)}, u32[]{:S(2)}) collective-permute-start(bf16[256,768]{1,0:T(8,128)(2,1)S(1)} %get-tuple-element.31.refs_4_), channel_id=1, source_target_pairs={{0,16},{2,18},{4,20},{6,22},{8,24},{10,26},{12,28},{14,30},{16,0},... | collective-permute-start | bytes 1179656 | tf_op jit(solution)/shard_map/ppermute | solution.py:345
  34.6 5.9 %collective-permute-done.14.refs_7_ = bf16[256,768]{1,0:T(8,128)(2,1)S(1)} collective-permute-done((bf16[256,768]{1,0:T(8,128)(2,1)S(1)}, bf16[256,768]{1,0:T(8,128)(2,1)S(1)}, u32[]{:S(2)}, u32[]{:S(2)}) %collective-permute-start.14) | collective-permute-done | bytes 393248 | tf_op jit(solution)/shard_map/ppermute | solution.py:345
  40.5 1.9 %collective-permute-start.6 = (bf16[256,768]{1,0:T(8,128)(2,1)}, bf16[256,768]{1,0:T(8,128)(2,1)}, u32[]{:S(2)}, u32[]{:S(2)}) collective-permute-start(bf16[256,768]{1,0:T(8,128)(2,1)} %get-tuple-element.32), channel_id=1, source_target_pairs={{0,18},{2,16},{4,22},{6,20},{8,26},{10,24},{12,30},{14,28},{16,2},... | collective-permute-start | bytes 1179656 | tf_op jit(solution)/shard_map/ppermute | solution.py:345
  42.4 1.6 project.3
  45.0 2.2 %dynamic-slice_bitcast_fusion.7 = (bf16[256,384]{1,0:T(8,128)(2,1)}, bf16[256,384]{1,0:T(8,128)(2,1)}, bf16[256,384]{1,0:T(8,128)(2,1)}, bf16[256,384]{1,0:T(8,128)(2,1)}) fusion(bf16[1,1,256,1536]{3,2,1,0:T(8,128)(2,1)} %param.8, s32[]{:T(128)S(6)} %select_n.137, s32[]{:T(128)S(6)} %select_n.135, s32[]{:T(128)S(6)} %select_n.134, s32[]{:T(128)S(6)} %select_n.136), kind=kLoop, calls=%fused_computation.11 | loop fusion | bytes 1572880 | tf_op jit(solution)/shard_map/dynamic_slice | solution.py:361
  47.2 2.0 %collective-permute-start.10 = (bf16[256,384]{1,0:T(8,128)(2,1)}, bf16[256,384]{1,0:T(8,128)(2,1)}, u32[]{:S(2)}, u32[]{:S(2)}) collective-permute-start(bf16[256,384]{1,0:T(8,128)(2,1)} %get-tuple-element.72), channel_id=1, source_target_pairs={{0,4},{2,6},{4,0},{6,2},{8,12},{10,14},{12,8},{14,10},{1,5},{3,7},... | collective-permute-start | bytes 589832 | tf_op jit(solution)/shard_map/ppermute | solution.py:29
  49.2 7.8 %collective-permute-done.6.refs_7_ = bf16[256,768]{1,0:T(8,128)(2,1)} collective-permute-done((bf16[256,768]{1,0:T(8,128)(2,1)}, bf16[256,768]{1,0:T(8,128)(2,1)}, u32[]{:S(2)}, u32[]{:S(2)}) %collective-permute-start.6) | collective-permute-done | bytes 393248 | tf_op jit(solution)/shard_map/ppermute | solution.py:345
  57.0 0.9 copy-done.4
  57.9 2.8 %project.2 = (f32[512,384]{1,0:T(8,128)S(1)}, bf16[512,384]{1,0:T(8,128)(2,1)}) custom-call(s32[1]{0:T(128)} %bitcast.7.scalar_ref, bf16[2,256,256]{2,1,0:T(8,128)(2,1)S(1)} %pad_maximum_fusion.refs_0_, bf16[2,256,256]{2,1,0:T(8,128)(2,1)S(1)} %collective-permute-done.1.refs_1_, bf16[2,256,256]{2,1,0:T(8,128)(2,1)S(1)} %collective-permute-done.2.refs_2_, ...), custom_call_target="tpu_custom_call" | custom-call | tf_op jit(solution)/shard_map/project/pallas_call | solution.py:128
  63.0 2.0 %fusion.4 = (bf16[512,384]{1,0:T(8,128)(2,1)S(1)}, f32[512,384]{1,0:T(8,128)}) fusion(f32[512,384]{1,0:T(8,128)S(1)} %copy-done.8, bf16[512,384]{1,0:T(8,128)(2,1)} %collective-permute-done.15), kind=kLoop, calls=%fused_computation.34 | loop fusion | flops 589824 | bytes 2359296 | tf_op jit(solution)/shard_map/convert_element_type | solution.py:370
  65.0 1.5 collective-permute-start.16
  66.5 11.2 %collective-permute-done.7 = bf16[512,384]{1,0:T(8,128)(2,1)} collective-permute-done((bf16[512,384]{1,0:T(8,128)(2,1)}, bf16[512,384]{1,0:T(8,128)(2,1)}, u32[]{:S(2)}, u32[]{:S(2)}) %collective-permute-start.7) | collective-permute-done | bytes 393248 | tf_op jit(solution)/shard_map/ppermute | solution.py:29
  77.7 1.1 fusion.5
  80.1 1.6 collective-permute-start.22
  81.9 1.4 collective-permute-start.9
  83.4 1.1 collective-permute-done.9.refs_1_
  85.1 1.5 collective-permute-start.24
  86.6 8.4 %collective-permute-done.22.refs_3_ = bf16[3,32,1536]{2,1,0:T(8,128)(2,1)S(1)} collective-permute-done((bf16[3,32,1536]{2,1,0:T(8,128)(2,1)S(1)}, bf16[3,32,1536]{2,1,0:T(8,128)(2,1)S(1)}, u32[]{:S(2)}, u32[]{:S(2)}) %collective-permute-start.22) | collective-permute-done | bytes 294944 | tf_op jit(solution)/shard_map/ppermute | solution.py:326
  95.7 27.1 %collective-permute-start.25 = (bf16[3,32,1536]{2,1,0:T(8,128)(2,1)}, bf16[3,32,1536]{2,1,0:T(8,128)(2,1)}, u32[]{:S(2)}, u32[]{:S(2)}) collective-permute-start(bf16[3,32,1536]{2,1,0:T(8,128)(2,1)} %get-tuple-element.58), channel_id=1, source_target_pairs={{0,10},{2,8},{4,14},{6,12},{8,2},{10,0},{12,6},{14,4},{1,11},{3,9}... | collective-permute-start | bytes 884744 | tf_op jit(solution)/shard_map/ppermute | solution.py:326
  124.4 2.4 %collective-permute-start.20 = (bf16[3,32,1536]{2,1,0:T(8,128)(2,1)}, bf16[3,32,1536]{2,1,0:T(8,128)(2,1)}, u32[]{:S(2)}, u32[]{:S(2)}) collective-permute-start(bf16[3,32,1536]{2,1,0:T(8,128)(2,1)} %get-tuple-element.42), channel_id=1, source_target_pairs={{0,12},{2,6},{4,8},{6,2},{8,4},{10,14},{12,0},{14,10},{1,13},{3,7}... | collective-permute-start | bytes 884744 | tf_op jit(solution)/shard_map/ppermute | solution.py:326
  132.5 1.0 copy-done.15
  133.5 0.9 copy-done.21
  134.4 3.3 %cross_weights.1.weight_ref = bf16[3,4,256,512]{3,2,1,0:T(8,128)(2,1)S(1)} custom-call(f32[1,512]{1,0:T(1,128)S(1)} %compare_select_fusion.bias_ref, f32[512,384]{1,0:T(8,128)S(1)} %get-tuple-element.56.kept_ref, bf16[512,384]{1,0:T(8,128)(2,1)S(1)} %copy-done.15, bf16[256,384]{1,0:T(8,128)(2,1)S(1)} %copy-done.5, bf16[256,384]{1,0:T(8,128)(2,1)S(1)} %copy-done.21, ...), custom_call_target="tpu_custom_call" | custom-call | tf_op jit(solution)/shard_map/cross_weights/pallas_call | solution.py:214
  137.7 1.0 cross_values.1
  138.7 1.8 %collective-permute-done.24.refs_5_ = bf16[3,32,1536]{2,1,0:T(8,128)(2,1)} collective-permute-done((bf16[3,32,1536]{2,1,0:T(8,128)(2,1)}, bf16[3,32,1536]{2,1,0:T(8,128)(2,1)}, u32[]{:S(2)}, u32[]{:S(2)}) %collective-permute-start.24) | collective-permute-done | bytes 294944 | tf_op jit(solution)/shard_map/ppermute | solution.py:326
  140.8 5.7 %collective-permute-done.25.refs_6_ = bf16[3,32,1536]{2,1,0:T(8,128)(2,1)} collective-permute-done((bf16[3,32,1536]{2,1,0:T(8,128)(2,1)}, bf16[3,32,1536]{2,1,0:T(8,128)(2,1)}, u32[]{:S(2)}, u32[]{:S(2)}) %collective-permute-start.25) | collective-permute-done | bytes 294944 | tf_op jit(solution)/shard_map/ppermute | solution.py:326
  147.4 4.7 %collective-permute-done.21.refs_2_ = bf16[3,32,1536]{2,1,0:T(8,128)(2,1)} collective-permute-done((bf16[3,32,1536]{2,1,0:T(8,128)(2,1)}, bf16[3,32,1536]{2,1,0:T(8,128)(2,1)}, u32[]{:S(2)}, u32[]{:S(2)}) %collective-permute-start.21) | collective-permute-done | bytes 294944 | tf_op jit(solution)/shard_map/ppermute | solution.py:326
  152.1 5.5 %temporal.1 = (bf16[32,1536]{1,0:T(8,128)(2,1)S(1)}, bf16[32,1536]{1,0:T(8,128)(2,1)S(1)}, bf16[32,1536]{1,0:T(8,128)(2,1)S(1)}, bf16[32,1536]{1,0:T(8,128)(2,1)...) custom-call(s32[1]{0:T(128)} %bitcast.21.scalar_ref, ...), custom_call_target="tpu_custom_call" | custom-call | tf_op jit(solution)/shard_map/temporal/pallas_call | solution.py:188
  157.7 1.9 %collective-permute-start.28 = (bf16[32,1536]{1,0:T(8,128)(2,1)S(1)}, bf16[32,1536]{1,0:T(8,128)(2,1)S(1)}, u32[]{:S(2)}, u32[]{:S(2)}) collective-permute-start(bf16[32,1536]{1,0:T(8,128)(2,1)S(1)} %get-tuple-element.47), channel_id=1, source_target_pairs={{0,4},{2,6},{4,0},{6,2},{8,12},{10,14},{12,8},{14,10},{1,5},{3,7},... | collective-permute-start | bytes 294920 | tf_op jit(solution)/shard_map/ppermute | solution.py:29
  159.6 1.0 collective-permute-start.29
  160.5 2.8 %collective-permute-done.28.refs_2_ = bf16[32,1536]{1,0:T(8,128)(2,1)S(1)} collective-permute-done((bf16[32,1536]{1,0:T(8,128)(2,1)S(1)}, bf16[32,1536]{1,0:T(8,128)(2,1)S(1)}, u32[]{:S(2)}, u32[]{:S(2)}) %collective-permute-start.28) | collective-permute-done | bytes 98336 | tf_op jit(solution)/shard_map/ppermute | solution.py:29
  163.3 2.2 %collective-permute-start.30 = (bf16[32,1536]{1,0:T(8,128)(2,1)S(1)}, bf16[32,1536]{1,0:T(8,128)(2,1)S(1)}, u32[]{:S(2)}, u32[]{:S(2)}) collective-permute-start(bf16[32,1536]{1,0:T(8,128)(2,1)S(1)} %get-tuple-element.49), channel_id=1, source_target_pairs={{0,8},{2,10},{4,12},{6,14},{8,0},{10,2},{12,4},{14,6},{1,9},{3,11}... | collective-permute-start | bytes 294920 | tf_op jit(solution)/shard_map/ppermute | solution.py:29
  165.6 2.1 %collective-permute-start.32 = (bf16[32,1536]{1,0:T(8,128)(2,1)S(1)}, bf16[32,1536]{1,0:T(8,128)(2,1)S(1)}, u32[]{:S(2)}, u32[]{:S(2)}) collective-permute-start(bf16[32,1536]{1,0:T(8,128)(2,1)S(1)} %get-tuple-element.51), channel_id=1, source_target_pairs={{0,12},{2,14},{4,8},{6,10},{8,4},{10,6},{12,0},{14,2},{1,13},{3,15... | collective-permute-start | bytes 294920 | tf_op jit(solution)/shard_map/ppermute | solution.py:29
  167.7 1.9 %collective-permute-start.33 = (bf16[32,1536]{1,0:T(8,128)(2,1)S(1)}, bf16[32,1536]{1,0:T(8,128)(2,1)S(1)}, u32[]{:S(2)}, u32[]{:S(2)}) collective-permute-start(bf16[32,1536]{1,0:T(8,128)(2,1)S(1)} %get-tuple-element.52), channel_id=1, source_target_pairs={{0,14},{2,12},{4,10},{6,8},{8,6},{10,4},{12,2},{14,0},{1,15},{3,13... | collective-permute-start | bytes 294920 | tf_op jit(solution)/shard_map/ppermute | solution.py:29
  169.5 5.3 %spatial.1.base_ref = f32[256,1536]{1,0:T(8,128)} custom-call(bf16[3,256,1536]{2,1,0:T(8,128)(2,1)S(1)} %bitcast.47, bf16[256,1536]{1,0:T(8,128)(2,1)S(1)} %bitcast.48), custom_call_target="tpu_custom_call" | custom-call | tf_op jit(solution)/shard_map/spatial/pallas_call | solution.py:149
  174.8 1.4 copy-done.1
  177.0 1.5 collective-permute-done.31.refs_5_
  178.5 1.0 final.1
  (94 shorter events, 16.8 us)
Async XLA Ops:
  1.8 16.1 %all-to-all-start = ((bf16[8,2,32,256]{3,2,1,0:T(8,128)(2,1)}), bf16[8,2,32,256]{3,2,1,0:T(8,128)(2,1)S(1)}, u32[]{:S(2)}, u32[]{:S(2)}) async-start(bf16[8,2,32,256]{3,2,1,0:T(8,128)(2,1)} %prompt_blocks.1), calls=%async_computation | async-start | bytes 524288 | tf_op jit(solution)/shard_map/all_to_all | solution.py:311
  9.7 8.1 %copy-start.22 = (s32[2]{0:T(128)S(1)}, s32[2]{0:T(128)}, u32[]{:S(2)}) copy-start(s32[2]{0:T(128)} %assignment_ref.1) | copy-start | bytes 28
  18.4 5.3 %collective-permute-start = (bf16[256,256]{1,0:T(8,128)(2,1)S(1)}, bf16[256,256]{1,0:T(8,128)(2,1)S(1)}, u32[]{:S(2)}, u32[]{:S(2)}) collective-permute-start(bf16[256,256]{1,0:T(8,128)(2,1)S(1)} %get-tuple-element.30), channel_id=1, source_target_pairs={{0,16},{16,0},{1,17},{17,1},{2,18},{18,2},{3,19},{19,3},{4,20},{20... | collective-permute-start | bytes 393224 | tf_op jit(solution)/shard_map/ppermute | solution.py:29
  20.0 10.6 %collective-permute-start.12 = (bf16[256,768]{1,0:T(8,128)(2,1)S(1)}, bf16[256,768]{1,0:T(8,128)(2,1)S(1)}, u32[]{:S(2)}, u32[]{:S(2)}) collective-permute-start(bf16[256,768]{1,0:T(8,128)(2,1)S(1)} %get-tuple-element.65), channel_id=1, source_target_pairs={{0,2},{2,0},{4,6},{6,4},{8,10},{10,8},{12,14},{14,12},{1,3},{3,1},... | collective-permute-start | bytes 1179656 | tf_op jit(solution)/shard_map/ppermute | solution.py:29
  20.1 12.1 %collective-permute-start.13 = (bf16[256,768]{1,0:T(8,128)(2,1)S(1)}, bf16[256,768]{1,0:T(8,128)(2,1)S(1)}, u32[]{:S(2)}, u32[]{:S(2)}) collective-permute-start(bf16[256,768]{1,0:T(8,128)(2,1)S(1)} %get-tuple-element.66.refs_4_), channel_id=1, source_target_pairs={{0,16},{2,18},{4,20},{6,22},{8,24},{10,26},{12,28},{14,30},{16,0},... | collective-permute-start | bytes 1179656 | tf_op jit(solution)/shard_map/ppermute | solution.py:345
  20.7 19.8 %collective-permute-start.14 = (bf16[256,768]{1,0:T(8,128)(2,1)S(1)}, bf16[256,768]{1,0:T(8,128)(2,1)S(1)}, u32[]{:S(2)}, u32[]{:S(2)}) collective-permute-start(bf16[256,768]{1,0:T(8,128)(2,1)S(1)} %get-tuple-element.65), channel_id=1, source_target_pairs={{0,18},{2,16},{4,22},{6,20},{8,26},{10,24},{12,30},{14,28},{16,2},... | collective-permute-start | bytes 1179656 | tf_op jit(solution)/shard_map/ppermute | solution.py:345
  23.7 6.9 %collective-permute-start.2 = (bf16[2,256,256]{2,1,0:T(8,128)(2,1)S(1)}, bf16[2,256,256]{2,1,0:T(8,128)(2,1)S(1)}, u32[]{:S(2)}, u32[]{:S(2)}) collective-permute-start(bf16[2,256,256]{2,1,0:T(8,128)(2,1)S(1)} %pad_maximum_fusion.refs_0_), channel_id=1, source_target_pairs={{0,1},{1,0},{2,3},{3,2},{4,5},{5,4},{6,7},{7,6},{8,9},{9,8},{10,11... | collective-permute-start | bytes 786440 | tf_op jit(solution)/shard_map/ppermute | solution.py:29
  25.3 17.1 %collective-permute-start.1 = (bf16[2,256,256]{2,1,0:T(8,128)(2,1)S(1)}, bf16[2,256,256]{2,1,0:T(8,128)(2,1)S(1)}, u32[]{:S(2)}, u32[]{:S(2)}) collective-permute-start(bf16[2,256,256]{2,1,0:T(8,128)(2,1)S(1)} %pad_maximum_fusion.refs_0_), channel_id=1, source_target_pairs={{0,2},{2,0},{4,6},{6,4},{8,10},{10,8},{12,14},{14,12},{1,3},{3,1},... | collective-permute-start | bytes 786440 | tf_op jit(solution)/shard_map/ppermute | solution.py:29
  30.6 11.8 %collective-permute-start.3 = (bf16[2,256,256]{2,1,0:T(8,128)(2,1)S(1)}, bf16[2,256,256]{2,1,0:T(8,128)(2,1)S(1)}, u32[]{:S(2)}, u32[]{:S(2)}) collective-permute-start(bf16[2,256,256]{2,1,0:T(8,128)(2,1)S(1)} %collective-permute-done.2.refs_2_), channel_id=1, source_target_pairs={{0,2},{2,0},{4,6},{6,4},{8,10},{10,8},{12,14},{14,12},{1,3},{3,1},... | collective-permute-start | bytes 786440 | tf_op jit(solution)/shard_map/ppermute | solution.py:29
  30.6 18.5 %collective-permute-start.4 = (bf16[256,768]{1,0:T(8,128)(2,1)}, bf16[256,768]{1,0:T(8,128)(2,1)}, u32[]{:S(2)}, u32[]{:S(2)}) collective-permute-start(bf16[256,768]{1,0:T(8,128)(2,1)} %get-tuple-element.32), channel_id=1, source_target_pairs={{0,2},{2,0},{4,6},{6,4},{8,10},{10,8},{12,14},{14,12},{1,3},{3,1},... | collective-permute-start | bytes 1179656 | tf_op jit(solution)/shard_map/ppermute | solution.py:29
  32.2 17.0 %collective-permute-start.5 = (bf16[256,768]{1,0:T(8,128)(2,1)S(1)}, bf16[256,768]{1,0:T(8,128)(2,1)}, u32[]{:S(2)}, u32[]{:S(2)}) collective-permute-start(bf16[256,768]{1,0:T(8,128)(2,1)S(1)} %get-tuple-element.31.refs_4_), channel_id=1, source_target_pairs={{0,16},{2,18},{4,20},{6,22},{8,24},{10,26},{12,28},{14,30},{16,0},... | collective-permute-start | bytes 1179656 | tf_op jit(solution)/shard_map/ppermute | solution.py:345
  40.5 16.4 %collective-permute-start.6 = (bf16[256,768]{1,0:T(8,128)(2,1)}, bf16[256,768]{1,0:T(8,128)(2,1)}, u32[]{:S(2)}, u32[]{:S(2)}) collective-permute-start(bf16[256,768]{1,0:T(8,128)(2,1)} %get-tuple-element.32), channel_id=1, source_target_pairs={{0,18},{2,16},{4,22},{6,20},{8,26},{10,24},{12,30},{14,28},{16,2},... | collective-permute-start | bytes 1179656 | tf_op jit(solution)/shard_map/ppermute | solution.py:345
  42.4 2.6 %copy-start.3 = (bf16[2,256,256]{2,1,0:T(8,128)(2,1)}, bf16[2,256,256]{2,1,0:T(8,128)(2,1)S(1)}, u32[]{:S(2)}) copy-start(bf16[2,256,256]{2,1,0:T(8,128)(2,1)S(1)} %collective-permute-done.3.refs_3_) | copy-start | bytes 786436
  45.0 17.6 %collective-permute-start.15 = (bf16[512,384]{1,0:T(8,128)(2,1)}, bf16[512,384]{1,0:T(8,128)(2,1)}, u32[]{:S(2)}, u32[]{:S(2)}) collective-permute-start(bf16[512,384]{1,0:T(8,128)(2,1)} %get-tuple-element.37), channel_id=1, source_target_pairs={{0,4},{2,6},{4,0},{6,2},{8,12},{10,14},{12,8},{14,10},{1,5},{3,7},... | collective-permute-start | bytes 1179656 | tf_op jit(solution)/shard_map/ppermute | solution.py:29
  47.2 14.5 %copy-start = (bf16[1,1,256,3,1536]{4,2,3,1,0:T(8,128)(2,1)S(1)}, bf16[1,1,256,3,1536]{4,2,3,1,0:T(8,128)(2,1)}, u32[]{:S(2)}) copy-start(bf16[1,1,256,3,1536]{4,2,3,1,0:T(8,128)(2,1)} %param.7) | copy-start | bytes 7077892
  47.2 34.5 %collective-permute-start.10 = (bf16[256,384]{1,0:T(8,128)(2,1)}, bf16[256,384]{1,0:T(8,128)(2,1)}, u32[]{:S(2)}, u32[]{:S(2)}) collective-permute-start(bf16[256,384]{1,0:T(8,128)(2,1)} %get-tuple-element.72), channel_id=1, source_target_pairs={{0,4},{2,6},{4,0},{6,2},{8,12},{10,14},{12,8},{14,10},{1,5},{3,7},... | collective-permute-start | bytes 589832 | tf_op jit(solution)/shard_map/ppermute | solution.py:29
  49.1 32.8 %collective-permute-start.11 = (bf16[256,384]{1,0:T(8,128)(2,1)}, bf16[256,384]{1,0:T(8,128)(2,1)}, u32[]{:S(2)}, u32[]{:S(2)}) collective-permute-start(bf16[256,384]{1,0:T(8,128)(2,1)} %get-tuple-element.69), channel_id=1, source_target_pairs={{0,6},{2,4},{4,2},{6,0},{8,14},{10,12},{12,10},{14,8},{1,7},{3,5},... | collective-permute-start | bytes 589832 | tf_op jit(solution)/shard_map/ppermute | solution.py:29
  61.6 1.3 copy-start.8
  61.6 16.0 %collective-permute-start.7 = (bf16[512,384]{1,0:T(8,128)(2,1)}, bf16[512,384]{1,0:T(8,128)(2,1)}, u32[]{:S(2)}, u32[]{:S(2)}) collective-permute-start(bf16[512,384]{1,0:T(8,128)(2,1)} %get-tuple-element.34), channel_id=1, source_target_pairs={{0,4},{2,6},{4,0},{6,2},{8,12},{10,14},{12,8},{14,10},{1,5},{3,7},... | collective-permute-start | bytes 1179656 | tf_op jit(solution)/shard_map/ppermute | solution.py:29
  62.6 15.1 %copy-start.10 = (f32[512,384]{1,0:T(8,128)S(1)}, f32[512,384]{1,0:T(8,128)}, u32[]{:S(2)}) copy-start(f32[512,384]{1,0:T(8,128)} %copy-done.9) | copy-start | bytes 2359300
  65.0 58.6 %collective-permute-start.16 = (bf16[512,384]{1,0:T(8,128)(2,1)S(1)}, bf16[512,384]{1,0:T(8,128)(2,1)S(1)}, u32[]{:S(2)}, u32[]{:S(2)}) collective-permute-start(bf16[512,384]{1,0:T(8,128)(2,1)S(1)} %get-tuple-element.53), channel_id=1, source_target_pairs={{0,8},{2,10},{4,12},{6,14},{8,0},{10,2},{12,4},{14,6},{1,9},{3,11}... | collective-permute-start | bytes 1179656 | tf_op jit(solution)/shard_map/ppermute | solution.py:29
  78.8 3.2 %copy-start.23 = (bf16[256,384]{1,0:T(8,128)(2,1)S(1)}, bf16[256,384]{1,0:T(8,128)(2,1)}, u32[]{:S(2)}) copy-start(bf16[256,384]{1,0:T(8,128)(2,1)} %get-tuple-element.70) | copy-start | bytes 589828
  78.8 51.4 %copy-start.24 = (s32[2]{0:T(128)S(1)}, s32[2]{0:T(128)}, u32[]{:S(2)}) copy-start(s32[2]{0:T(128)} %param.12) | copy-start | bytes 28
  78.8 48.0 %collective-permute-start.8 = (bf16[512,384]{1,0:T(8,128)(2,1)S(1)}, bf16[512,384]{1,0:T(8,128)(2,1)S(1)}, u32[]{:S(2)}, u32[]{:S(2)}) collective-permute-start(bf16[512,384]{1,0:T(8,128)(2,1)S(1)} %get-tuple-element.55), channel_id=1, source_target_pairs={{0,8},{2,10},{4,12},{6,14},{8,0},{10,2},{12,4},{14,6},{1,9},{3,11}... | collective-permute-start | bytes 1179656 | tf_op jit(solution)/shard_map/ppermute | solution.py:29
  80.1 14.9 %collective-permute-start.22 = (bf16[3,32,1536]{2,1,0:T(8,128)(2,1)S(1)}, bf16[3,32,1536]{2,1,0:T(8,128)(2,1)S(1)}, u32[]{:S(2)}, u32[]{:S(2)}) collective-permute-start(bf16[3,32,1536]{2,1,0:T(8,128)(2,1)S(1)} %get-tuple-element.61), channel_id=1, source_target_pairs={{0,14},{2,4},{4,10},{6,0},{8,6},{10,12},{12,2},{14,8},{1,15},{3,5}... | collective-permute-start | bytes 884744 | tf_op jit(solution)/shard_map/ppermute | solution.py:326
  81.6 41.2 %collective-permute-start.23 = (bf16[3,32,1536]{2,1,0:T(8,128)(2,1)S(1)}, bf16[3,32,1536]{2,1,0:T(8,128)(2,1)S(1)}, u32[]{:S(2)}, u32[]{:S(2)}) collective-permute-start(bf16[3,32,1536]{2,1,0:T(8,128)(2,1)S(1)} %get-tuple-element.60), channel_id=1, source_target_pairs={{0,6},{2,12},{4,2},{6,8},{8,14},{10,4},{12,10},{14,0},{1,7},{3,13}... | collective-permute-start | bytes 884744 | tf_op jit(solution)/shard_map/ppermute | solution.py:326
  81.9 2.5 %collective-permute-start.9 = (bf16[256,384]{1,0:T(8,128)(2,1)S(1)}, bf16[256,384]{1,0:T(8,128)(2,1)S(1)}, u32[]{:S(2)}, u32[]{:S(2)}) collective-permute-start(bf16[256,384]{1,0:T(8,128)(2,1)S(1)} %copy-done.23), channel_id=1, source_target_pairs={{0,2},{2,0},{4,6},{6,4},{8,10},{10,8},{12,14},{14,12},{1,3},{3,1},... | collective-permute-start | bytes 589832 | tf_op jit(solution)/shard_map/ppermute | solution.py:29
  85.1 55.4 %collective-permute-start.24 = (bf16[3,32,1536]{2,1,0:T(8,128)(2,1)}, bf16[3,32,1536]{2,1,0:T(8,128)(2,1)}, u32[]{:S(2)}, u32[]{:S(2)}) collective-permute-start(bf16[3,32,1536]{2,1,0:T(8,128)(2,1)} %get-tuple-element.59), channel_id=1, source_target_pairs={{0,8},{2,10},{4,12},{6,14},{8,0},{10,2},{12,4},{14,6},{1,9},{3,11}... | collective-permute-start | bytes 884744 | tf_op jit(solution)/shard_map/ppermute | solution.py:326
  95.7 50.8 %collective-permute-start.25 = (bf16[3,32,1536]{2,1,0:T(8,128)(2,1)}, bf16[3,32,1536]{2,1,0:T(8,128)(2,1)}, u32[]{:S(2)}, u32[]{:S(2)}) collective-permute-start(bf16[3,32,1536]{2,1,0:T(8,128)(2,1)} %get-tuple-element.58), channel_id=1, source_target_pairs={{0,10},{2,8},{4,14},{6,12},{8,2},{10,0},{12,6},{14,4},{1,11},{3,9}... | collective-permute-start | bytes 884744 | tf_op jit(solution)/shard_map/ppermute | solution.py:326
  123.6 23.9 %collective-permute-start.26 = (bf16[3,32,1536]{2,1,0:T(8,128)(2,1)}, bf16[3,32,1536]{2,1,0:T(8,128)(2,1)}, u32[]{:S(2)}, u32[]{:S(2)}) collective-permute-start(bf16[3,32,1536]{2,1,0:T(8,128)(2,1)} %get-tuple-element.57), channel_id=1, source_target_pairs={{0,2},{2,0},{4,6},{6,4},{8,10},{10,8},{12,14},{14,12},{1,3},{3,1},... | collective-permute-start | bytes 884744 | tf_op jit(solution)/shard_map/ppermute | solution.py:326
  124.4 23.1 %collective-permute-start.20 = (bf16[3,32,1536]{2,1,0:T(8,128)(2,1)}, bf16[3,32,1536]{2,1,0:T(8,128)(2,1)}, u32[]{:S(2)}, u32[]{:S(2)}) collective-permute-start(bf16[3,32,1536]{2,1,0:T(8,128)(2,1)} %get-tuple-element.42), channel_id=1, source_target_pairs={{0,12},{2,6},{4,8},{6,2},{8,4},{10,14},{12,0},{14,10},{1,13},{3,7}... | collective-permute-start | bytes 884744 | tf_op jit(solution)/shard_map/ppermute | solution.py:326
  127.5 24.6 %collective-permute-start.21 = (bf16[3,32,1536]{2,1,0:T(8,128)(2,1)}, bf16[3,32,1536]{2,1,0:T(8,128)(2,1)}, u32[]{:S(2)}, u32[]{:S(2)}) collective-permute-start(bf16[3,32,1536]{2,1,0:T(8,128)(2,1)} %get-tuple-element.43), channel_id=1, source_target_pairs={{0,4},{2,14},{4,0},{6,10},{8,12},{10,6},{12,8},{14,2},{1,5},{3,15}... | collective-permute-start | bytes 884744 | tf_op jit(solution)/shard_map/ppermute | solution.py:326
  134.4 3.3 %copy-start.2 = (f32[512,384]{1,0:T(8,128)S(1)}, f32[512,384]{1,0:T(8,128)}, u32[]{:S(2)}) copy-start(f32[512,384]{1,0:T(8,128)} %get-tuple-element.54.kept_ref) | copy-start | bytes 2359300
  134.4 3.3 %copy-start.13 = (bf16[512,384]{1,0:T(8,128)(2,1)S(1)}, bf16[512,384]{1,0:T(8,128)(2,1)}, u32[]{:S(2)}) copy-start(bf16[512,384]{1,0:T(8,128)(2,1)} %copy-done.12) | copy-start | bytes 1179652
  137.7 14.4 %copy-start.17 = (bf16[3,32,1536]{2,1,0:T(8,128)(2,1)S(1)}, bf16[3,32,1536]{2,1,0:T(8,128)(2,1)}, u32[]{:S(2)}) copy-start(bf16[3,32,1536]{2,1,0:T(8,128)(2,1)} %copy-done.16) | copy-start | bytes 884740
  137.7 14.4 %copy-start.19 = (bf16[3,32,1536]{2,1,0:T(8,128)(2,1)S(1)}, bf16[3,32,1536]{2,1,0:T(8,128)(2,1)}, u32[]{:S(2)}) copy-start(bf16[3,32,1536]{2,1,0:T(8,128)(2,1)} %copy-done.18) | copy-start | bytes 884740
  138.7 30.8 %copy-start.6 = (bf16[1,1,256,1536]{3,2,1,0:T(8,128)(2,1)S(1)}, bf16[1,1,256,1536]{3,2,1,0:T(8,128)(2,1)}, u32[]{:S(2)}) copy-start(bf16[1,1,256,1536]{3,2,1,0:T(8,128)(2,1)} %param.9) | copy-start | bytes 2359300
  140.6 25.0 %collective-permute-start.17 = (bf16[256,384]{1,0:T(8,128)(2,1)S(1)}, bf16[256,384]{1,0:T(8,128)(2,1)S(1)}, u32[]{:S(2)}, u32[]{:S(2)}) collective-permute-start(bf16[256,384]{1,0:T(8,128)(2,1)S(1)} %get-tuple-element.39), channel_id=1, source_target_pairs={{0,4},{2,6},{4,0},{6,2},{8,12},{10,14},{12,8},{14,10},{1,5},{3,7},... | collective-permute-start | bytes 589832 | tf_op jit(solution)/shard_map/ppermute | solution.py:29
  146.5 19.0 %collective-permute-start.18 = (bf16[256,384]{1,0:T(8,128)(2,1)S(1)}, bf16[256,384]{1,0:T(8,128)(2,1)S(1)}, u32[]{:S(2)}, u32[]{:S(2)}) collective-permute-start(bf16[256,384]{1,0:T(8,128)(2,1)S(1)} %get-tuple-element.40), channel_id=1, source_target_pairs={{0,2},{2,0},{4,6},{6,4},{8,10},{10,8},{12,14},{14,12},{1,3},{3,1},... | collective-permute-start | bytes 589832 | tf_op jit(solution)/shard_map/ppermute | solution.py:29
  147.4 20.3 %collective-permute-start.19 = (bf16[256,384]{1,0:T(8,128)(2,1)S(1)}, bf16[256,384]{1,0:T(8,128)(2,1)S(1)}, u32[]{:S(2)}, u32[]{:S(2)}) collective-permute-start(bf16[256,384]{1,0:T(8,128)(2,1)S(1)} %get-tuple-element.41), channel_id=1, source_target_pairs={{0,6},{2,4},{4,2},{6,0},{8,14},{10,12},{12,10},{14,8},{1,7},{3,5},... | collective-permute-start | bytes 589832 | tf_op jit(solution)/shard_map/ppermute | solution.py:29
  157.6 2.0 %collective-permute-start.27 = (bf16[32,1536]{1,0:T(8,128)(2,1)S(1)}, bf16[32,1536]{1,0:T(8,128)(2,1)S(1)}, u32[]{:S(2)}, u32[]{:S(2)}) collective-permute-start(bf16[32,1536]{1,0:T(8,128)(2,1)S(1)} %get-tuple-element.46), channel_id=1, source_target_pairs={{0,2},{2,0},{4,6},{6,4},{8,10},{10,8},{12,14},{14,12},{1,3},{3,1},... | collective-permute-start | bytes 294920 | tf_op jit(solution)/shard_map/ppermute | solution.py:29
  157.7 5.7 %collective-permute-start.28 = (bf16[32,1536]{1,0:T(8,128)(2,1)S(1)}, bf16[32,1536]{1,0:T(8,128)(2,1)S(1)}, u32[]{:S(2)}, u32[]{:S(2)}) collective-permute-start(bf16[32,1536]{1,0:T(8,128)(2,1)S(1)} %get-tuple-element.47), channel_id=1, source_target_pairs={{0,4},{2,6},{4,0},{6,2},{8,12},{10,14},{12,8},{14,10},{1,5},{3,7},... | collective-permute-start | bytes 294920 | tf_op jit(solution)/shard_map/ppermute | solution.py:29
  159.6 17.2 %collective-permute-start.29 = (bf16[32,1536]{1,0:T(8,128)(2,1)S(1)}, bf16[32,1536]{1,0:T(8,128)(2,1)S(1)}, u32[]{:S(2)}, u32[]{:S(2)}) collective-permute-start(bf16[32,1536]{1,0:T(8,128)(2,1)S(1)} %get-tuple-element.48), channel_id=1, source_target_pairs={{0,6},{2,4},{4,2},{6,0},{8,14},{10,12},{12,10},{14,8},{1,7},{3,5},... | collective-permute-start | bytes 294920 | tf_op jit(solution)/shard_map/ppermute | solution.py:29
  163.3 13.6 %collective-permute-start.30 = (bf16[32,1536]{1,0:T(8,128)(2,1)S(1)}, bf16[32,1536]{1,0:T(8,128)(2,1)S(1)}, u32[]{:S(2)}, u32[]{:S(2)}) collective-permute-start(bf16[32,1536]{1,0:T(8,128)(2,1)S(1)} %get-tuple-element.49), channel_id=1, source_target_pairs={{0,8},{2,10},{4,12},{6,14},{8,0},{10,2},{12,4},{14,6},{1,9},{3,11}... | collective-permute-start | bytes 294920 | tf_op jit(solution)/shard_map/ppermute | solution.py:29
  165.5 12.9 %collective-permute-start.31 = (bf16[32,1536]{1,0:T(8,128)(2,1)S(1)}, bf16[32,1536]{1,0:T(8,128)(2,1)S(1)}, u32[]{:S(2)}, u32[]{:S(2)}) collective-permute-start(bf16[32,1536]{1,0:T(8,128)(2,1)S(1)} %get-tuple-element.50), channel_id=1, source_target_pairs={{0,10},{2,8},{4,14},{6,12},{8,2},{10,0},{12,6},{14,4},{1,11},{3,9}... | collective-permute-start | bytes 294920 | tf_op jit(solution)/shard_map/ppermute | solution.py:29
  165.6 12.9 %collective-permute-start.32 = (bf16[32,1536]{1,0:T(8,128)(2,1)S(1)}, bf16[32,1536]{1,0:T(8,128)(2,1)S(1)}, u32[]{:S(2)}, u32[]{:S(2)}) collective-permute-start(bf16[32,1536]{1,0:T(8,128)(2,1)S(1)} %get-tuple-element.51), channel_id=1, source_target_pairs={{0,12},{2,14},{4,8},{6,10},{8,4},{10,6},{12,0},{14,2},{1,13},{3,15... | collective-permute-start | bytes 294920 | tf_op jit(solution)/shard_map/ppermute | solution.py:29
  167.7 10.8 %collective-permute-start.33 = (bf16[32,1536]{1,0:T(8,128)(2,1)S(1)}, bf16[32,1536]{1,0:T(8,128)(2,1)S(1)}, u32[]{:S(2)}, u32[]{:S(2)}) collective-permute-start(bf16[32,1536]{1,0:T(8,128)(2,1)S(1)} %get-tuple-element.52), channel_id=1, source_target_pairs={{0,14},{2,12},{4,10},{6,8},{8,6},{10,4},{12,2},{14,0},{1,15},{3,13... | collective-permute-start | bytes 294920 | tf_op jit(solution)/shard_map/ppermute | solution.py:29
  174.8 1.4 copy-start.1
  (12 other events, 10.3 us)

commit v6 on v5

--- a/solution.py
+++ b/solution.py
@@ -99,7 +99,7 @@
     )(assignment, group.reshape(1), *on_chip(parts))
 
 
-def project_kernel(n_rows, scalar_ref, *refs):
+def project_kernel(n_rows, places, scalar_ref, *refs):
     near = scalar_ref[0]
     state_refs = refs[: 2 * n_rows]
     kept_ref, sent_ref = refs[-2:]
@@ -108,8 +108,8 @@
 
     def product(i, start):
         total = None
-        for j, weight_ref in enumerate(weight_refs):
-            state = state_refs[2 * i + j % 2][j // 2]
+        for (core, group, first), weight_ref in zip(places, weight_refs):
+            state = state_refs[2 * i + core][group, :, first : first + weight_ref.shape[0]]
             weight = weight_ref[:, pl.ds(pl.multiple_of(start, HDIM), cols)]
             part = jnp.dot(state, weight, preferred_element_type=F32)
             total = part if total is None else total + part
@@ -124,15 +124,16 @@
 def project(states, weights, near):
     _, rows, _ = states[0].shape
     n_rows = len(states) // 2
-    shape = (n_rows * rows, weights[0].shape[1] // 2)
-    return pl.pallas_call(
-        functools.partial(project_kernel, n_rows),
-        in_specs=[SMEM_SPEC] + [VMEM_SPEC] * (len(states) + len(weights)),
+    places, arrays = zip(*weights)
+    shape = (n_rows * rows, arrays[0].shape[1] // 2)
+    return pl.pallas_call(
+        functools.partial(project_kernel, n_rows, places),
+        in_specs=[SMEM_SPEC] + [VMEM_SPEC] * (len(states) + len(arrays)),
         out_specs=[VMEM_SPEC] * 2,
-        out_shape=[jax.ShapeDtypeStruct(shape, F32), pltpu.VMEM(shape, BF16)],
+        out_shape=[pltpu.HBM(shape, F32), pltpu.VMEM(shape, BF16)],
         compiler_params=MODEST,
         name="project",
-    )(near.reshape(1), *states, *weights[:2], *on_chip(*weights[2:]))
+    )(near.reshape(1), *states, *arrays)
 
 
 def spatial_kernel(qkv_ref, residual_ref, out_ref):
@@ -199,26 +200,35 @@
     )(core.reshape(1), *pieces)
 
 
-def weigh_kernel(bias_ref, kept_ref, come_ref, *refs):
+def weigh_kernel(sides, rows_side, scalar_ref, assignment_ref, length_ref, kept_ref, come_ref, *refs):
     query_refs, out_ref = refs[:-1], refs[-1]
+    group, side = scalar_ref[0], scalar_ref[1]
+    length = length_ref[assignment_ref[group]]
+    total = kept_ref.shape[0]
+    row = lax.broadcasted_iota(jnp.int32, (1, total), 1)
+    each = total // sides
+    which, inner = lax.div(row, each), lax.rem(row, each)
+    source, inner = lax.div(inner, rows_side), lax.rem(inner, rows_side)
+    position = (source * sides + (which ^ side)) * rows_side + inner
+    bias = jnp.where(position < length, 0.0, -1e9).astype(F32)
     for head in range(out_ref.shape[0]):
         at = lanes(head)
         key_rows = (kept_ref[:, at] + come_ref[:, at].astype(F32)).astype(BF16)
         for j, query_ref in enumerate(query_refs):
-            out_ref[head, j] = softmax(scores_of(query_ref[:, at], key_rows) + bias_ref[...])
-
-
-def cross_weights(bias, kept, come, queries):
+            out_ref[head, j] = softmax(scores_of(query_ref[:, at], key_rows) + bias)
+
+
+def cross_weights(place, assignment, lengths, sides, rows_side, kept, come, queries):
     rows, width = kept.shape
     tokens = queries[0].shape[0]
     return pl.pallas_call(
-        weigh_kernel,
-        in_specs=[VMEM_SPEC] * (3 + len(queries)),
+        functools.partial(weigh_kernel, sides, rows_side),
+        in_specs=[SMEM_SPEC] * 3 + [VMEM_SPEC] * (2 + len(queries)),
         out_specs=VMEM_SPEC,
         out_shape=pltpu.VMEM((width // HDIM, len(queries), tokens, rows), BF16),
         compiler_params=MODEST,
         name="cross_weights",
-    )(bias, kept, *on_chip(come), *queries)
+    )(place, assignment, lengths, kept, *on_chip(come), *queries)
 
 
 def value_kernel(weight_ref, kept_ref, come_ref, *out_refs):
@@ -305,7 +315,6 @@
     feats = kv_weight.shape[0]
     _, rows_here, _ = prompt_states.shape
     rows_side = rows_here // sides
-    rows = seq * rows_side
 
     parts = prompt_blocks(prompt_states, side, sides, seq)
     parts = lax.all_to_all(parts, "seq", 0, 0, tiled=True)
@@ -326,23 +335,37 @@
         pieces.append(lax.ppermute(blocks[number], "seq", pairs))
 
     half = width // 2
+    cut = feats // 2 if feats % (2 * HDIM) == 0 else 0
+    across = [(g, q) for g in range(grp) for q in range(seq)]
+
+    def halves(source, kind, first, count):
+        parts = (
+            lax.dynamic_slice(source, (kind, first, c * half), (1, count, half)) for c in (core, 1 - core)
+        )
+        return tuple(part.reshape(count, half) for part in parts)
+
+    early = []
+    if cut:
+        for k in range(1, grp):
+            early.append(swap(kv_weight[:cut], "grp", k))
     planes = lax.optimization_barrier(kv_weight.transpose(1, 0, 2))
-    across = [(g, q) for g in range(grp) for q in range(seq)]
-
-    def halves(source, kind):
-        cut = (lax.dynamic_slice(source, (kind, 0, c * half), (1, feats, half)) for c in (core, 1 - core))
-        return tuple(c.reshape(feats, half) for c in cut)
-
-    keys = halves(planes, 0)
-    later, keys = lax.optimization_barrier((planes, keys))
-    weights = [keys, halves(later, 1)]
+    weights, later = [], planes
     for kind in range(2):
-        mine, theirs = weights[kind]
-        weights[kind] = [mine, swap(theirs, "seq", 1)]
+        weights.append([])
+        mine, theirs = halves(later, kind, cut, feats - cut)
         for k in range(1, grp):
             for c, part in enumerate((mine, theirs)):
                 pairs = [(g * seq + q, (g ^ k) * seq + (q ^ c)) for g, q in across]
-                weights[kind].append(lax.ppermute(part, ("grp", "seq"), pairs))
+                weights[kind].append(((c, k, cut), lax.ppermute(part, ("grp", "seq"), pairs)))
+        later, _ = lax.optimization_barrier((later, (mine, theirs)))
+    for kind in range(2):
+        mine, theirs = halves(later, kind, 0, feats)
+        weights[kind] += [((0, 0, 0), mine), ((1, 0, 0), swap(theirs, "seq", 1))]
+    for k, come in enumerate(early, 1):
+        come = lax.optimization_barrier(come.transpose(1, 0, 2))
+        for kind in range(2):
+            mine, theirs = halves(come, kind, 0, cut)
+            weights[kind] += [((0, k, 0), mine), ((1, k, 0), swap(theirs, "seq", 1))]
 
     slots = pick_slots(assignment, group, parts, grp)
     wanted = jnp.stack([slots[0]] + [swap(slots[k], "grp", k) for k in range(1, grp)])
@@ -373,13 +396,6 @@
                 kept = kept + come.astype(F32)
         sums.append((kept, come))
 
-    row = jnp.arange(rows * sides)
-    which, source, inner = row // rows, (row % rows) // rows_side, row % rows_side
-    position = source * rows_here + (which ^ side) * rows_side + inner
-    served = lax.dynamic_index_in_dim(assignment, group, keepdims=False)
-    length = lax.dynamic_index_in_dim(prompt_lengths, served, keepdims=False)
-    bias = jnp.where(position < length, 0.0, -1e9).astype(F32)[None]
-
     base = spatial_attention(qkv, residual[0, 0])
     plan = []
     for here in range(2):
@@ -390,7 +406,8 @@
     for k in range(1, seq):
         returned.append(swap(moved[k], "seq", k))
 
-    shares = cross_weights(bias, *sums[0], queries)
+    device = jnp.stack([group, side]).astype(jnp.int32)
+    shares = cross_weights(device, assignment, prompt_lengths, sides, rows_side, *sums[0], queries)
     crossed = cross_values(shares, *sums[1])
     results = [crossed[0]]
     for k in range(1, 4):

time: 182 us -> 184 us (1.011)
  waiting for transfers between devices: 66.5 us -> 88.2 us
  starting transfers between devices: 64.8 us -> 52.6 us
  local copies, waits for them, and re-layouts: 19.9 us -> 13.8 us
  between operations: 2.26 us -> 0.23 us
    ppermute x23 -> x26, waiting for transfers between devices: 23.8 us -> 56.4 us  [swap(): return lax.ppermute(value, axis, pairs)]
    ppermute x7, starting transfers between devices: 32.8 us -> 19.2 us  [block(): pieces.append(lax.ppermute(blocks[number], 'seq', pairs))]
    ppermute x4, waiting for transfers between devices: 14.8 us -> 5.74 us  [block(): lax.ppermute(part, ('grp', 'seq'), pairs)]
    unnamed x51 -> x32, local copies, waits for them, and re-layouts: 13.7 us -> 6.89 us
    ppermute x23 -> x26, starting transfers between devices: 19.4 us -> 23.6 us  [swap(): return lax.ppermute(value, axis, pairs)]
    reshape x2 -> x4, local copies, waits for them, and re-layouts: 0.86 us -> 3.73 us  [halves(): return tuple((part.reshape(count, half) for part in parts))]
    ppermute x4, starting transfers between devices: 6.17 us -> 3.43 us  [block(): lax.ppermute(part, ('grp', 'seq'), pairs)]
  transfers between devices with their start and end apart: 35 -> 38, of which waited for: 15 -> 15; matrix products, arithmetic and copies ran while one was open for 6% -> 7% of each run, Pallas kernels for 11% -> 12%
where the time goes in v6:
time: 184 us; the launch traced here: 180 us
  waiting for transfers between devices  88.2 us (48%)
  starting transfers between devices  52.6 us (29%)
  Pallas kernels  23.1 us (13%)
  local copies, waits for them, and re-layouts  13.8 us (8%)
  other arithmetic  2.39 us (1%)
    ppermute x26, waiting for transfers between devices, swap(): return lax.ppermute(value, axis, pairs)  56.4 us
    ppermute x26, starting transfers between devices, swap(): return lax.ppermute(value, axis, pairs)  23.6 us
    ppermute x7, starting transfers between devices, block(): pieces.append(lax.ppermute(blocks[number], 'seq', pairs))  19.2 us
    ppermute x7, waiting for transfers between devices, block(): pieces.append(lax.ppermute(blocks[number], 'seq', pairs))  18.9 us
    all_to_all x1, waiting for transfers between devices, block(): parts = lax.all_to_all(parts, 'seq', 0, 0, tiled=True)  7.24 us
    unnamed x32, local copies, waits for them, and re-layouts  6.89 us
    all_to_all x1, starting transfers between devices, block(): parts = lax.all_to_all(parts, 'seq', 0, 0, tiled=True)  6.35 us
    pallas_call x2, Pallas kernels, project(): pl.pallas_call(functools.partial(project_kernel, n_rows, places), in_spec...  6.1 us
  transfers between devices with their start and end apart: 38, of which 15 were waited for; matrix products, arithmetic and copies ran while one was open for 7% of the time, Pallas kernels for 12%

profile of v6, /device:TPU:0, one launch (start us, length us, event | category | flops | bytes accessed | tf_op | source)
XLA Modules:
  0.0 180.3 jit_solution(235825597761187977)
XLA Ops:
  0.0 1.0 copy-done.7
  1.8 6.4 %all-to-all-start = ((bf16[8,2,32,256]{3,2,1,0:T(8,128)(2,1)}), bf16[8,2,32,256]{3,2,1,0:T(8,128)(2,1)S(1)}, u32[]{:S(2)}, u32[]{:S(2)}) async-start(bf16[8,2,32,256]{3,2,1,0:T(8,128)(2,1)} %prompt_blocks.1), calls=%async_computation | async-start | bytes 524288 | tf_op jit(solution)/shard_map/all_to_all | solution.py:320
  8.1 1.0 copy.11
  9.1 1.5 collective-permute-start.7
  10.6 7.2 %all-to-all-done.parts_ref = bf16[8,2,32,256]{3,2,1,0:T(8,128)(2,1)S(1)} async-done(((bf16[8,2,32,256]{3,2,1,0:T(8,128)(2,1)}), bf16[8,2,32,256]{3,2,1,0:T(8,128)(2,1)S(1)}, u32[]{:S(2)}, u32[]{:S(2)}) %all-to-all-start) | async-done | bytes 262176 | tf_op jit(solution)/shard_map/all_to_all | solution.py:320
  18.4 1.6 collective-permute-start
  19.9 1.6 copy.12
  22.3 9.7 %collective-permute-done = bf16[256,256]{1,0:T(8,128)(2,1)S(1)} collective-permute-done((bf16[256,256]{1,0:T(8,128)(2,1)S(1)}, bf16[256,256]{1,0:T(8,128)(2,1)S(1)}, u32[]{:S(2)}, u32[]{:S(2)}) %collective-permute-start) | collective-permute-done | bytes 131104 | tf_op jit(solution)/shard_map/ppermute | solution.py:29
  32.1 1.6 collective-permute-start.2
  34.6 1.5 collective-permute-start.14
  36.7 3.3 %collective-permute-done.2.refs_2_ = bf16[2,256,256]{2,1,0:T(8,128)(2,1)S(1)} collective-permute-done((bf16[2,256,256]{2,1,0:T(8,128)(2,1)S(1)}, bf16[2,256,256]{2,1,0:T(8,128)(2,1)S(1)}, u32[]{:S(2)}, u32[]{:S(2)}) %collective-permute-start.2) | collective-permute-done | bytes 262176 | tf_op jit(solution)/shard_map/ppermute | solution.py:29
  40.0 2.0 %dynamic-slice_bitcast_fusion.7 = (bf16[128,768]{1,0:T(8,128)(2,1)S(1)}, bf16[128,768]{1,0:T(8,128)(2,1)S(1)}, bf16[128,768]{1,0:T(8,128)(2,1)}, bf16[128,768]{1,0:T(8,128)(2,1)}) fusion(bf16[2,128,1536]{2,1,0:T(8,128)(2,1)} %bitcast.17, s32[]{:T(128)S(6)} %select_n.69, s32[]{:T(128)S(6)} %select_n.68), kind=kLoop, calls=%fused_computation.10 | loop fusion | bytes 1572872 | tf_op jit(solution)/shard_map/reshape | solution.py:345
  42.5 3.1 %collective-permute-done.15.refs_5_ = bf16[128,768]{1,0:T(8,128)(2,1)S(1)} collective-permute-done((bf16[128,768]{1,0:T(8,128)(2,1)S(1)}, bf16[128,768]{1,0:T(8,128)(2,1)S(1)}, u32[]{:S(2)}, u32[]{:S(2)}) %collective-permute-start.15) | collective-permute-done | bytes 196640 | tf_op jit(solution)/shard_map/ppermute | solution.py:359
  45.9 1.5 collective-permute-start.4
  48.1 2.4 %project.3 = (f32[512,384]{1,0:T(8,128)}, bf16[512,384]{1,0:T(8,128)(2,1)}) custom-call(s32[1]{0:T(128)} %bitcast.7.scalar_ref, bf16[2,256,256]{2,1,0:T(8,128)(2,1)S(1)} %pad_maximum_fusion.refs_0_, bf16[2,256,256]{2,1,0:T(8,128)(2,1)S(1)} %collective-permute-done.1.refs_1_, bf16[2,256,256]{2,1,0:T(8,128)(2,1)S(1)} %collective-permute-done.2.refs_2_, ...), custom_call_target="tpu_custom_call" | custom-call | tf_op jit(solution)/shard_map/project/pallas_call | solution.py:129
  50.5 1.6 collective-permute-start.18
  52.1 2.1 %dynamic-slice_bitcast_fusion.9 = (bf16[256,384]{1,0:T(8,128)(2,1)}, bf16[256,384]{1,0:T(8,128)(2,1)}, bf16[256,384]{1,0:T(8,128)(2,1)}, bf16[256,384]{1,0:T(8,128)(2,1)}) fusion(bf16[1,1,256,1536]{3,2,1,0:T(8,128)(2,1)} %param.8, s32[]{:T(128)S(6)} %select_n.73, s32[]{:T(128)S(6)} %select_n.71, s32[]{:T(128)S(6)} %select_n.70, s32[]{:T(128)S(6)} %select_n.72), kind=kLoop, calls=%fused_computation.12 | loop fusion | bytes 1572880 | tf_op jit(solution)/shard_map/dynamic_slice | solution.py:384
  54.4 2.4 %collective-permute-done.5.refs_5_ = bf16[128,768]{1,0:T(8,128)(2,1)} collective-permute-done((bf16[128,768]{1,0:T(8,128)(2,1)}, bf16[128,768]{1,0:T(8,128)(2,1)}, u32[]{:S(2)}, u32[]{:S(2)}) %collective-permute-start.5) | collective-permute-done | bytes 196640 | tf_op jit(solution)/shard_map/ppermute | solution.py:359
  56.7 1.6 collective-permute-start.12
  58.4 0.9 copy-done.3
  59.3 0.9 copy-done.6
  60.2 3.7 %project.2 = (f32[512,384]{1,0:T(8,128)}, bf16[512,384]{1,0:T(8,128)(2,1)}) custom-call(s32[1]{0:T(128)} %bitcast.7.scalar_ref, bf16[2,256,256]{2,1,0:T(8,128)(2,1)S(1)} %pad_maximum_fusion.refs_0_, bf16[2,256,256]{2,1,0:T(8,128)(2,1)S(1)} %collective-permute-done.1.refs_1_, bf16[2,256,256]{2,1,0:T(8,128)(2,1)S(1)} %collective-permute-done.2.refs_2_, ...), custom_call_target="tpu_custom_call" | custom-call | tf_op jit(solution)/shard_map/project/pallas_call | solution.py:129
  65.2 1.2 fusion
  66.4 2.6 %collective-permute-start.19 = (bf16[512,384]{1,0:T(8,128)(2,1)S(1)}, bf16[512,384]{1,0:T(8,128)(2,1)S(1)}, u32[]{:S(2)}, u32[]{:S(2)}) collective-permute-start(bf16[512,384]{1,0:T(8,128)(2,1)S(1)} %get-tuple-element.51), channel_id=1, source_target_pairs={{0,8},{2,10},{4,12},{6,14},{8,0},{10,2},{12,4},{14,6},{1,9},{3,11}... | collective-permute-start | bytes 1179656 | tf_op jit(solution)/shard_map/ppermute | solution.py:29
  69.0 14.0 %collective-permute-done.9 = bf16[512,384]{1,0:T(8,128)(2,1)} collective-permute-done((bf16[512,384]{1,0:T(8,128)(2,1)}, bf16[512,384]{1,0:T(8,128)(2,1)}, u32[]{:S(2)}, u32[]{:S(2)}) %collective-permute-start.9) | collective-permute-done | bytes 393248 | tf_op jit(solution)/shard_map/ppermute | solution.py:29
  83.0 1.1 fusion.1
  84.4 1.0 collective-permute-start.25
  86.2 1.7 collective-permute-start.13
  87.9 24.6 %collective-permute-done.13.refs_3_ = bf16[256,384]{1,0:T(8,128)(2,1)S(1)} collective-permute-done((bf16[256,384]{1,0:T(8,128)(2,1)S(1)}, bf16[256,384]{1,0:T(8,128)(2,1)S(1)}, u32[]{:S(2)}, u32[]{:S(2)}) %collective-permute-start.13) | collective-permute-done | bytes 196640 | tf_op jit(solution)/shard_map/ppermute | solution.py:29
  112.5 2.0 %collective-permute-start.27 = (bf16[3,32,1536]{2,1,0:T(8,128)(2,1)S(1)}, bf16[3,32,1536]{2,1,0:T(8,128)(2,1)S(1)}, u32[]{:S(2)}, u32[]{:S(2)}) collective-permute-start(bf16[3,32,1536]{2,1,0:T(8,128)(2,1)S(1)} %get-tuple-element.57), channel_id=1, source_target_pairs={{0,8},{2,10},{4,12},{6,14},{8,0},{10,2},{12,4},{14,6},{1,9},{3,11}... | collective-permute-start | bytes 884744 | tf_op jit(solution)/shard_map/ppermute | solution.py:335
  114.5 14.3 %collective-permute-start.28 = (bf16[3,32,1536]{2,1,0:T(8,128)(2,1)S(1)}, bf16[3,32,1536]{2,1,0:T(8,128)(2,1)S(1)}, u32[]{:S(2)}, u32[]{:S(2)}) collective-permute-start(bf16[3,32,1536]{2,1,0:T(8,128)(2,1)S(1)} %get-tuple-element.56), channel_id=1, source_target_pairs={{0,10},{2,8},{4,14},{6,12},{8,2},{10,0},{12,6},{14,4},{1,11},{3,9}... | collective-permute-start | bytes 884744 | tf_op jit(solution)/shard_map/ppermute | solution.py:335
  128.8 1.1 collective-permute-start.23
  130.0 3.2 %cross_weights.1.weight_ref = bf16[3,4,256,512]{3,2,1,0:T(8,128)(2,1)S(1)} custom-call(s32[2]{0:T(128)S(1)} %pad_add_fusion.scalar_ref, s32[2]{0:T(128)S(1)} %copy-done.8, s32[2]{0:T(128)S(1)} %copy-done.9, f32[512,384]{1,0:T(8,128)S(1)} %get-tuple-element.54.kept_ref, bf16[512,384]{1,0:T(8,128)(2,1)S(1)} %collective-permute-done.10.come_ref, ...), custom_call_target="tpu_custom_call" | custom-call | tf_op jit(solution)/shard_map/cross_weights/pallas_call | solution.py:224
  133.2 1.0 cross_values.1
  134.2 3.5 %collective-permute-done.27.refs_5_ = bf16[3,32,1536]{2,1,0:T(8,128)(2,1)S(1)} collective-permute-done((bf16[3,32,1536]{2,1,0:T(8,128)(2,1)S(1)}, bf16[3,32,1536]{2,1,0:T(8,128)(2,1)S(1)}, u32[]{:S(2)}, u32[]{:S(2)}) %collective-permute-start.27) | collective-permute-done | bytes 294944 | tf_op jit(solution)/shard_map/ppermute | solution.py:335
  137.7 10.8 %collective-permute-done.28.refs_6_ = bf16[3,32,1536]{2,1,0:T(8,128)(2,1)S(1)} collective-permute-done((bf16[3,32,1536]{2,1,0:T(8,128)(2,1)S(1)}, bf16[3,32,1536]{2,1,0:T(8,128)(2,1)S(1)}, u32[]{:S(2)}, u32[]{:S(2)}) %collective-permute-start.28) | collective-permute-done | bytes 294944 | tf_op jit(solution)/shard_map/ppermute | solution.py:335
  148.6 1.1 collective-permute-start.22
  149.7 4.6 %collective-permute-done.24.refs_2_ = bf16[3,32,1536]{2,1,0:T(8,128)(2,1)S(1)} collective-permute-done((bf16[3,32,1536]{2,1,0:T(8,128)(2,1)S(1)}, bf16[3,32,1536]{2,1,0:T(8,128)(2,1)S(1)}, u32[]{:S(2)}, u32[]{:S(2)}) %collective-permute-start.24) | collective-permute-done | bytes 294944 | tf_op jit(solution)/shard_map/ppermute | solution.py:335
  154.3 4.7 %temporal.1 = (bf16[32,1536]{1,0:T(8,128)(2,1)S(1)}, bf16[32,1536]{1,0:T(8,128)(2,1)S(1)}, bf16[32,1536]{1,0:T(8,128)(2,1)S(1)}, bf16[32,1536]{1,0:T(8,128)(2,1)...) custom-call(s32[1]{0:T(128)} %bitcast.28.scalar_ref, ...), custom_call_target="tpu_custom_call" | custom-call | tf_op jit(solution)/shard_map/temporal/pallas_call | solution.py:189
  159.0 1.2 collective-permute-start.31
  160.3 0.9 collective-permute-start.32
  161.2 3.5 %collective-permute-done.31.refs_2_ = bf16[32,1536]{1,0:T(8,128)(2,1)S(1)} collective-permute-done((bf16[32,1536]{1,0:T(8,128)(2,1)S(1)}, bf16[32,1536]{1,0:T(8,128)(2,1)S(1)}, u32[]{:S(2)}, u32[]{:S(2)}) %collective-permute-start.31) | collective-permute-done | bytes 98336 | tf_op jit(solution)/shard_map/ppermute | solution.py:29
  164.7 2.9 %collective-permute-start.33 = (bf16[32,1536]{1,0:T(8,128)(2,1)S(1)}, bf16[32,1536]{1,0:T(8,128)(2,1)S(1)}, u32[]{:S(2)}, u32[]{:S(2)}) collective-permute-start(bf16[32,1536]{1,0:T(8,128)(2,1)S(1)} %get-tuple-element.47), channel_id=1, source_target_pairs={{0,8},{2,10},{4,12},{6,14},{8,0},{10,2},{12,4},{14,6},{1,9},{3,11}... | collective-permute-start | bytes 294920 | tf_op jit(solution)/shard_map/ppermute | solution.py:29
  167.6 1.3 collective-permute-start.35
  168.9 2.0 %collective-permute-start.36 = (bf16[32,1536]{1,0:T(8,128)(2,1)S(1)}, bf16[32,1536]{1,0:T(8,128)(2,1)S(1)}, u32[]{:S(2)}, u32[]{:S(2)}) collective-permute-start(bf16[32,1536]{1,0:T(8,128)(2,1)S(1)} %get-tuple-element.50), channel_id=1, source_target_pairs={{0,14},{2,12},{4,10},{6,8},{8,6},{10,4},{12,2},{14,0},{1,15},{3,13... | collective-permute-start | bytes 294920 | tf_op jit(solution)/shard_map/ppermute | solution.py:29
  170.9 5.3 %spatial.1.base_ref = f32[256,1536]{1,0:T(8,128)} custom-call(bf16[3,256,1536]{2,1,0:T(8,128)(2,1)S(1)} %bitcast.62, bf16[256,1536]{1,0:T(8,128)(2,1)S(1)} %bitcast.63), custom_call_target="tpu_custom_call" | custom-call | tf_op jit(solution)/shard_map/spatial/pallas_call | solution.py:150
  176.2 1.4 copy-done.1
  179.3 1.0 final.1
  (83 shorter events, 9.5 us)
Async XLA Ops:
  1.0 7.1 %slice-start = ((bf16[256,2,1536]{2,1,0:T(2,128)(2,1)}), bf16[128,2,1536]{2,1,0:T(2,128)(2,1)S(1)}, s32[]{:S(2)}) async-start(bf16[256,2,1536]{2,1,0:T(2,128)(2,1)} %param.11), calls=%async_computation.1 | async-start | bytes 1572864 | tf_op jit(solution)/shard_map/slice | solution.py:350
  1.8 16.1 %all-to-all-start = ((bf16[8,2,32,256]{3,2,1,0:T(8,128)(2,1)}), bf16[8,2,32,256]{3,2,1,0:T(8,128)(2,1)S(1)}, u32[]{:S(2)}, u32[]{:S(2)}) async-start(bf16[8,2,32,256]{3,2,1,0:T(8,128)(2,1)} %prompt_blocks.1), calls=%async_computation | async-start | bytes 524288 | tf_op jit(solution)/shard_map/all_to_all | solution.py:320
  8.1 9.7 %copy-start.8 = (s32[2]{0:T(128)S(1)}, s32[2]{0:T(128)}, u32[]{:S(2)}) copy-start(s32[2]{0:T(128)} %assignment_ref.3) | copy-start | bytes 28
  9.1 27.3 %collective-permute-start.7 = (bf16[128,2,1536]{2,0,1:T(8,128)(2,1)}, bf16[128,2,1536]{2,0,1:T(8,128)(2,1)}, u32[]{:S(2)}, u32[]{:S(2)}) collective-permute-start(bf16[128,2,1536]{2,0,1:T(8,128)(2,1)} %copy.11), channel_id=1, source_target_pairs={{0,16},{16,0},{1,17},{17,1},{2,18},{18,2},{3,19},{19,3},{4,20},{20... | collective-permute-start | bytes 2359304 | tf_op jit(solution)/shard_map/ppermute | solution.py:29
  18.4 13.7 %collective-permute-start = (bf16[256,256]{1,0:T(8,128)(2,1)S(1)}, bf16[256,256]{1,0:T(8,128)(2,1)S(1)}, u32[]{:S(2)}, u32[]{:S(2)}) collective-permute-start(bf16[256,256]{1,0:T(8,128)(2,1)S(1)} %get-tuple-element.29), channel_id=1, source_target_pairs={{0,16},{16,0},{1,17},{17,1},{2,18},{18,2},{3,19},{19,3},{4,20},{20... | collective-permute-start | bytes 393224 | tf_op jit(solution)/shard_map/ppermute | solution.py:29
  32.1 7.9 %collective-permute-start.2 = (bf16[2,256,256]{2,1,0:T(8,128)(2,1)S(1)}, bf16[2,256,256]{2,1,0:T(8,128)(2,1)S(1)}, u32[]{:S(2)}, u32[]{:S(2)}) collective-permute-start(bf16[2,256,256]{2,1,0:T(8,128)(2,1)S(1)} %pad_maximum_fusion.refs_0_), channel_id=1, source_target_pairs={{0,1},{1,0},{2,3},{3,2},{4,5},{5,4},{6,7},{7,6},{8,9},{9,8},{10,11... | collective-permute-start | bytes 786440 | tf_op jit(solution)/shard_map/ppermute | solution.py:29
  34.6 11.4 %collective-permute-start.16 = (bf16[256,768]{1,0:T(8,128)(2,1)S(1)}, bf16[256,768]{1,0:T(8,128)(2,1)S(1)}, u32[]{:S(2)}, u32[]{:S(2)}) collective-permute-start(bf16[256,768]{1,0:T(8,128)(2,1)S(1)} %get-tuple-element.63), channel_id=1, source_target_pairs={{0,2},{2,0},{4,6},{6,4},{8,10},{10,8},{12,14},{14,12},{1,3},{3,1},... | collective-permute-start | bytes 1179656 | tf_op jit(solution)/shard_map/ppermute | solution.py:29
  34.6 7.8 %collective-permute-start.14 = (bf16[128,768]{1,0:T(8,128)(2,1)S(1)}, bf16[128,768]{1,0:T(8,128)(2,1)S(1)}, u32[]{:S(2)}, u32[]{:S(2)}) collective-permute-start(bf16[128,768]{1,0:T(8,128)(2,1)S(1)} %get-tuple-element.68), channel_id=1, source_target_pairs={{0,16},{2,18},{4,20},{6,22},{8,24},{10,26},{12,28},{14,30},{16,0},... | collective-permute-start | bytes 589832 | tf_op jit(solution)/shard_map/ppermute | solution.py:359
  36.1 9.6 %collective-permute-start.15 = (bf16[128,768]{1,0:T(8,128)(2,1)S(1)}, bf16[128,768]{1,0:T(8,128)(2,1)S(1)}, u32[]{:S(2)}, u32[]{:S(2)}) collective-permute-start(bf16[128,768]{1,0:T(8,128)(2,1)S(1)} %get-tuple-element.67), channel_id=1, source_target_pairs={{0,18},{2,16},{4,22},{6,20},{8,26},{10,24},{12,30},{14,28},{16,2},... | collective-permute-start | bytes 589832 | tf_op jit(solution)/shard_map/ppermute | solution.py:359
  36.4 11.0 %collective-permute-start.1 = (bf16[2,256,256]{2,1,0:T(8,128)(2,1)S(1)}, bf16[2,256,256]{2,1,0:T(8,128)(2,1)S(1)}, u32[]{:S(2)}, u32[]{:S(2)}) collective-permute-start(bf16[2,256,256]{2,1,0:T(8,128)(2,1)S(1)} %pad_maximum_fusion.refs_0_), channel_id=1, source_target_pairs={{0,2},{2,0},{4,6},{6,4},{8,10},{10,8},{12,14},{14,12},{1,3},{3,1},... | collective-permute-start | bytes 786440 | tf_op jit(solution)/shard_map/ppermute | solution.py:29
  40.0 8.1 %collective-permute-start.3 = (bf16[2,256,256]{2,1,0:T(8,128)(2,1)S(1)}, bf16[2,256,256]{2,1,0:T(8,128)(2,1)S(1)}, u32[]{:S(2)}, u32[]{:S(2)}) collective-permute-start(bf16[2,256,256]{2,1,0:T(8,128)(2,1)S(1)} %collective-permute-done.2.refs_2_), channel_id=1, source_target_pairs={{0,2},{2,0},{4,6},{6,4},{8,10},{10,8},{12,14},{14,12},{1,3},{3,1},... | collective-permute-start | bytes 786440 | tf_op jit(solution)/shard_map/ppermute | solution.py:29
  42.3 5.2 %collective-permute-start.17 = (bf16[128,768]{1,0:T(8,128)(2,1)S(1)}, bf16[128,768]{1,0:T(8,128)(2,1)S(1)}, u32[]{:S(2)}, u32[]{:S(2)}) collective-permute-start(bf16[128,768]{1,0:T(8,128)(2,1)S(1)} %get-tuple-element.71), channel_id=1, source_target_pairs={{0,2},{2,0},{4,6},{6,4},{8,10},{10,8},{12,14},{14,12},{1,3},{3,1},... | collective-permute-start | bytes 589832 | tf_op jit(solution)/shard_map/ppermute | solution.py:29
  45.6 12.7 %collective-permute-start.6 = (bf16[256,768]{1,0:T(8,128)(2,1)}, bf16[256,768]{1,0:T(8,128)(2,1)}, u32[]{:S(2)}, u32[]{:S(2)}) collective-permute-start(bf16[256,768]{1,0:T(8,128)(2,1)} %get-tuple-element.65), channel_id=1, source_target_pairs={{0,2},{2,0},{4,6},{6,4},{8,10},{10,8},{12,14},{14,12},{1,3},{3,1},... | collective-permute-start | bytes 1179656 | tf_op jit(solution)/shard_map/ppermute | solution.py:29
  45.9 8.4 %collective-permute-start.4 = (bf16[128,768]{1,0:T(8,128)(2,1)}, bf16[128,768]{1,0:T(8,128)(2,1)}, u32[]{:S(2)}, u32[]{:S(2)}) collective-permute-start(bf16[128,768]{1,0:T(8,128)(2,1)} %get-tuple-element.70), channel_id=1, source_target_pairs={{0,16},{2,18},{4,20},{6,22},{8,24},{10,26},{12,28},{14,30},{16,0},... | collective-permute-start | bytes 589832 | tf_op jit(solution)/shard_map/ppermute | solution.py:359
  47.4 9.3 %collective-permute-start.5 = (bf16[128,768]{1,0:T(8,128)(2,1)}, bf16[128,768]{1,0:T(8,128)(2,1)}, u32[]{:S(2)}, u32[]{:S(2)}) collective-permute-start(bf16[128,768]{1,0:T(8,128)(2,1)} %get-tuple-element.69), channel_id=1, source_target_pairs={{0,18},{2,16},{4,22},{6,20},{8,26},{10,24},{12,30},{14,28},{16,2},... | collective-permute-start | bytes 589832 | tf_op jit(solution)/shard_map/ppermute | solution.py:359
  47.5 10.9 %collective-permute-start.8 = (bf16[128,768]{1,0:T(8,128)(2,1)}, bf16[128,768]{1,0:T(8,128)(2,1)}, u32[]{:S(2)}, u32[]{:S(2)}) collective-permute-start(bf16[128,768]{1,0:T(8,128)(2,1)} %get-tuple-element.73), channel_id=1, source_target_pairs={{0,2},{2,0},{4,6},{6,4},{8,10},{10,8},{12,14},{14,12},{1,3},{3,1},... | collective-permute-start | bytes 589832 | tf_op jit(solution)/shard_map/ppermute | solution.py:29
  48.1 4.1 %copy-start.2 = (bf16[2,256,256]{2,1,0:T(8,128)(2,1)}, bf16[2,256,256]{2,1,0:T(8,128)(2,1)S(1)}, u32[]{:S(2)}) copy-start(bf16[2,256,256]{2,1,0:T(8,128)(2,1)S(1)} %collective-permute-done.3.refs_3_) | copy-start | bytes 786436
  50.5 14.7 %collective-permute-start.18 = (bf16[512,384]{1,0:T(8,128)(2,1)}, bf16[512,384]{1,0:T(8,128)(2,1)}, u32[]{:S(2)}, u32[]{:S(2)}) collective-permute-start(bf16[512,384]{1,0:T(8,128)(2,1)} %get-tuple-element.35), channel_id=1, source_target_pairs={{0,4},{2,6},{4,0},{6,2},{8,12},{10,14},{12,8},{14,10},{1,5},{3,7},... | collective-permute-start | bytes 1179656 | tf_op jit(solution)/shard_map/ppermute | solution.py:29
  54.3 10.0 %copy-start = (bf16[1,1,256,3,1536]{4,2,3,1,0:T(8,128)(2,1)S(1)}, bf16[1,1,256,3,1536]{4,2,3,1,0:T(8,128)(2,1)}, u32[]{:S(2)}) copy-start(bf16[1,1,256,3,1536]{4,2,3,1,0:T(8,128)(2,1)} %param.7) | copy-start | bytes 7077892
  54.3 31.1 %collective-permute-start.11 = (bf16[256,384]{1,0:T(8,128)(2,1)}, bf16[256,384]{1,0:T(8,128)(2,1)}, u32[]{:S(2)}, u32[]{:S(2)}) collective-permute-start(bf16[256,384]{1,0:T(8,128)(2,1)} %get-tuple-element.76), channel_id=1, source_target_pairs={{0,2},{2,0},{4,6},{6,4},{8,10},{10,8},{12,14},{14,12},{1,3},{3,1},... | collective-permute-start | bytes 589832 | tf_op jit(solution)/shard_map/ppermute | solution.py:29
  56.7 29.5 %collective-permute-start.12 = (bf16[256,384]{1,0:T(8,128)(2,1)}, bf16[256,384]{1,0:T(8,128)(2,1)}, u32[]{:S(2)}, u32[]{:S(2)}) collective-permute-start(bf16[256,384]{1,0:T(8,128)(2,1)} %get-tuple-element.78), channel_id=1, source_target_pairs={{0,4},{2,6},{4,0},{6,2},{8,12},{10,14},{12,8},{14,10},{1,5},{3,7},... | collective-permute-start | bytes 589832 | tf_op jit(solution)/shard_map/ppermute | solution.py:29
  63.9 19.1 %collective-permute-start.9 = (bf16[512,384]{1,0:T(8,128)(2,1)}, bf16[512,384]{1,0:T(8,128)(2,1)}, u32[]{:S(2)}, u32[]{:S(2)}) collective-permute-start(bf16[512,384]{1,0:T(8,128)(2,1)} %get-tuple-element.33), channel_id=1, source_target_pairs={{0,4},{2,6},{4,0},{6,2},{8,12},{10,14},{12,8},{14,10},{1,5},{3,7},... | collective-permute-start | bytes 1179656 | tf_op jit(solution)/shard_map/ppermute | solution.py:29
  65.2 17.8 %copy-start.11 = (f32[512,384]{1,0:T(8,128)S(1)}, f32[512,384]{1,0:T(8,128)}, u32[]{:S(2)}) copy-start(f32[512,384]{1,0:T(8,128)} %get-tuple-element.32) | copy-start | bytes 2359300
  66.4 62.4 %collective-permute-start.19 = (bf16[512,384]{1,0:T(8,128)(2,1)S(1)}, bf16[512,384]{1,0:T(8,128)(2,1)S(1)}, u32[]{:S(2)}, u32[]{:S(2)}) collective-permute-start(bf16[512,384]{1,0:T(8,128)(2,1)S(1)} %get-tuple-element.51), channel_id=1, source_target_pairs={{0,8},{2,10},{4,12},{6,14},{8,0},{10,2},{12,4},{14,6},{1,9},{3,11}... | collective-permute-start | bytes 1179656 | tf_op jit(solution)/shard_map/ppermute | solution.py:29
  84.1 44.7 %copy-start.13 = (bf16[3,32,1536]{2,1,0:T(8,128)(2,1)S(1)}, bf16[3,32,1536]{2,1,0:T(8,128)(2,1)}, u32[]{:S(2)}) copy-start(bf16[3,32,1536]{2,1,0:T(8,128)(2,1)} %get-tuple-element.40) | copy-start | bytes 884740
  84.1 45.8 %copy-start.12 = (bf16[3,32,1536]{2,1,0:T(8,128)(2,1)S(1)}, bf16[3,32,1536]{2,1,0:T(8,128)(2,1)}, u32[]{:S(2)}) copy-start(bf16[3,32,1536]{2,1,0:T(8,128)(2,1)} %get-tuple-element.41) | copy-start | bytes 884740
  84.1 45.9 %copy-start.4 = (bf16[256,384]{1,0:T(8,128)(2,1)S(1)}, bf16[256,384]{1,0:T(8,128)(2,1)}, u32[]{:S(2)}) copy-start(bf16[256,384]{1,0:T(8,128)(2,1)} %get-tuple-element.77.refs_0_) | copy-start | bytes 589828
  84.2 45.9 %copy-start.9 = (s32[2]{0:T(128)S(1)}, s32[2]{0:T(128)}, u32[]{:S(2)}) copy-start(s32[2]{0:T(128)} %length_ref.1) | copy-start | bytes 28
  84.2 45.8 %collective-permute-start.10 = (bf16[512,384]{1,0:T(8,128)(2,1)S(1)}, bf16[512,384]{1,0:T(8,128)(2,1)S(1)}, u32[]{:S(2)}, u32[]{:S(2)}) collective-permute-start(bf16[512,384]{1,0:T(8,128)(2,1)S(1)} %get-tuple-element.53), channel_id=1, source_target_pairs={{0,8},{2,10},{4,12},{6,14},{8,0},{10,2},{12,4},{14,6},{1,9},{3,11}... | collective-permute-start | bytes 1179656 | tf_op jit(solution)/shard_map/ppermute | solution.py:29
  84.4 30.1 %collective-permute-start.25 = (bf16[3,32,1536]{2,1,0:T(8,128)(2,1)S(1)}, bf16[3,32,1536]{2,1,0:T(8,128)(2,1)S(1)}, u32[]{:S(2)}, u32[]{:S(2)}) collective-permute-start(bf16[3,32,1536]{2,1,0:T(8,128)(2,1)S(1)} %get-tuple-element.59), channel_id=1, source_target_pairs={{0,14},{2,4},{4,10},{6,0},{8,6},{10,12},{12,2},{14,8},{1,15},{3,5}... | collective-permute-start | bytes 884744 | tf_op jit(solution)/shard_map/ppermute | solution.py:335
  85.4 43.4 %collective-permute-start.26 = (bf16[3,32,1536]{2,1,0:T(8,128)(2,1)S(1)}, bf16[3,32,1536]{2,1,0:T(8,128)(2,1)S(1)}, u32[]{:S(2)}, u32[]{:S(2)}) collective-permute-start(bf16[3,32,1536]{2,1,0:T(8,128)(2,1)S(1)} %get-tuple-element.58), channel_id=1, source_target_pairs={{0,6},{2,12},{4,2},{6,8},{8,14},{10,4},{12,10},{14,0},{1,7},{3,13}... | collective-permute-start | bytes 884744 | tf_op jit(solution)/shard_map/ppermute | solution.py:335
  86.2 26.3 %collective-permute-start.13 = (bf16[256,384]{1,0:T(8,128)(2,1)S(1)}, bf16[256,384]{1,0:T(8,128)(2,1)S(1)}, u32[]{:S(2)}, u32[]{:S(2)}) collective-permute-start(bf16[256,384]{1,0:T(8,128)(2,1)S(1)} %copy-done.14), channel_id=1, source_target_pairs={{0,6},{2,4},{4,2},{6,0},{8,14},{10,12},{12,10},{14,8},{1,7},{3,5},... | collective-permute-start | bytes 589832 | tf_op jit(solution)/shard_map/ppermute | solution.py:29
  112.5 25.2 %collective-permute-start.27 = (bf16[3,32,1536]{2,1,0:T(8,128)(2,1)S(1)}, bf16[3,32,1536]{2,1,0:T(8,128)(2,1)S(1)}, u32[]{:S(2)}, u32[]{:S(2)}) collective-permute-start(bf16[3,32,1536]{2,1,0:T(8,128)(2,1)S(1)} %get-tuple-element.57), channel_id=1, source_target_pairs={{0,8},{2,10},{4,12},{6,14},{8,0},{10,2},{12,4},{14,6},{1,9},{3,11}... | collective-permute-start | bytes 884744 | tf_op jit(solution)/shard_map/ppermute | solution.py:335
  114.5 34.0 %collective-permute-start.28 = (bf16[3,32,1536]{2,1,0:T(8,128)(2,1)S(1)}, bf16[3,32,1536]{2,1,0:T(8,128)(2,1)S(1)}, u32[]{:S(2)}, u32[]{:S(2)}) collective-permute-start(bf16[3,32,1536]{2,1,0:T(8,128)(2,1)S(1)} %get-tuple-element.56), channel_id=1, source_target_pairs={{0,10},{2,8},{4,14},{6,12},{8,2},{10,0},{12,6},{14,4},{1,11},{3,9}... | collective-permute-start | bytes 884744 | tf_op jit(solution)/shard_map/ppermute | solution.py:335
  128.8 19.8 %collective-permute-start.29 = (bf16[3,32,1536]{2,1,0:T(8,128)(2,1)S(1)}, bf16[3,32,1536]{2,1,0:T(8,128)(2,1)S(1)}, u32[]{:S(2)}, u32[]{:S(2)}) collective-permute-start(bf16[3,32,1536]{2,1,0:T(8,128)(2,1)S(1)} %get-tuple-element.55), channel_id=1, source_target_pairs={{0,2},{2,0},{4,6},{6,4},{8,10},{10,8},{12,14},{14,12},{1,3},{3,1},... | collective-permute-start | bytes 884744 | tf_op jit(solution)/shard_map/ppermute | solution.py:335
  128.8 20.9 %collective-permute-start.23 = (bf16[3,32,1536]{2,1,0:T(8,128)(2,1)S(1)}, bf16[3,32,1536]{2,1,0:T(8,128)(2,1)S(1)}, u32[]{:S(2)}, u32[]{:S(2)}) collective-permute-start(bf16[3,32,1536]{2,1,0:T(8,128)(2,1)S(1)} %copy-done.13), channel_id=1, source_target_pairs={{0,12},{2,6},{4,8},{6,2},{8,4},{10,14},{12,0},{14,10},{1,13},{3,7}... | collective-permute-start | bytes 884744 | tf_op jit(solution)/shard_map/ppermute | solution.py:335
  129.9 24.3 %collective-permute-start.24 = (bf16[3,32,1536]{2,1,0:T(8,128)(2,1)S(1)}, bf16[3,32,1536]{2,1,0:T(8,128)(2,1)S(1)}, u32[]{:S(2)}, u32[]{:S(2)}) collective-permute-start(bf16[3,32,1536]{2,1,0:T(8,128)(2,1)S(1)} %copy-done.12), channel_id=1, source_target_pairs={{0,4},{2,14},{4,0},{6,10},{8,12},{10,6},{12,8},{14,2},{1,5},{3,15}... | collective-permute-start | bytes 884744 | tf_op jit(solution)/shard_map/ppermute | solution.py:335
  134.2 36.7 %copy-start.5 = (bf16[1,1,256,1536]{3,2,1,0:T(8,128)(2,1)S(1)}, bf16[1,1,256,1536]{3,2,1,0:T(8,128)(2,1)}, u32[]{:S(2)}) copy-start(bf16[1,1,256,1536]{3,2,1,0:T(8,128)(2,1)} %param.9) | copy-start | bytes 2359300
  137.7 29.9 %collective-permute-start.20 = (bf16[256,384]{1,0:T(8,128)(2,1)S(1)}, bf16[256,384]{1,0:T(8,128)(2,1)S(1)}, u32[]{:S(2)}, u32[]{:S(2)}) collective-permute-start(bf16[256,384]{1,0:T(8,128)(2,1)S(1)} %get-tuple-element.37), channel_id=1, source_target_pairs={{0,4},{2,6},{4,0},{6,2},{8,12},{10,14},{12,8},{14,10},{1,5},{3,7},... | collective-permute-start | bytes 589832 | tf_op jit(solution)/shard_map/ppermute | solution.py:29
  148.5 19.1 %collective-permute-start.21 = (bf16[256,384]{1,0:T(8,128)(2,1)S(1)}, bf16[256,384]{1,0:T(8,128)(2,1)S(1)}, u32[]{:S(2)}, u32[]{:S(2)}) collective-permute-start(bf16[256,384]{1,0:T(8,128)(2,1)S(1)} %get-tuple-element.38), channel_id=1, source_target_pairs={{0,2},{2,0},{4,6},{6,4},{8,10},{10,8},{12,14},{14,12},{1,3},{3,1},... | collective-permute-start | bytes 589832 | tf_op jit(solution)/shard_map/ppermute | solution.py:29
  148.6 20.3 %collective-permute-start.22 = (bf16[256,384]{1,0:T(8,128)(2,1)S(1)}, bf16[256,384]{1,0:T(8,128)(2,1)S(1)}, u32[]{:S(2)}, u32[]{:S(2)}) collective-permute-start(bf16[256,384]{1,0:T(8,128)(2,1)S(1)} %get-tuple-element.39), channel_id=1, source_target_pairs={{0,6},{2,4},{4,2},{6,0},{8,14},{10,12},{12,10},{14,8},{1,7},{3,5},... | collective-permute-start | bytes 589832 | tf_op jit(solution)/shard_map/ppermute | solution.py:29
  158.9 1.4 collective-permute-start.30
  159.0 5.7 %collective-permute-start.31 = (bf16[32,1536]{1,0:T(8,128)(2,1)S(1)}, bf16[32,1536]{1,0:T(8,128)(2,1)S(1)}, u32[]{:S(2)}, u32[]{:S(2)}) collective-permute-start(bf16[32,1536]{1,0:T(8,128)(2,1)S(1)} %get-tuple-element.45), channel_id=1, source_target_pairs={{0,4},{2,6},{4,0},{6,2},{8,12},{10,14},{12,8},{14,10},{1,5},{3,7},... | collective-permute-start | bytes 294920 | tf_op jit(solution)/shard_map/ppermute | solution.py:29
  160.3 17.9 %collective-permute-start.32 = (bf16[32,1536]{1,0:T(8,128)(2,1)S(1)}, bf16[32,1536]{1,0:T(8,128)(2,1)S(1)}, u32[]{:S(2)}, u32[]{:S(2)}) collective-permute-start(bf16[32,1536]{1,0:T(8,128)(2,1)S(1)} %get-tuple-element.46), channel_id=1, source_target_pairs={{0,6},{2,4},{4,2},{6,0},{8,14},{10,12},{12,10},{14,8},{1,7},{3,5},... | collective-permute-start | bytes 294920 | tf_op jit(solution)/shard_map/ppermute | solution.py:29
  164.7 14.3 %collective-permute-start.33 = (bf16[32,1536]{1,0:T(8,128)(2,1)S(1)}, bf16[32,1536]{1,0:T(8,128)(2,1)S(1)}, u32[]{:S(2)}, u32[]{:S(2)}) collective-permute-start(bf16[32,1536]{1,0:T(8,128)(2,1)S(1)} %get-tuple-element.47), channel_id=1, source_target_pairs={{0,8},{2,10},{4,12},{6,14},{8,0},{10,2},{12,4},{14,6},{1,9},{3,11}... | collective-permute-start | bytes 294920 | tf_op jit(solution)/shard_map/ppermute | solution.py:29
  167.6 11.6 %collective-permute-start.34 = (bf16[32,1536]{1,0:T(8,128)(2,1)S(1)}, bf16[32,1536]{1,0:T(8,128)(2,1)S(1)}, u32[]{:S(2)}, u32[]{:S(2)}) collective-permute-start(bf16[32,1536]{1,0:T(8,128)(2,1)S(1)} %get-tuple-element.48), channel_id=1, source_target_pairs={{0,10},{2,8},{4,14},{6,12},{8,2},{10,0},{12,6},{14,4},{1,11},{3,9}... | collective-permute-start | bytes 294920 | tf_op jit(solution)/shard_map/ppermute | solution.py:29
  167.6 11.6 %collective-permute-start.35 = (bf16[32,1536]{1,0:T(8,128)(2,1)S(1)}, bf16[32,1536]{1,0:T(8,128)(2,1)S(1)}, u32[]{:S(2)}, u32[]{:S(2)}) collective-permute-start(bf16[32,1536]{1,0:T(8,128)(2,1)S(1)} %get-tuple-element.49), channel_id=1, source_target_pairs={{0,12},{2,14},{4,8},{6,10},{8,4},{10,6},{12,0},{14,2},{1,13},{3,15... | collective-permute-start | bytes 294920 | tf_op jit(solution)/shard_map/ppermute | solution.py:29
  168.9 10.4 %collective-permute-start.36 = (bf16[32,1536]{1,0:T(8,128)(2,1)S(1)}, bf16[32,1536]{1,0:T(8,128)(2,1)S(1)}, u32[]{:S(2)}, u32[]{:S(2)}) collective-permute-start(bf16[32,1536]{1,0:T(8,128)(2,1)S(1)} %get-tuple-element.50), channel_id=1, source_target_pairs={{0,14},{2,12},{4,10},{6,8},{8,6},{10,4},{12,2},{14,0},{1,15},{3,13... | collective-permute-start | bytes 294920 | tf_op jit(solution)/shard_map/ppermute | solution.py:29
  (6 other events, 7.7 us)

commit v7 on v6

--- a/solution.py
+++ b/solution.py
@@ -124,7 +124,8 @@
 def project(states, weights, near):
     _, rows, _ = states[0].shape
     n_rows = len(states) // 2
-    places, arrays = zip(*weights)
+    places = [place for place, _ in weights]
+    arrays = [on_chip(array)[0] if place[1] else array for place, array in weights]
     shape = (n_rows * rows, arrays[0].shape[1] // 2)
     return pl.pallas_call(
         functools.partial(project_kernel, n_rows, places),
@@ -133,7 +134,7 @@
         out_shape=[pltpu.HBM(shape, F32), pltpu.VMEM(shape, BF16)],
         compiler_params=MODEST,
         name="project",
-    )(near.reshape(1), *states, *arrays)
+    )(near.reshape(1), *on_chip(*states), *arrays)
 
 
 def spatial_kernel(qkv_ref, residual_ref, out_ref):

time: 184 us -> 184 us (level)
  no operation moved by 1% of the time
where the time goes in v7:
time: 184 us; the launch traced here: 180 us
  waiting for transfers between devices  88.2 us (48%)
  starting transfers between devices  52.6 us (29%)
  Pallas kernels  23.1 us (13%)
  local copies, waits for them, and re-layouts  13.8 us (8%)
  other arithmetic  2.39 us (1%)
    ppermute x26, waiting for transfers between devices, swap(): return lax.ppermute(value, axis, pairs)  56.4 us
    ppermute x26, starting transfers between devices, swap(): return lax.ppermute(value, axis, pairs)  23.6 us
    ppermute x7, starting transfers between devices, block(): pieces.append(lax.ppermute(blocks[number], 'seq', pairs))  19.2 us
    ppermute x7, waiting for transfers between devices, block(): pieces.append(lax.ppermute(blocks[number], 'seq', pairs))  18.9 us
    all_to_all x1, waiting for transfers between devices, block(): parts = lax.all_to_all(parts, 'seq', 0, 0, tiled=True)  7.24 us
    unnamed x32, local copies, waits for them, and re-layouts  6.89 us
    all_to_all x1, starting transfers between devices, block(): parts = lax.all_to_all(parts, 'seq', 0, 0, tiled=True)  6.35 us
    pallas_call x2, Pallas kernels, project(): pl.pallas_call(functools.partial(project_kernel, n_rows, places), in_spec...  6.1 us
  transfers between devices with their start and end apart: 38, of which 15 were waited for; matrix products, arithmetic and copies ran while one was open for 7% of the time, Pallas kernels for 12%

profile of v7, /device:TPU:0, one launch (start us, length us, event | category | flops | bytes accessed | tf_op | source)
XLA Modules:
  0.0 180.3 jit_solution(235825597761187977)
XLA Ops:
  0.0 1.0 copy-done.7
  1.8 6.4 %all-to-all-start = ((bf16[8,2,32,256]{3,2,1,0:T(8,128)(2,1)}), bf16[8,2,32,256]{3,2,1,0:T(8,128)(2,1)S(1)}, u32[]{:S(2)}, u32[]{:S(2)}) async-start(bf16[8,2,32,256]{3,2,1,0:T(8,128)(2,1)} %prompt_blocks.1), calls=%async_computation | async-start | bytes 524288 | tf_op jit(solution)/shard_map/all_to_all | solution.py:321
  8.1 1.0 copy.11
  9.1 1.5 collective-permute-start.7
  10.6 7.2 %all-to-all-done.parts_ref = bf16[8,2,32,256]{3,2,1,0:T(8,128)(2,1)S(1)} async-done(((bf16[8,2,32,256]{3,2,1,0:T(8,128)(2,1)}), bf16[8,2,32,256]{3,2,1,0:T(8,128)(2,1)S(1)}, u32[]{:S(2)}, u32[]{:S(2)}) %all-to-all-start) | async-done | bytes 262176 | tf_op jit(solution)/shard_map/all_to_all | solution.py:321
  18.4 1.6 collective-permute-start
  19.9 1.6 copy.12
  22.3 9.7 %collective-permute-done = bf16[256,256]{1,0:T(8,128)(2,1)S(1)} collective-permute-done((bf16[256,256]{1,0:T(8,128)(2,1)S(1)}, bf16[256,256]{1,0:T(8,128)(2,1)S(1)}, u32[]{:S(2)}, u32[]{:S(2)}) %collective-permute-start) | collective-permute-done | bytes 131104 | tf_op jit(solution)/shard_map/ppermute | solution.py:29
  32.1 1.6 collective-permute-start.2
  34.6 1.5 collective-permute-start.14
  36.7 3.3 %collective-permute-done.2.refs_2_ = bf16[2,256,256]{2,1,0:T(8,128)(2,1)S(1)} collective-permute-done((bf16[2,256,256]{2,1,0:T(8,128)(2,1)S(1)}, bf16[2,256,256]{2,1,0:T(8,128)(2,1)S(1)}, u32[]{:S(2)}, u32[]{:S(2)}) %collective-permute-start.2) | collective-permute-done | bytes 262176 | tf_op jit(solution)/shard_map/ppermute | solution.py:29
  40.0 2.0 %dynamic-slice_bitcast_fusion.7 = (bf16[128,768]{1,0:T(8,128)(2,1)S(1)}, bf16[128,768]{1,0:T(8,128)(2,1)S(1)}, bf16[128,768]{1,0:T(8,128)(2,1)}, bf16[128,768]{1,0:T(8,128)(2,1)}) fusion(bf16[2,128,1536]{2,1,0:T(8,128)(2,1)} %bitcast.17, s32[]{:T(128)S(6)} %select_n.69, s32[]{:T(128)S(6)} %select_n.68), kind=kLoop, calls=%fused_computation.10 | loop fusion | bytes 1572872 | tf_op jit(solution)/shard_map/reshape | solution.py:346
  42.5 3.1 %collective-permute-done.15.refs_5_ = bf16[128,768]{1,0:T(8,128)(2,1)S(1)} collective-permute-done((bf16[128,768]{1,0:T(8,128)(2,1)S(1)}, bf16[128,768]{1,0:T(8,128)(2,1)S(1)}, u32[]{:S(2)}, u32[]{:S(2)}) %collective-permute-start.15) | collective-permute-done | bytes 196640 | tf_op jit(solution)/shard_map/ppermute | solution.py:360
  45.9 1.5 collective-permute-start.4
  48.1 2.4 %project.3 = (f32[512,384]{1,0:T(8,128)}, bf16[512,384]{1,0:T(8,128)(2,1)}) custom-call(s32[1]{0:T(128)} %bitcast.7.scalar_ref, bf16[2,256,256]{2,1,0:T(8,128)(2,1)S(1)} %pad_maximum_fusion.refs_0_, bf16[2,256,256]{2,1,0:T(8,128)(2,1)S(1)} %collective-permute-done.1.refs_1_, bf16[2,256,256]{2,1,0:T(8,128)(2,1)S(1)} %collective-permute-done.2.refs_2_, ...), custom_call_target="tpu_custom_call" | custom-call | tf_op jit(solution)/shard_map/project/pallas_call | solution.py:130
  50.5 1.6 collective-permute-start.18
  52.1 2.1 %dynamic-slice_bitcast_fusion.9 = (bf16[256,384]{1,0:T(8,128)(2,1)}, bf16[256,384]{1,0:T(8,128)(2,1)}, bf16[256,384]{1,0:T(8,128)(2,1)}, bf16[256,384]{1,0:T(8,128)(2,1)}) fusion(bf16[1,1,256,1536]{3,2,1,0:T(8,128)(2,1)} %param.8, s32[]{:T(128)S(6)} %select_n.73, s32[]{:T(128)S(6)} %select_n.71, s32[]{:T(128)S(6)} %select_n.70, s32[]{:T(128)S(6)} %select_n.72), kind=kLoop, calls=%fused_computation.12 | loop fusion | bytes 1572880 | tf_op jit(solution)/shard_map/dynamic_slice | solution.py:385
  54.4 2.4 %collective-permute-done.5.refs_5_ = bf16[128,768]{1,0:T(8,128)(2,1)} collective-permute-done((bf16[128,768]{1,0:T(8,128)(2,1)}, bf16[128,768]{1,0:T(8,128)(2,1)}, u32[]{:S(2)}, u32[]{:S(2)}) %collective-permute-start.5) | collective-permute-done | bytes 196640 | tf_op jit(solution)/shard_map/ppermute | solution.py:360
  56.7 1.6 collective-permute-start.12
  58.4 0.9 copy-done.3
  59.3 0.9 copy-done.6
  60.2 3.7 %project.2 = (f32[512,384]{1,0:T(8,128)}, bf16[512,384]{1,0:T(8,128)(2,1)}) custom-call(s32[1]{0:T(128)} %bitcast.7.scalar_ref, bf16[2,256,256]{2,1,0:T(8,128)(2,1)S(1)} %pad_maximum_fusion.refs_0_, bf16[2,256,256]{2,1,0:T(8,128)(2,1)S(1)} %collective-permute-done.1.refs_1_, bf16[2,256,256]{2,1,0:T(8,128)(2,1)S(1)} %collective-permute-done.2.refs_2_, ...), custom_call_target="tpu_custom_call" | custom-call | tf_op jit(solution)/shard_map/project/pallas_call | solution.py:130
  65.2 1.2 fusion
  66.4 2.6 %collective-permute-start.19 = (bf16[512,384]{1,0:T(8,128)(2,1)S(1)}, bf16[512,384]{1,0:T(8,128)(2,1)S(1)}, u32[]{:S(2)}, u32[]{:S(2)}) collective-permute-start(bf16[512,384]{1,0:T(8,128)(2,1)S(1)} %get-tuple-element.51), channel_id=1, source_target_pairs={{0,8},{2,10},{4,12},{6,14},{8,0},{10,2},{12,4},{14,6},{1,9},{3,11}... | collective-permute-start | bytes 1179656 | tf_op jit(solution)/shard_map/ppermute | solution.py:29
  69.0 14.0 %collective-permute-done.9 = bf16[512,384]{1,0:T(8,128)(2,1)} collective-permute-done((bf16[512,384]{1,0:T(8,128)(2,1)}, bf16[512,384]{1,0:T(8,128)(2,1)}, u32[]{:S(2)}, u32[]{:S(2)}) %collective-permute-start.9) | collective-permute-done | bytes 393248 | tf_op jit(solution)/shard_map/ppermute | solution.py:29
  83.0 1.1 fusion.1
  84.4 1.0 collective-permute-start.25
  86.2 1.7 collective-permute-start.13
  87.9 24.6 %collective-permute-done.13.refs_3_ = bf16[256,384]{1,0:T(8,128)(2,1)S(1)} collective-permute-done((bf16[256,384]{1,0:T(8,128)(2,1)S(1)}, bf16[256,384]{1,0:T(8,128)(2,1)S(1)}, u32[]{:S(2)}, u32[]{:S(2)}) %collective-permute-start.13) | collective-permute-done | bytes 196640 | tf_op jit(solution)/shard_map/ppermute | solution.py:29
  112.5 2.0 %collective-permute-start.27 = (bf16[3,32,1536]{2,1,0:T(8,128)(2,1)S(1)}, bf16[3,32,1536]{2,1,0:T(8,128)(2,1)S(1)}, u32[]{:S(2)}, u32[]{:S(2)}) collective-permute-start(bf16[3,32,1536]{2,1,0:T(8,128)(2,1)S(1)} %get-tuple-element.57), channel_id=1, source_target_pairs={{0,8},{2,10},{4,12},{6,14},{8,0},{10,2},{12,4},{14,6},{1,9},{3,11}... | collective-permute-start | bytes 884744 | tf_op jit(solution)/shard_map/ppermute | solution.py:336
  114.5 14.3 %collective-permute-start.28 = (bf16[3,32,1536]{2,1,0:T(8,128)(2,1)S(1)}, bf16[3,32,1536]{2,1,0:T(8,128)(2,1)S(1)}, u32[]{:S(2)}, u32[]{:S(2)}) collective-permute-start(bf16[3,32,1536]{2,1,0:T(8,128)(2,1)S(1)} %get-tuple-element.56), channel_id=1, source_target_pairs={{0,10},{2,8},{4,14},{6,12},{8,2},{10,0},{12,6},{14,4},{1,11},{3,9}... | collective-permute-start | bytes 884744 | tf_op jit(solution)/shard_map/ppermute | solution.py:336
  128.8 1.1 collective-permute-start.23
  130.0 3.2 %cross_weights.1.weight_ref = bf16[3,4,256,512]{3,2,1,0:T(8,128)(2,1)S(1)} custom-call(s32[2]{0:T(128)S(1)} %pad_add_fusion.scalar_ref, s32[2]{0:T(128)S(1)} %copy-done.8, s32[2]{0:T(128)S(1)} %copy-done.9, f32[512,384]{1,0:T(8,128)S(1)} %get-tuple-element.54.kept_ref, bf16[512,384]{1,0:T(8,128)(2,1)S(1)} %collective-permute-done.10.come_ref, ...), custom_call_target="tpu_custom_call" | custom-call | tf_op jit(solution)/shard_map/cross_weights/pallas_call | solution.py:225
  133.2 1.0 cross_values.1
  134.2 3.5 %collective-permute-done.27.refs_5_ = bf16[3,32,1536]{2,1,0:T(8,128)(2,1)S(1)} collective-permute-done((bf16[3,32,1536]{2,1,0:T(8,128)(2,1)S(1)}, bf16[3,32,1536]{2,1,0:T(8,128)(2,1)S(1)}, u32[]{:S(2)}, u32[]{:S(2)}) %collective-permute-start.27) | collective-permute-done | bytes 294944 | tf_op jit(solution)/shard_map/ppermute | solution.py:336
  137.7 10.8 %collective-permute-done.28.refs_6_ = bf16[3,32,1536]{2,1,0:T(8,128)(2,1)S(1)} collective-permute-done((bf16[3,32,1536]{2,1,0:T(8,128)(2,1)S(1)}, bf16[3,32,1536]{2,1,0:T(8,128)(2,1)S(1)}, u32[]{:S(2)}, u32[]{:S(2)}) %collective-permute-start.28) | collective-permute-done | bytes 294944 | tf_op jit(solution)/shard_map/ppermute | solution.py:336
  148.6 1.1 collective-permute-start.22
  149.7 4.6 %collective-permute-done.24.refs_2_ = bf16[3,32,1536]{2,1,0:T(8,128)(2,1)S(1)} collective-permute-done((bf16[3,32,1536]{2,1,0:T(8,128)(2,1)S(1)}, bf16[3,32,1536]{2,1,0:T(8,128)(2,1)S(1)}, u32[]{:S(2)}, u32[]{:S(2)}) %collective-permute-start.24) | collective-permute-done | bytes 294944 | tf_op jit(solution)/shard_map/ppermute | solution.py:336
  154.3 4.7 %temporal.1 = (bf16[32,1536]{1,0:T(8,128)(2,1)S(1)}, bf16[32,1536]{1,0:T(8,128)(2,1)S(1)}, bf16[32,1536]{1,0:T(8,128)(2,1)S(1)}, bf16[32,1536]{1,0:T(8,128)(2,1)...) custom-call(s32[1]{0:T(128)} %bitcast.28.scalar_ref, ...), custom_call_target="tpu_custom_call" | custom-call | tf_op jit(solution)/shard_map/temporal/pallas_call | solution.py:190
  159.0 1.2 collective-permute-start.31
  160.3 0.9 collective-permute-start.32
  161.2 3.5 %collective-permute-done.31.refs_2_ = bf16[32,1536]{1,0:T(8,128)(2,1)S(1)} collective-permute-done((bf16[32,1536]{1,0:T(8,128)(2,1)S(1)}, bf16[32,1536]{1,0:T(8,128)(2,1)S(1)}, u32[]{:S(2)}, u32[]{:S(2)}) %collective-permute-start.31) | collective-permute-done | bytes 98336 | tf_op jit(solution)/shard_map/ppermute | solution.py:29
  164.7 2.9 %collective-permute-start.33 = (bf16[32,1536]{1,0:T(8,128)(2,1)S(1)}, bf16[32,1536]{1,0:T(8,128)(2,1)S(1)}, u32[]{:S(2)}, u32[]{:S(2)}) collective-permute-start(bf16[32,1536]{1,0:T(8,128)(2,1)S(1)} %get-tuple-element.47), channel_id=1, source_target_pairs={{0,8},{2,10},{4,12},{6,14},{8,0},{10,2},{12,4},{14,6},{1,9},{3,11}... | collective-permute-start | bytes 294920 | tf_op jit(solution)/shard_map/ppermute | solution.py:29
  167.6 1.3 collective-permute-start.35
  168.9 2.0 %collective-permute-start.36 = (bf16[32,1536]{1,0:T(8,128)(2,1)S(1)}, bf16[32,1536]{1,0:T(8,128)(2,1)S(1)}, u32[]{:S(2)}, u32[]{:S(2)}) collective-permute-start(bf16[32,1536]{1,0:T(8,128)(2,1)S(1)} %get-tuple-element.50), channel_id=1, source_target_pairs={{0,14},{2,12},{4,10},{6,8},{8,6},{10,4},{12,2},{14,0},{1,15},{3,13... | collective-permute-start | bytes 294920 | tf_op jit(solution)/shard_map/ppermute | solution.py:29
  170.9 5.3 %spatial.1.base_ref = f32[256,1536]{1,0:T(8,128)} custom-call(bf16[3,256,1536]{2,1,0:T(8,128)(2,1)S(1)} %bitcast.62, bf16[256,1536]{1,0:T(8,128)(2,1)S(1)} %bitcast.63), custom_call_target="tpu_custom_call" | custom-call | tf_op jit(solution)/shard_map/spatial/pallas_call | solution.py:151
  176.2 1.4 copy-done.1
  179.3 1.0 final.1
  (83 shorter events, 9.5 us)
Async XLA Ops:
  1.0 7.1 %slice-start = ((bf16[256,2,1536]{2,1,0:T(2,128)(2,1)}), bf16[128,2,1536]{2,1,0:T(2,128)(2,1)S(1)}, s32[]{:S(2)}) async-start(bf16[256,2,1536]{2,1,0:T(2,128)(2,1)} %param.11), calls=%async_computation.1 | async-start | bytes 1572864 | tf_op jit(solution)/shard_map/slice | solution.py:351
  1.8 16.1 %all-to-all-start = ((bf16[8,2,32,256]{3,2,1,0:T(8,128)(2,1)}), bf16[8,2,32,256]{3,2,1,0:T(8,128)(2,1)S(1)}, u32[]{:S(2)}, u32[]{:S(2)}) async-start(bf16[8,2,32,256]{3,2,1,0:T(8,128)(2,1)} %prompt_blocks.1), calls=%async_computation | async-start | bytes 524288 | tf_op jit(solution)/shard_map/all_to_all | solution.py:321
  8.1 9.7 %copy-start.8 = (s32[2]{0:T(128)S(1)}, s32[2]{0:T(128)}, u32[]{:S(2)}) copy-start(s32[2]{0:T(128)} %assignment_ref.3) | copy-start | bytes 28
  9.1 27.3 %collective-permute-start.7 = (bf16[128,2,1536]{2,0,1:T(8,128)(2,1)}, bf16[128,2,1536]{2,0,1:T(8,128)(2,1)}, u32[]{:S(2)}, u32[]{:S(2)}) collective-permute-start(bf16[128,2,1536]{2,0,1:T(8,128)(2,1)} %copy.11), channel_id=1, source_target_pairs={{0,16},{16,0},{1,17},{17,1},{2,18},{18,2},{3,19},{19,3},{4,20},{20... | collective-permute-start | bytes 2359304 | tf_op jit(solution)/shard_map/ppermute | solution.py:29
  18.4 13.7 %collective-permute-start = (bf16[256,256]{1,0:T(8,128)(2,1)S(1)}, bf16[256,256]{1,0:T(8,128)(2,1)S(1)}, u32[]{:S(2)}, u32[]{:S(2)}) collective-permute-start(bf16[256,256]{1,0:T(8,128)(2,1)S(1)} %get-tuple-element.29), channel_id=1, source_target_pairs={{0,16},{16,0},{1,17},{17,1},{2,18},{18,2},{3,19},{19,3},{4,20},{20... | collective-permute-start | bytes 393224 | tf_op jit(solution)/shard_map/ppermute | solution.py:29
  32.1 7.9 %collective-permute-start.2 = (bf16[2,256,256]{2,1,0:T(8,128)(2,1)S(1)}, bf16[2,256,256]{2,1,0:T(8,128)(2,1)S(1)}, u32[]{:S(2)}, u32[]{:S(2)}) collective-permute-start(bf16[2,256,256]{2,1,0:T(8,128)(2,1)S(1)} %pad_maximum_fusion.refs_0_), channel_id=1, source_target_pairs={{0,1},{1,0},{2,3},{3,2},{4,5},{5,4},{6,7},{7,6},{8,9},{9,8},{10,11... | collective-permute-start | bytes 786440 | tf_op jit(solution)/shard_map/ppermute | solution.py:29
  34.6 11.4 %collective-permute-start.16 = (bf16[256,768]{1,0:T(8,128)(2,1)S(1)}, bf16[256,768]{1,0:T(8,128)(2,1)S(1)}, u32[]{:S(2)}, u32[]{:S(2)}) collective-permute-start(bf16[256,768]{1,0:T(8,128)(2,1)S(1)} %get-tuple-element.63), channel_id=1, source_target_pairs={{0,2},{2,0},{4,6},{6,4},{8,10},{10,8},{12,14},{14,12},{1,3},{3,1},... | collective-permute-start | bytes 1179656 | tf_op jit(solution)/shard_map/ppermute | solution.py:29
  34.6 7.8 %collective-permute-start.14 = (bf16[128,768]{1,0:T(8,128)(2,1)S(1)}, bf16[128,768]{1,0:T(8,128)(2,1)S(1)}, u32[]{:S(2)}, u32[]{:S(2)}) collective-permute-start(bf16[128,768]{1,0:T(8,128)(2,1)S(1)} %get-tuple-element.68), channel_id=1, source_target_pairs={{0,16},{2,18},{4,20},{6,22},{8,24},{10,26},{12,28},{14,30},{16,0},... | collective-permute-start | bytes 589832 | tf_op jit(solution)/shard_map/ppermute | solution.py:360
  36.1 9.6 %collective-permute-start.15 = (bf16[128,768]{1,0:T(8,128)(2,1)S(1)}, bf16[128,768]{1,0:T(8,128)(2,1)S(1)}, u32[]{:S(2)}, u32[]{:S(2)}) collective-permute-start(bf16[128,768]{1,0:T(8,128)(2,1)S(1)} %get-tuple-element.67), channel_id=1, source_target_pairs={{0,18},{2,16},{4,22},{6,20},{8,26},{10,24},{12,30},{14,28},{16,2},... | collective-permute-start | bytes 589832 | tf_op jit(solution)/shard_map/ppermute | solution.py:360
  36.4 11.0 %collective-permute-start.1 = (bf16[2,256,256]{2,1,0:T(8,128)(2,1)S(1)}, bf16[2,256,256]{2,1,0:T(8,128)(2,1)S(1)}, u32[]{:S(2)}, u32[]{:S(2)}) collective-permute-start(bf16[2,256,256]{2,1,0:T(8,128)(2,1)S(1)} %pad_maximum_fusion.refs_0_), channel_id=1, source_target_pairs={{0,2},{2,0},{4,6},{6,4},{8,10},{10,8},{12,14},{14,12},{1,3},{3,1},... | collective-permute-start | bytes 786440 | tf_op jit(solution)/shard_map/ppermute | solution.py:29
  40.0 8.1 %collective-permute-start.3 = (bf16[2,256,256]{2,1,0:T(8,128)(2,1)S(1)}, bf16[2,256,256]{2,1,0:T(8,128)(2,1)S(1)}, u32[]{:S(2)}, u32[]{:S(2)}) collective-permute-start(bf16[2,256,256]{2,1,0:T(8,128)(2,1)S(1)} %collective-permute-done.2.refs_2_), channel_id=1, source_target_pairs={{0,2},{2,0},{4,6},{6,4},{8,10},{10,8},{12,14},{14,12},{1,3},{3,1},... | collective-permute-start | bytes 786440 | tf_op jit(solution)/shard_map/ppermute | solution.py:29
  42.3 5.2 %collective-permute-start.17 = (bf16[128,768]{1,0:T(8,128)(2,1)S(1)}, bf16[128,768]{1,0:T(8,128)(2,1)S(1)}, u32[]{:S(2)}, u32[]{:S(2)}) collective-permute-start(bf16[128,768]{1,0:T(8,128)(2,1)S(1)} %get-tuple-element.71), channel_id=1, source_target_pairs={{0,2},{2,0},{4,6},{6,4},{8,10},{10,8},{12,14},{14,12},{1,3},{3,1},... | collective-permute-start | bytes 589832 | tf_op jit(solution)/shard_map/ppermute | solution.py:29
  45.6 12.7 %collective-permute-start.6 = (bf16[256,768]{1,0:T(8,128)(2,1)}, bf16[256,768]{1,0:T(8,128)(2,1)}, u32[]{:S(2)}, u32[]{:S(2)}) collective-permute-start(bf16[256,768]{1,0:T(8,128)(2,1)} %get-tuple-element.65), channel_id=1, source_target_pairs={{0,2},{2,0},{4,6},{6,4},{8,10},{10,8},{12,14},{14,12},{1,3},{3,1},... | collective-permute-start | bytes 1179656 | tf_op jit(solution)/shard_map/ppermute | solution.py:29
  45.9 8.4 %collective-permute-start.4 = (bf16[128,768]{1,0:T(8,128)(2,1)}, bf16[128,768]{1,0:T(8,128)(2,1)}, u32[]{:S(2)}, u32[]{:S(2)}) collective-permute-start(bf16[128,768]{1,0:T(8,128)(2,1)} %get-tuple-element.70), channel_id=1, source_target_pairs={{0,16},{2,18},{4,20},{6,22},{8,24},{10,26},{12,28},{14,30},{16,0},... | collective-permute-start | bytes 589832 | tf_op jit(solution)/shard_map/ppermute | solution.py:360
  47.4 9.3 %collective-permute-start.5 = (bf16[128,768]{1,0:T(8,128)(2,1)}, bf16[128,768]{1,0:T(8,128)(2,1)}, u32[]{:S(2)}, u32[]{:S(2)}) collective-permute-start(bf16[128,768]{1,0:T(8,128)(2,1)} %get-tuple-element.69), channel_id=1, source_target_pairs={{0,18},{2,16},{4,22},{6,20},{8,26},{10,24},{12,30},{14,28},{16,2},... | collective-permute-start | bytes 589832 | tf_op jit(solution)/shard_map/ppermute | solution.py:360
  47.5 10.9 %collective-permute-start.8 = (bf16[128,768]{1,0:T(8,128)(2,1)}, bf16[128,768]{1,0:T(8,128)(2,1)}, u32[]{:S(2)}, u32[]{:S(2)}) collective-permute-start(bf16[128,768]{1,0:T(8,128)(2,1)} %get-tuple-element.73), channel_id=1, source_target_pairs={{0,2},{2,0},{4,6},{6,4},{8,10},{10,8},{12,14},{14,12},{1,3},{3,1},... | collective-permute-start | bytes 589832 | tf_op jit(solution)/shard_map/ppermute | solution.py:29
  48.1 4.1 %copy-start.2 = (bf16[2,256,256]{2,1,0:T(8,128)(2,1)}, bf16[2,256,256]{2,1,0:T(8,128)(2,1)S(1)}, u32[]{:S(2)}) copy-start(bf16[2,256,256]{2,1,0:T(8,128)(2,1)S(1)} %collective-permute-done.3.refs_3_) | copy-start | bytes 786436
  50.5 14.7 %collective-permute-start.18 = (bf16[512,384]{1,0:T(8,128)(2,1)}, bf16[512,384]{1,0:T(8,128)(2,1)}, u32[]{:S(2)}, u32[]{:S(2)}) collective-permute-start(bf16[512,384]{1,0:T(8,128)(2,1)} %get-tuple-element.35), channel_id=1, source_target_pairs={{0,4},{2,6},{4,0},{6,2},{8,12},{10,14},{12,8},{14,10},{1,5},{3,7},... | collective-permute-start | bytes 1179656 | tf_op jit(solution)/shard_map/ppermute | solution.py:29
  54.3 10.0 %copy-start = (bf16[1,1,256,3,1536]{4,2,3,1,0:T(8,128)(2,1)S(1)}, bf16[1,1,256,3,1536]{4,2,3,1,0:T(8,128)(2,1)}, u32[]{:S(2)}) copy-start(bf16[1,1,256,3,1536]{4,2,3,1,0:T(8,128)(2,1)} %param.7) | copy-start | bytes 7077892
  54.3 31.1 %collective-permute-start.11 = (bf16[256,384]{1,0:T(8,128)(2,1)}, bf16[256,384]{1,0:T(8,128)(2,1)}, u32[]{:S(2)}, u32[]{:S(2)}) collective-permute-start(bf16[256,384]{1,0:T(8,128)(2,1)} %get-tuple-element.76), channel_id=1, source_target_pairs={{0,2},{2,0},{4,6},{6,4},{8,10},{10,8},{12,14},{14,12},{1,3},{3,1},... | collective-permute-start | bytes 589832 | tf_op jit(solution)/shard_map/ppermute | solution.py:29
  56.7 29.5 %collective-permute-start.12 = (bf16[256,384]{1,0:T(8,128)(2,1)}, bf16[256,384]{1,0:T(8,128)(2,1)}, u32[]{:S(2)}, u32[]{:S(2)}) collective-permute-start(bf16[256,384]{1,0:T(8,128)(2,1)} %get-tuple-element.78), channel_id=1, source_target_pairs={{0,4},{2,6},{4,0},{6,2},{8,12},{10,14},{12,8},{14,10},{1,5},{3,7},... | collective-permute-start | bytes 589832 | tf_op jit(solution)/shard_map/ppermute | solution.py:29
  63.9 19.1 %collective-permute-start.9 = (bf16[512,384]{1,0:T(8,128)(2,1)}, bf16[512,384]{1,0:T(8,128)(2,1)}, u32[]{:S(2)}, u32[]{:S(2)}) collective-permute-start(bf16[512,384]{1,0:T(8,128)(2,1)} %get-tuple-element.33), channel_id=1, source_target_pairs={{0,4},{2,6},{4,0},{6,2},{8,12},{10,14},{12,8},{14,10},{1,5},{3,7},... | collective-permute-start | bytes 1179656 | tf_op jit(solution)/shard_map/ppermute | solution.py:29
  65.2 17.8 %copy-start.11 = (f32[512,384]{1,0:T(8,128)S(1)}, f32[512,384]{1,0:T(8,128)}, u32[]{:S(2)}) copy-start(f32[512,384]{1,0:T(8,128)} %get-tuple-element.32) | copy-start | bytes 2359300
  66.4 62.4 %collective-permute-start.19 = (bf16[512,384]{1,0:T(8,128)(2,1)S(1)}, bf16[512,384]{1,0:T(8,128)(2,1)S(1)}, u32[]{:S(2)}, u32[]{:S(2)}) collective-permute-start(bf16[512,384]{1,0:T(8,128)(2,1)S(1)} %get-tuple-element.51), channel_id=1, source_target_pairs={{0,8},{2,10},{4,12},{6,14},{8,0},{10,2},{12,4},{14,6},{1,9},{3,11}... | collective-permute-start | bytes 1179656 | tf_op jit(solution)/shard_map/ppermute | solution.py:29
  84.1 44.7 %copy-start.13 = (bf16[3,32,1536]{2,1,0:T(8,128)(2,1)S(1)}, bf16[3,32,1536]{2,1,0:T(8,128)(2,1)}, u32[]{:S(2)}) copy-start(bf16[3,32,1536]{2,1,0:T(8,128)(2,1)} %get-tuple-element.40) | copy-start | bytes 884740
  84.1 45.8 %copy-start.12 = (bf16[3,32,1536]{2,1,0:T(8,128)(2,1)S(1)}, bf16[3,32,1536]{2,1,0:T(8,128)(2,1)}, u32[]{:S(2)}) copy-start(bf16[3,32,1536]{2,1,0:T(8,128)(2,1)} %get-tuple-element.41) | copy-start | bytes 884740
  84.1 45.9 %copy-start.4 = (bf16[256,384]{1,0:T(8,128)(2,1)S(1)}, bf16[256,384]{1,0:T(8,128)(2,1)}, u32[]{:S(2)}) copy-start(bf16[256,384]{1,0:T(8,128)(2,1)} %get-tuple-element.77.refs_0_) | copy-start | bytes 589828
  84.2 45.9 %copy-start.9 = (s32[2]{0:T(128)S(1)}, s32[2]{0:T(128)}, u32[]{:S(2)}) copy-start(s32[2]{0:T(128)} %length_ref.1) | copy-start | bytes 28
  84.2 45.8 %collective-permute-start.10 = (bf16[512,384]{1,0:T(8,128)(2,1)S(1)}, bf16[512,384]{1,0:T(8,128)(2,1)S(1)}, u32[]{:S(2)}, u32[]{:S(2)}) collective-permute-start(bf16[512,384]{1,0:T(8,128)(2,1)S(1)} %get-tuple-element.53), channel_id=1, source_target_pairs={{0,8},{2,10},{4,12},{6,14},{8,0},{10,2},{12,4},{14,6},{1,9},{3,11}... | collective-permute-start | bytes 1179656 | tf_op jit(solution)/shard_map/ppermute | solution.py:29
  84.4 30.1 %collective-permute-start.25 = (bf16[3,32,1536]{2,1,0:T(8,128)(2,1)S(1)}, bf16[3,32,1536]{2,1,0:T(8,128)(2,1)S(1)}, u32[]{:S(2)}, u32[]{:S(2)}) collective-permute-start(bf16[3,32,1536]{2,1,0:T(8,128)(2,1)S(1)} %get-tuple-element.59), channel_id=1, source_target_pairs={{0,14},{2,4},{4,10},{6,0},{8,6},{10,12},{12,2},{14,8},{1,15},{3,5}... | collective-permute-start | bytes 884744 | tf_op jit(solution)/shard_map/ppermute | solution.py:336
  85.4 43.4 %collective-permute-start.26 = (bf16[3,32,1536]{2,1,0:T(8,128)(2,1)S(1)}, bf16[3,32,1536]{2,1,0:T(8,128)(2,1)S(1)}, u32[]{:S(2)}, u32[]{:S(2)}) collective-permute-start(bf16[3,32,1536]{2,1,0:T(8,128)(2,1)S(1)} %get-tuple-element.58), channel_id=1, source_target_pairs={{0,6},{2,12},{4,2},{6,8},{8,14},{10,4},{12,10},{14,0},{1,7},{3,13}... | collective-permute-start | bytes 884744 | tf_op jit(solution)/shard_map/ppermute | solution.py:336
  86.2 26.3 %collective-permute-start.13 = (bf16[256,384]{1,0:T(8,128)(2,1)S(1)}, bf16[256,384]{1,0:T(8,128)(2,1)S(1)}, u32[]{:S(2)}, u32[]{:S(2)}) collective-permute-start(bf16[256,384]{1,0:T(8,128)(2,1)S(1)} %copy-done.14), channel_id=1, source_target_pairs={{0,6},{2,4},{4,2},{6,0},{8,14},{10,12},{12,10},{14,8},{1,7},{3,5},... | collective-permute-start | bytes 589832 | tf_op jit(solution)/shard_map/ppermute | solution.py:29
  112.5 25.2 %collective-permute-start.27 = (bf16[3,32,1536]{2,1,0:T(8,128)(2,1)S(1)}, bf16[3,32,1536]{2,1,0:T(8,128)(2,1)S(1)}, u32[]{:S(2)}, u32[]{:S(2)}) collective-permute-start(bf16[3,32,1536]{2,1,0:T(8,128)(2,1)S(1)} %get-tuple-element.57), channel_id=1, source_target_pairs={{0,8},{2,10},{4,12},{6,14},{8,0},{10,2},{12,4},{14,6},{1,9},{3,11}... | collective-permute-start | bytes 884744 | tf_op jit(solution)/shard_map/ppermute | solution.py:336
  114.5 34.0 %collective-permute-start.28 = (bf16[3,32,1536]{2,1,0:T(8,128)(2,1)S(1)}, bf16[3,32,1536]{2,1,0:T(8,128)(2,1)S(1)}, u32[]{:S(2)}, u32[]{:S(2)}) collective-permute-start(bf16[3,32,1536]{2,1,0:T(8,128)(2,1)S(1)} %get-tuple-element.56), channel_id=1, source_target_pairs={{0,10},{2,8},{4,14},{6,12},{8,2},{10,0},{12,6},{14,4},{1,11},{3,9}... | collective-permute-start | bytes 884744 | tf_op jit(solution)/shard_map/ppermute | solution.py:336
  128.8 19.8 %collective-permute-start.29 = (bf16[3,32,1536]{2,1,0:T(8,128)(2,1)S(1)}, bf16[3,32,1536]{2,1,0:T(8,128)(2,1)S(1)}, u32[]{:S(2)}, u32[]{:S(2)}) collective-permute-start(bf16[3,32,1536]{2,1,0:T(8,128)(2,1)S(1)} %get-tuple-element.55), channel_id=1, source_target_pairs={{0,2},{2,0},{4,6},{6,4},{8,10},{10,8},{12,14},{14,12},{1,3},{3,1},... | collective-permute-start | bytes 884744 | tf_op jit(solution)/shard_map/ppermute | solution.py:336
  128.8 20.9 %collective-permute-start.23 = (bf16[3,32,1536]{2,1,0:T(8,128)(2,1)S(1)}, bf16[3,32,1536]{2,1,0:T(8,128)(2,1)S(1)}, u32[]{:S(2)}, u32[]{:S(2)}) collective-permute-start(bf16[3,32,1536]{2,1,0:T(8,128)(2,1)S(1)} %copy-done.13), channel_id=1, source_target_pairs={{0,12},{2,6},{4,8},{6,2},{8,4},{10,14},{12,0},{14,10},{1,13},{3,7}... | collective-permute-start | bytes 884744 | tf_op jit(solution)/shard_map/ppermute | solution.py:336
  129.9 24.3 %collective-permute-start.24 = (bf16[3,32,1536]{2,1,0:T(8,128)(2,1)S(1)}, bf16[3,32,1536]{2,1,0:T(8,128)(2,1)S(1)}, u32[]{:S(2)}, u32[]{:S(2)}) collective-permute-start(bf16[3,32,1536]{2,1,0:T(8,128)(2,1)S(1)} %copy-done.12), channel_id=1, source_target_pairs={{0,4},{2,14},{4,0},{6,10},{8,12},{10,6},{12,8},{14,2},{1,5},{3,15}... | collective-permute-start | bytes 884744 | tf_op jit(solution)/shard_map/ppermute | solution.py:336
  134.2 36.7 %copy-start.5 = (bf16[1,1,256,1536]{3,2,1,0:T(8,128)(2,1)S(1)}, bf16[1,1,256,1536]{3,2,1,0:T(8,128)(2,1)}, u32[]{:S(2)}) copy-start(bf16[1,1,256,1536]{3,2,1,0:T(8,128)(2,1)} %param.9) | copy-start | bytes 2359300
  137.7 29.9 %collective-permute-start.20 = (bf16[256,384]{1,0:T(8,128)(2,1)S(1)}, bf16[256,384]{1,0:T(8,128)(2,1)S(1)}, u32[]{:S(2)}, u32[]{:S(2)}) collective-permute-start(bf16[256,384]{1,0:T(8,128)(2,1)S(1)} %get-tuple-element.37), channel_id=1, source_target_pairs={{0,4},{2,6},{4,0},{6,2},{8,12},{10,14},{12,8},{14,10},{1,5},{3,7},... | collective-permute-start | bytes 589832 | tf_op jit(solution)/shard_map/ppermute | solution.py:29
  148.5 19.1 %collective-permute-start.21 = (bf16[256,384]{1,0:T(8,128)(2,1)S(1)}, bf16[256,384]{1,0:T(8,128)(2,1)S(1)}, u32[]{:S(2)}, u32[]{:S(2)}) collective-permute-start(bf16[256,384]{1,0:T(8,128)(2,1)S(1)} %get-tuple-element.38), channel_id=1, source_target_pairs={{0,2},{2,0},{4,6},{6,4},{8,10},{10,8},{12,14},{14,12},{1,3},{3,1},... | collective-permute-start | bytes 589832 | tf_op jit(solution)/shard_map/ppermute | solution.py:29
  148.6 20.3 %collective-permute-start.22 = (bf16[256,384]{1,0:T(8,128)(2,1)S(1)}, bf16[256,384]{1,0:T(8,128)(2,1)S(1)}, u32[]{:S(2)}, u32[]{:S(2)}) collective-permute-start(bf16[256,384]{1,0:T(8,128)(2,1)S(1)} %get-tuple-element.39), channel_id=1, source_target_pairs={{0,6},{2,4},{4,2},{6,0},{8,14},{10,12},{12,10},{14,8},{1,7},{3,5},... | collective-permute-start | bytes 589832 | tf_op jit(solution)/shard_map/ppermute | solution.py:29
  158.9 1.4 collective-permute-start.30
  159.0 5.7 %collective-permute-start.31 = (bf16[32,1536]{1,0:T(8,128)(2,1)S(1)}, bf16[32,1536]{1,0:T(8,128)(2,1)S(1)}, u32[]{:S(2)}, u32[]{:S(2)}) collective-permute-start(bf16[32,1536]{1,0:T(8,128)(2,1)S(1)} %get-tuple-element.45), channel_id=1, source_target_pairs={{0,4},{2,6},{4,0},{6,2},{8,12},{10,14},{12,8},{14,10},{1,5},{3,7},... | collective-permute-start | bytes 294920 | tf_op jit(solution)/shard_map/ppermute | solution.py:29
  160.3 17.9 %collective-permute-start.32 = (bf16[32,1536]{1,0:T(8,128)(2,1)S(1)}, bf16[32,1536]{1,0:T(8,128)(2,1)S(1)}, u32[]{:S(2)}, u32[]{:S(2)}) collective-permute-start(bf16[32,1536]{1,0:T(8,128)(2,1)S(1)} %get-tuple-element.46), channel_id=1, source_target_pairs={{0,6},{2,4},{4,2},{6,0},{8,14},{10,12},{12,10},{14,8},{1,7},{3,5},... | collective-permute-start | bytes 294920 | tf_op jit(solution)/shard_map/ppermute | solution.py:29
  164.7 14.3 %collective-permute-start.33 = (bf16[32,1536]{1,0:T(8,128)(2,1)S(1)}, bf16[32,1536]{1,0:T(8,128)(2,1)S(1)}, u32[]{:S(2)}, u32[]{:S(2)}) collective-permute-start(bf16[32,1536]{1,0:T(8,128)(2,1)S(1)} %get-tuple-element.47), channel_id=1, source_target_pairs={{0,8},{2,10},{4,12},{6,14},{8,0},{10,2},{12,4},{14,6},{1,9},{3,11}... | collective-permute-start | bytes 294920 | tf_op jit(solution)/shard_map/ppermute | solution.py:29
  167.6 11.6 %collective-permute-start.34 = (bf16[32,1536]{1,0:T(8,128)(2,1)S(1)}, bf16[32,1536]{1,0:T(8,128)(2,1)S(1)}, u32[]{:S(2)}, u32[]{:S(2)}) collective-permute-start(bf16[32,1536]{1,0:T(8,128)(2,1)S(1)} %get-tuple-element.48), channel_id=1, source_target_pairs={{0,10},{2,8},{4,14},{6,12},{8,2},{10,0},{12,6},{14,4},{1,11},{3,9}... | collective-permute-start | bytes 294920 | tf_op jit(solution)/shard_map/ppermute | solution.py:29
  167.6 11.6 %collective-permute-start.35 = (bf16[32,1536]{1,0:T(8,128)(2,1)S(1)}, bf16[32,1536]{1,0:T(8,128)(2,1)S(1)}, u32[]{:S(2)}, u32[]{:S(2)}) collective-permute-start(bf16[32,1536]{1,0:T(8,128)(2,1)S(1)} %get-tuple-element.49), channel_id=1, source_target_pairs={{0,12},{2,14},{4,8},{6,10},{8,4},{10,6},{12,0},{14,2},{1,13},{3,15... | collective-permute-start | bytes 294920 | tf_op jit(solution)/shard_map/ppermute | solution.py:29
  168.9 10.4 %collective-permute-start.36 = (bf16[32,1536]{1,0:T(8,128)(2,1)S(1)}, bf16[32,1536]{1,0:T(8,128)(2,1)S(1)}, u32[]{:S(2)}, u32[]{:S(2)}) collective-permute-start(bf16[32,1536]{1,0:T(8,128)(2,1)S(1)} %get-tuple-element.50), channel_id=1, source_target_pairs={{0,14},{2,12},{4,10},{6,8},{8,6},{10,4},{12,2},{14,0},{1,15},{3,13... | collective-permute-start | bytes 294920 | tf_op jit(solution)/shard_map/ppermute | solution.py:29
  (6 other events, 7.7 us)
